TPU v7x, 512 devices: a whole 4x4x16 slice. The times are simulated.
512 devices in a mesh: row: 16 (over z), col: 32 (over x, y, core).
Axes of the slice: x: 4, y: 4, z: 16, core: 2. Of those that a mesh axis runs over, the one named last changes fastest.
Arguments:
- operator_tiles: bfloat16 [64, 128, 9, 64, 64], P('row', 'col'), may hold values from -0.25 to 0.25
- neighbour_codes: int32 [64, 128, 9], P('row', 'col'), may hold values from 0 to 8, as said below
- live_slots: int32 [64, 128], P('row', 'col'), may hold values from 1 to 9, as said below
- prolong_tiles: bfloat16 [64, 128, 6, 64, 64], P('row', 'col'), may hold values from -0.75 to 0.75
- coarse_blocks: int32 [64, 128, 6], P('row', 'col'), may hold values from 0 to 127, as said below
Outputs:
- coarse_band: float32 [32, 256, 1792], P('col', 'row')
Inputs may be any that keep to these rules, and one draw needn't show every extreme that they name: `neighbour_codes`: A fine block's 9 codes differ; slot 0 holds 4, the block itself. Slots 0 to live_slots - 1 of a fine block are used; some fine block uses all 9. `coarse_blocks`: the 6 coarse blocks of a fine block in slab s differ and lie in slabs s - 1, s, s + 1 (mod 32); the first lies in slab s.
All inputs are finite; a program needn't handle non-finite values.
Results may differ from a plain program's by a relative error of at most 0.0029.
Values may be sent and summed in bfloat16 or wider, within the bound.
No kernel may reach another device: no remote copies, remote signals or barrier semaphores. Data moves between devices by JAX's collectives and lax.ppermute only.
A program may use at most 128 MiB of HBM per device.

v0:
```python
import jax
import jax.numpy as jnp
from jax import lax
from jax.sharding import PartitionSpec as P

CB = 4


def padded(value, sides, width):
    for axis, dim in sides:
        size, length = (lax.axis_size(axis), value.shape[dim])
        up = [(i, (i + 1) % size) for i in range(size)]
        down = [(j, i) for i, j in up]
        last = lax.slice_in_dim(value, length - width, length, axis=dim)
        first = lax.slice_in_dim(value, 0, width, axis=dim)
        before = lax.ppermute(last, axis, up)
        after = lax.ppermute(first, axis, down)
        value = jnp.concatenate([before, value, after], axis=dim)
    return value


def from_behind(value, axis, steps):
    count = lax.axis_size(axis)
    pairs = [(source, (source + steps) % count) for source in range(count)]
    return lax.ppermute(value, axis, pairs)


def per_device(operator_tiles, neighbour_codes, live_slots, prolong_tiles, coarse_blocks):
    rows_first, rows_second, slot_count = neighbour_codes.shape
    prolong_width = prolong_tiles.shape[2]
    tile_size = operator_tiles.shape[-1]
    columns = lax.axis_size("col")
    slab_index = lax.axis_index("col")
    window_cols = 5 * CB
    window_rows = 3 * CB
    slab_rows = CB * tile_size
    block_count = rows_first * rows_second
    ext_tiles = padded(prolong_tiles, (("row", 0), ("col", 1)), 1)
    ext_blocks = padded(coarse_blocks, (("row", 0), ("col", 1)), 1)
    col_place = jnp.mod(ext_blocks // CB - slab_index + 2, columns) * CB + ext_blocks % CB
    col_place = col_place.reshape(-1, prolong_width)
    flat_tiles = ext_tiles.reshape(-1, prolong_width, tile_size, tile_size)
    first_index = jnp.arange(rows_first, dtype=jnp.int32)[:, None, None]
    second_index = jnp.arange(rows_second, dtype=jnp.int32)[None, :, None]
    source_index = (
        (first_index + neighbour_codes // 3) * (rows_second + 2)
        + second_index
        + neighbour_codes % 3
    )
    live_mask = jnp.arange(slot_count) < live_slots[..., None]
    masked_tiles = jnp.where(
        live_mask[..., None, None], operator_tiles, jnp.zeros((), operator_tiles.dtype)
    )

    def image_row(operands):
        tiles_row, index_row = operands
        products = jnp.einsum(
            "mkab,mklbc->mklac",
            tiles_row,
            flat_tiles[index_row],
            preferred_element_type=jnp.float32,
        )
        block_ids = jnp.arange(rows_second, dtype=jnp.int32)[:, None, None] * window_cols
        segment_ids = (block_ids + col_place[index_row]).reshape(-1)
        placed = jax.ops.segment_sum(
            products.reshape(-1, tile_size, tile_size),
            segment_ids,
            num_segments=rows_second * window_cols,
        )
        return placed.reshape(rows_second, window_cols, tile_size, tile_size).transpose(0, 2, 1, 3)

    image_panel = lax.map(image_row, (masked_tiles, source_index))
    image_panel = image_panel.reshape(block_count * tile_size, window_cols * tile_size).astype(
        jnp.bfloat16
    )
    row_place = jnp.mod(coarse_blocks // CB - slab_index + 1, columns) * CB + coarse_blocks % CB
    row_hot = (row_place[..., None] == jnp.arange(window_rows)).astype(jnp.bfloat16)
    spread = jnp.einsum(
        "xylba,xylr->xybra", prolong_tiles, row_hot, preferred_element_type=jnp.float32
    ).astype(jnp.bfloat16)
    spread = spread.reshape(block_count * tile_size, 3, slab_rows)
    reduced = lax.psum_scatter(
        jnp.einsum("kst,kc->tsc", spread, image_panel, preferred_element_type=jnp.float32),
        "row",
        scatter_dimension=0,
        tiled=True,
    )
    from_next = from_behind(reduced[:, 0], "col", -1)
    from_prev = from_behind(reduced[:, 2], "col", 1)
    combined = jnp.pad(reduced[:, 1], ((0, 0), (slab_rows, slab_rows)))
    combined = combined + jnp.pad(from_next, ((0, 0), (2 * slab_rows, 0)))
    combined = combined + jnp.pad(from_prev, ((0, 0), (0, 2 * slab_rows)))
    return combined[None]


def solution(mesh):
    in_specs = (
        P("row", "col", None, None, None),
        P("row", "col", None),
        P("row", "col"),
        P("row", "col", None, None, None),
        P("row", "col", None),
    )
    out_specs = P("col", "row", None)
    return jax.shard_map(
        per_device, mesh=mesh, in_specs=in_specs, out_specs=out_specs, check_vma=False
    )
```

profile of v0, /device:TPU:1, one launch (start us, length us, event | category | flops | bytes accessed | tf_op | source)
XLA Modules:
  0.0 455.0 jit_solution(2099151213609877863)
XLA Ops:
  7.2 4.4 collective-permute-start
  11.6 9.5 %collective-permute-start.1 = (s32[1,4,6]{2,1,0:T(4,128)S(1)}, s32[1,4,6]{2,1,0:T(4,128)S(1)}, u32[]{:S(2)}, u32[]{:S(2)}) collective-permute-start(s32[1,4,6]{2,1,0:T(4,128)S(1)} %get-tuple-element.73), channel_id=1, source_target_pairs={{32,0},{64,32},{96,64},{128,96},{160,128},{192,160},{224,192},{256... | collective-permute-start | bytes 296 | tf_op jit(solution)/shard_map/ppermute | solution.py:17
  21.1 1.2 fusion.25
  22.3 2.1 collective-permute-start.4
  24.4 4.6 %collective-permute-start.5 = (bf16[1,4,6,64,64]{4,3,2,1,0:T(8,128)(2,1)S(1)}, bf16[1,4,6,64,64]{4,3,2,1,0:T(8,128)(2,1)S(1)}, u32[]{:S(2)}, u32[]{:S(2)}) collective-permute-start(bf16[1,4,6,64,64]{4,3,2,1,0:T(8,128)(2,1)S(1)} %get-tuple-element.67), channel_id=1, source_target_pairs={{32,0},{64,32},{96,64},{128,96},{160,128},{192,160},{224,192},{256... | collective-permute-start | bytes 589832 | tf_op jit(solution)/shard_map/ppermute | solution.py:17
  29.0 0.8 iota_compare_fusion.1
  30.5 3.4 broadcast_select_fusion
  33.9 4.6 %collective-permute-start.2 = (s32[6,1,6]{2,1,0:T(1,128)S(1)}, s32[6,1,6]{2,1,0:T(1,128)S(1)}, u32[]{:S(2)}, u32[]{:S(2)}) collective-permute-start(s32[6,1,6]{2,1,0:T(1,128)S(1)} %get-tuple-element.69), channel_id=1, source_target_pairs={{0,1},{1,2},{2,3},{3,4},{4,5},{5,6},{6,7},{7,8},{8,9},{9,10},{10,1... | collective-permute-start | bytes 440 | tf_op jit(solution)/shard_map/ppermute | solution.py:16
  38.5 1.9 collective-permute-start.3
  40.5 4.2 convert_bitcast_fusion
  44.7 7.4 %reshape.109 = bf16[1024,3,256]{2,1,0:T(4,128)(2,1)} reshape(bf16[4,4,64,12,64]{4,3,2,1,0:T(8,128)(2,1)} %convert_bitcast_fusion) | data formatting | bytes 3145728 | tf_op jit(solution)/shard_map/reshape | solution.py:81
  52.6 1.4 copy-done.2
  54.1 3.6 collective-permute-start.6
  57.8 4.1 collective-permute-start.7
  62.7 1.9 collective-permute-done.6
  64.6 4.7 %collective-permute-done.7 = bf16[6,1,6,64,64]{4,3,2,1,0:T(8,128)(2,1)S(1)} collective-permute-done((bf16[6,1,6,64,64]{4,3,2,1,0:T(8,128)(2,1)S(1)}, bf16[6,1,6,64,64]{4,3,2,1,0:T(8,128)(2,1)S(1)}, u32[]{:S(2)}, u32[]{:S(2)}) %collective-permute-start.7) | collective-permute-done | bytes 294944 | tf_op jit(solution)/shard_map/ppermute | solution.py:17
  69.3 3.5 pad_maximum_fusion
  72.8 171.1 %while.10 = (s32[]{:T(128)}, bf16[4,4,64,20,64]{4,2,3,1,0:T(8,128)(2,1)}, s32[4,4,9]{2,1,0:T(4,128)S(1)}, s32[36,6]{1,0:T(8,128)}, bf16[36,6,64,64]{3,2,1,0:T(8,...) while((s32[]{:T(128)}, bf16[4,4,64,20,64]{4,2,3,1,0:T(8,128)(2,1)}, ...), condition=%wide.region_2.3_spmd, body=%wide.region_0.2_spmd.sunk | while | flops 114132296 | bytes 32395752 | solution.py:72
  72.9 3.2 gather_fusion.1
  76.1 5.1 %fusion.35 = f32[4,9,6,64,64]{4,3,2,1,0:T(8,128)} fusion(bf16[4,9,6,64,64]{4,3,2,1,0:T(8,128)(2,1)S(1)} %bitcast.61, bf16[4,4,9,64,64]{4,3,2,1,0:T(8,128)(2,1)} %get-tuple-element.133, s32[]{:T(128)} %get-tuple-element.120), kind=kOutput, calls=%fused_computation.3.clone.1 | convolution fusion | flops 113246208 | bytes 5898752 | tf_op jit(solution)/shard_map/while/body/eval_jaxpr/mkab,mklbc->mklac/dot_general | solution.py:57
  81.2 8.5 %copy.59 = f32[216,64,64]{2,1,0:T(8,128)} copy(f32[216,64,64]{1,2,0:T(8,128)} %bitcast.60) | data formatting | bytes 7077888 | tf_op jit(solution)/shard_map/while/body/eval_jaxpr/reshape | solution.py:66
  91.0 23.2 %scatter_fusion = f32[80,64,64]{2,1,0:T(8,128)S(1)} fusion(f32[80,64,64]{2,1,0:T(8,128)S(1)} %broadcast.131, s32[216]{0:T(256)S(1)} %reshape.128, f32[216,64,64]{2,1,0:T(8,128)} %copy.59), kind=kCustom, calls=%fused_computation.2.clone.1 | custom fusion | flops 884736 | bytes 10617696 | tf_op jit(solution)/shard_map/while/body/eval_jaxpr/scatter-add | solution.py:65
  114.2 1.4 constant_dynamic-update-slice_fusion.8
  115.6 3.2 gather_fusion.1
  118.9 5.1 %fusion.35 = f32[4,9,6,64,64]{4,3,2,1,0:T(8,128)} fusion(bf16[4,9,6,64,64]{4,3,2,1,0:T(8,128)(2,1)S(1)} %bitcast.61, bf16[4,4,9,64,64]{4,3,2,1,0:T(8,128)(2,1)} %get-tuple-element.133, s32[]{:T(128)} %get-tuple-element.120), kind=kOutput, calls=%fused_computation.3.clone.1 | convolution fusion | flops 113246208 | bytes 5898752 | tf_op jit(solution)/shard_map/while/body/eval_jaxpr/mkab,mklbc->mklac/dot_general | solution.py:57
  124.0 8.5 %copy.59 = f32[216,64,64]{2,1,0:T(8,128)} copy(f32[216,64,64]{1,2,0:T(8,128)} %bitcast.60) | data formatting | bytes 7077888 | tf_op jit(solution)/shard_map/while/body/eval_jaxpr/reshape | solution.py:66
  133.8 23.2 %scatter_fusion = f32[80,64,64]{2,1,0:T(8,128)S(1)} fusion(f32[80,64,64]{2,1,0:T(8,128)S(1)} %broadcast.131, s32[216]{0:T(256)S(1)} %reshape.128, f32[216,64,64]{2,1,0:T(8,128)} %copy.59), kind=kCustom, calls=%fused_computation.2.clone.1 | custom fusion | flops 884736 | bytes 10617696 | tf_op jit(solution)/shard_map/while/body/eval_jaxpr/scatter-add | solution.py:65
  157.0 1.3 constant_dynamic-update-slice_fusion.8
  158.4 3.2 gather_fusion.1
  161.6 5.1 %fusion.35 = f32[4,9,6,64,64]{4,3,2,1,0:T(8,128)} fusion(bf16[4,9,6,64,64]{4,3,2,1,0:T(8,128)(2,1)S(1)} %bitcast.61, bf16[4,4,9,64,64]{4,3,2,1,0:T(8,128)(2,1)} %get-tuple-element.133, s32[]{:T(128)} %get-tuple-element.120), kind=kOutput, calls=%fused_computation.3.clone.1 | convolution fusion | flops 113246208 | bytes 5898752 | tf_op jit(solution)/shard_map/while/body/eval_jaxpr/mkab,mklbc->mklac/dot_general | solution.py:57
  166.7 8.5 %copy.59 = f32[216,64,64]{2,1,0:T(8,128)} copy(f32[216,64,64]{1,2,0:T(8,128)} %bitcast.60) | data formatting | bytes 7077888 | tf_op jit(solution)/shard_map/while/body/eval_jaxpr/reshape | solution.py:66
  176.6 23.1 %scatter_fusion = f32[80,64,64]{2,1,0:T(8,128)S(1)} fusion(f32[80,64,64]{2,1,0:T(8,128)S(1)} %broadcast.131, s32[216]{0:T(256)S(1)} %reshape.128, f32[216,64,64]{2,1,0:T(8,128)} %copy.59), kind=kCustom, calls=%fused_computation.2.clone.1 | custom fusion | flops 884736 | bytes 10617696 | tf_op jit(solution)/shard_map/while/body/eval_jaxpr/scatter-add | solution.py:65
  199.7 1.4 constant_dynamic-update-slice_fusion.8
  201.2 3.2 gather_fusion.1
  204.4 5.1 %fusion.35 = f32[4,9,6,64,64]{4,3,2,1,0:T(8,128)} fusion(bf16[4,9,6,64,64]{4,3,2,1,0:T(8,128)(2,1)S(1)} %bitcast.61, bf16[4,4,9,64,64]{4,3,2,1,0:T(8,128)(2,1)} %get-tuple-element.133, s32[]{:T(128)} %get-tuple-element.120), kind=kOutput, calls=%fused_computation.3.clone.1 | convolution fusion | flops 113246208 | bytes 5898752 | tf_op jit(solution)/shard_map/while/body/eval_jaxpr/mkab,mklbc->mklac/dot_general | solution.py:57
  209.5 8.5 %copy.59 = f32[216,64,64]{2,1,0:T(8,128)} copy(f32[216,64,64]{1,2,0:T(8,128)} %bitcast.60) | data formatting | bytes 7077888 | tf_op jit(solution)/shard_map/while/body/eval_jaxpr/reshape | solution.py:66
  219.3 23.2 %scatter_fusion = f32[80,64,64]{2,1,0:T(8,128)S(1)} fusion(f32[80,64,64]{2,1,0:T(8,128)S(1)} %broadcast.131, s32[216]{0:T(256)S(1)} %reshape.128, f32[216,64,64]{2,1,0:T(8,128)} %copy.59), kind=kCustom, calls=%fused_computation.2.clone.1 | custom fusion | flops 884736 | bytes 10617696 | tf_op jit(solution)/shard_map/while/body/eval_jaxpr/scatter-add | solution.py:65
  242.5 1.4 constant_dynamic-update-slice_fusion.8
  243.8 9.6 %copy.28 = bf16[4,4,64,20,64]{2,1,0,4,3:T(4,128)(2,1)} copy(bf16[4,4,64,20,64]{4,2,3,1,0:T(8,128)(2,1)} %get-tuple-element.37) | data formatting | bytes 5242880 | tf_op jit(solution)/shard_map/convert_element_type | solution.py:73
  253.4 8.2 %reshape.106 = bf16[1024,1280,1]{0,1,2:T(8,128)(2,1)S(1)} reshape(bf16[4,4,64,20,64]{2,1,0,4,3:T(4,128)(2,1)} %copy.28) | data formatting | bytes 5242880 | tf_op jit(solution)/shard_map/convert_element_type | solution.py:73
  261.6 5.7 %convolution_bitcast_fusion = f32[256,3,1280]{0,2,1:T(8,128)} fusion(bf16[1024,1280,1]{0,1,2:T(8,128)(2,1)S(1)} %reshape.106, bf16[1024,3,256]{2,1,0:T(4,128)(2,1)} %reshape.109), kind=kOutput, calls=%fused_computation.13 | convolution fusion | flops 2013265920 | bytes 8126464 | tf_op jit(solution)/shard_map/kst,kc->tsc/dot_general | solution.py:83
  267.3 6.6 %copy.32 = f32[256,3,1280]{2,1,0:T(4,128)} copy(f32[256,3,1280]{0,2,1:T(8,128)} %convolution_bitcast_fusion) | data formatting | bytes 7864320 | tf_op jit(solution)/shard_map/kst,kc->tsc/transpose | solution.py:83
  273.9 1.3 dynamic-slice
  275.8 155.4 %all-reduce.6.cloned.1.call-done = f32[256,3,1280]{2,1,0:T(4,128)} async-done(((f32[256,3,1280]{2,1,0:T(4,128)}), f32[256,3,1280]{2,1,0:T(4,128)}) %all-reduce.6.cloned.1.call-update) | async-done | bytes 3932176
  431.2 1.5 constant_dynamic-slice_fusion.1
  432.7 10.1 %collective-permute-start.8 = (f32[16,1280]{1,0:T(8,128)S(1)}, f32[16,1280]{1,0:T(8,128)S(1)}, u32[]{:S(2)}, u32[]{:S(2)}) collective-permute-start(f32[16,1280]{1,0:T(8,128)S(1)} %bitcast.64), channel_id=1, source_target_pairs={{0,31},{1,0},{2,1},{3,2},{4,3},{5,4},{6,5},{7,6},{8,7},{9,8},{10,9... | collective-permute-start | bytes 245768 | tf_op jit(solution)/shard_map/ppermute | solution.py:25
  442.9 3.1 collective-permute-start.9
  446.2 1.3 collective-permute-done.9
  (86 shorter events, 9.5 us)
Async XLA Ops:
  6.5 424.7 %all-reduce.6.cloned.1.call-start = ((), (), s32[]{:S(2)}) async-start(), calls=%async_computation | async-start | bytes 10485760
  7.2 26.6 %collective-permute-start = (s32[1,4,6]{2,1,0:T(4,128)S(1)}, s32[1,4,6]{2,1,0:T(4,128)S(1)}, u32[]{:S(2)}, u32[]{:S(2)}) collective-permute-start(s32[1,4,6]{2,1,0:T(4,128)S(1)} %get-tuple-element.74), channel_id=1, source_target_pairs={{0,32},{32,64},{64,96},{96,128},{128,160},{160,192},{192,224},{224... | collective-permute-start | bytes 296 | tf_op jit(solution)/shard_map/ppermute | solution.py:16
  11.6 22.3 %collective-permute-start.1 = (s32[1,4,6]{2,1,0:T(4,128)S(1)}, s32[1,4,6]{2,1,0:T(4,128)S(1)}, u32[]{:S(2)}, u32[]{:S(2)}) collective-permute-start(s32[1,4,6]{2,1,0:T(4,128)S(1)} %get-tuple-element.73), channel_id=1, source_target_pairs={{32,0},{64,32},{96,64},{128,96},{160,128},{192,160},{224,192},{256... | collective-permute-start | bytes 296 | tf_op jit(solution)/shard_map/ppermute | solution.py:17
  22.3 11.5 %copy-start.3 = (s32[4,4,6]{2,1,0:T(4,128)S(1)}, s32[4,4,6]{2,1,0:T(4,128)}, u32[]{:S(2)}) copy-start(s32[4,4,6]{2,1,0:T(4,128)} %param.11) | copy-start | bytes 1156
  22.3 18.2 %copy-start.1 = (bf16[4,4,6,64,64]{4,3,2,1,0:T(8,128)(2,1)S(1)}, bf16[4,4,6,64,64]{4,3,2,1,0:T(8,128)(2,1)}, u32[]{:S(2)}) copy-start(bf16[4,4,6,64,64]{4,3,2,1,0:T(8,128)(2,1)} %param.10) | copy-start | bytes 2359300
  22.3 29.8 %collective-permute-start.4 = (bf16[1,4,6,64,64]{4,3,2,1,0:T(8,128)(2,1)S(1)}, bf16[1,4,6,64,64]{4,3,2,1,0:T(8,128)(2,1)S(1)}, u32[]{:S(2)}, u32[]{:S(2)}) collective-permute-start(bf16[1,4,6,64,64]{4,3,2,1,0:T(8,128)(2,1)S(1)} %get-tuple-element.68), channel_id=1, source_target_pairs={{0,32},{32,64},{64,96},{96,128},{128,160},{160,192},{192,224},{224... | collective-permute-start | bytes 589832 | tf_op jit(solution)/shard_map/ppermute | solution.py:16
  24.4 28.1 %collective-permute-start.5 = (bf16[1,4,6,64,64]{4,3,2,1,0:T(8,128)(2,1)S(1)}, bf16[1,4,6,64,64]{4,3,2,1,0:T(8,128)(2,1)S(1)}, u32[]{:S(2)}, u32[]{:S(2)}) collective-permute-start(bf16[1,4,6,64,64]{4,3,2,1,0:T(8,128)(2,1)S(1)} %get-tuple-element.67), channel_id=1, source_target_pairs={{32,0},{64,32},{96,64},{128,96},{160,128},{192,160},{224,192},{256... | collective-permute-start | bytes 589832 | tf_op jit(solution)/shard_map/ppermute | solution.py:17
  33.9 27.9 %collective-permute-start.2 = (s32[6,1,6]{2,1,0:T(1,128)S(1)}, s32[6,1,6]{2,1,0:T(1,128)S(1)}, u32[]{:S(2)}, u32[]{:S(2)}) collective-permute-start(s32[6,1,6]{2,1,0:T(1,128)S(1)} %get-tuple-element.69), channel_id=1, source_target_pairs={{0,1},{1,2},{2,3},{3,4},{4,5},{5,6},{6,7},{7,8},{8,9},{9,10},{10,1... | collective-permute-start | bytes 440 | tf_op jit(solution)/shard_map/ppermute | solution.py:16
  38.5 23.3 %collective-permute-start.3 = (s32[6,1,6]{2,1,0:T(1,128)S(1)}, s32[6,1,6]{2,1,0:T(1,128)S(1)}, u32[]{:S(2)}, u32[]{:S(2)}) collective-permute-start(s32[6,1,6]{2,1,0:T(1,128)S(1)} %get-tuple-element.70), channel_id=1, source_target_pairs={{1,0},{2,1},{3,2},{4,3},{5,4},{6,5},{7,6},{8,7},{9,8},{10,9},{11,1... | collective-permute-start | bytes 440 | tf_op jit(solution)/shard_map/ppermute | solution.py:17
  52.5 1.4 copy-start.2
  54.1 10.5 %collective-permute-start.6 = (bf16[6,1,6,64,64]{4,3,2,1,0:T(8,128)(2,1)S(1)}, bf16[6,1,6,64,64]{4,3,2,1,0:T(8,128)(2,1)S(1)}, u32[]{:S(2)}, u32[]{:S(2)}) collective-permute-start(bf16[6,1,6,64,64]{4,3,2,1,0:T(8,128)(2,1)S(1)} %get-tuple-element.65), channel_id=1, source_target_pairs={{0,1},{1,2},{2,3},{3,4},{4,5},{5,6},{6,7},{7,8},{8,9},{9,10},{10,1... | collective-permute-start | bytes 884744 | tf_op jit(solution)/shard_map/ppermute | solution.py:16
  57.8 11.5 %collective-permute-start.7 = (bf16[6,1,6,64,64]{4,3,2,1,0:T(8,128)(2,1)S(1)}, bf16[6,1,6,64,64]{4,3,2,1,0:T(8,128)(2,1)S(1)}, u32[]{:S(2)}, u32[]{:S(2)}) collective-permute-start(bf16[6,1,6,64,64]{4,3,2,1,0:T(8,128)(2,1)S(1)} %get-tuple-element.66), channel_id=1, source_target_pairs={{1,0},{2,1},{3,2},{4,3},{5,4},{6,5},{7,6},{8,7},{9,8},{10,9},{11,1... | collective-permute-start | bytes 884744 | tf_op jit(solution)/shard_map/ppermute | solution.py:17
  81.2 8.5 %copy-start = (s32[36,6]{1,0:T(8,128)S(1)}, s32[36,6]{1,0:T(8,128)}, u32[]{:S(2)}) copy-start(s32[36,6]{1,0:T(8,128)} %get-tuple-element.131) | copy-start | bytes 2596 | tf_op jit(solution)/shard_map/while
  124.0 8.5 %copy-start = (s32[36,6]{1,0:T(8,128)S(1)}, s32[36,6]{1,0:T(8,128)}, u32[]{:S(2)}) copy-start(s32[36,6]{1,0:T(8,128)} %get-tuple-element.131) | copy-start | bytes 2596 | tf_op jit(solution)/shard_map/while
  166.7 8.5 %copy-start = (s32[36,6]{1,0:T(8,128)S(1)}, s32[36,6]{1,0:T(8,128)}, u32[]{:S(2)}) copy-start(s32[36,6]{1,0:T(8,128)} %get-tuple-element.131) | copy-start | bytes 2596 | tf_op jit(solution)/shard_map/while
  209.5 8.5 %copy-start = (s32[36,6]{1,0:T(8,128)S(1)}, s32[36,6]{1,0:T(8,128)}, u32[]{:S(2)}) copy-start(s32[36,6]{1,0:T(8,128)} %get-tuple-element.131) | copy-start | bytes 2596 | tf_op jit(solution)/shard_map/while
  432.7 13.4 %collective-permute-start.8 = (f32[16,1280]{1,0:T(8,128)S(1)}, f32[16,1280]{1,0:T(8,128)S(1)}, u32[]{:S(2)}, u32[]{:S(2)}) collective-permute-start(f32[16,1280]{1,0:T(8,128)S(1)} %bitcast.64), channel_id=1, source_target_pairs={{0,31},{1,0},{2,1},{3,2},{4,3},{5,4},{6,5},{7,6},{8,7},{9,8},{10,9... | collective-permute-start | bytes 245768 | tf_op jit(solution)/shard_map/ppermute | solution.py:25
  442.9 4.6 %collective-permute-start.9 = (f32[16,1280]{1,0:T(8,128)S(1)}, f32[16,1280]{1,0:T(8,128)S(1)}, u32[]{:S(2)}, u32[]{:S(2)}) collective-permute-start(f32[16,1280]{1,0:T(8,128)S(1)} %bitcast.65), channel_id=1, source_target_pairs={{0,1},{1,2},{2,3},{3,4},{4,5},{5,6},{6,7},{7,8},{8,9},{9,10},{10,1... | collective-permute-start | bytes 245768 | tf_op jit(solution)/shard_map/ppermute | solution.py:25
Sparse Core Ops, SparseCore 0:
  274.0 157.1 all-reduce.5
where the time goes:
time: 462 us; the launch traced here: 455 us
  waiting for transfers between devices  163 us (35%)
  other arithmetic  102 us (22%)
  local copies, waits for them, and re-layouts  96.8 us (21%)
  starting transfers between devices  47.9 us (10%)
  matrix products  30.3 us (7%)
  between operations  14.3 us (3%)
    unnamed x2, waiting for transfers between devices  155 us
    scatter-add x4, other arithmetic, image_row(): jax.ops.segment_sum(products.reshape(-1, tile_size, tile_size), segment_i...  92.6 us
    reshape x4, local copies, waits for them, and re-layouts, image_row(): products.reshape(-1, tile_size, tile_size)  33.9 us
    dot_general x4, matrix products, image_row(): jnp.einsum('mkab,mklbc->mklac', tiles_row, flat_tiles[index_row], preferr...  20.3 us
    ppermute x4, starting transfers between devices, padded(): after = lax.ppermute(first, axis, down)  20.1 us
    convert_element_type x2, local copies, waits for them, and re-layouts, per_device(): image_panel.reshape(block_count * tile_size, window_cols * tile_size)  17.7 us
    ppermute x4, starting transfers between devices, padded(): before = lax.ppermute(last, axis, up)  14.6 us
    ppermute x2, starting transfers between devices, from_behind(): return lax.ppermute(value, axis, pairs)  13.2 us
  transfers between devices with their start and end apart: 11, of which 5 were waited for; matrix products, arithmetic and copies ran while one was open for 4% of the time, Pallas kernels for 0%

commit v1 on v0

v1 whole, which is shorter than its diff:
```python
import jax
import jax.numpy as jnp
from jax import lax
from jax.experimental import pallas as pl
from jax.experimental.pallas import tpu as pltpu
from jax.sharding import PartitionSpec as P

CB = 4
B = 64
ROWS = 16
COLS = 32
F32 = jnp.float32
BF16 = jnp.bfloat16


def joint(rule):
    pairs = []
    for r in range(ROWS):
        for s in range(COLS):
            r2, s2 = rule(r, s)
            pairs.append((r * COLS + s, (r2 % ROWS) * COLS + s2 % COLS))
    return pairs


def send(value, rule):
    return lax.ppermute(value, ("row", "col"), joint(rule))


def sign(s):
    return 1 if s % 2 == 0 else -1


def place_kernel(core_ref, inv_ref, p_ref, po_ref, cross_ref, chip_ref, up_ref, down_ref):
    def block(b, carry):
        y = b // 4
        x = b % 4
        row = pl.multiple_of(b * B, B)

        def tile(r):
            j = inv_ref[b * 12 + r]
            value = p_ref[(x * 4 + y) * 6 + jnp.maximum(j - 1, 0)]
            return jnp.where(j > 0, value, jnp.zeros_like(value))

        for m in range(6):
            pair = jnp.concatenate([tile(2 * m), tile(2 * m + 1)], axis=1)
            po_ref[pl.ds(row, B), 128 * m : 128 * (m + 1)] = pair
        return carry

    lax.fori_loop(0, 16, block, 0)
    core = core_ref[0]
    cross_row = pl.multiple_of(core * 768, 256)
    chip_row = pl.multiple_of(768 - core * 768, 256)
    cross_ref[...] = po_ref[pl.ds(cross_row, 256), :]
    chip_ref[...] = po_ref[pl.ds(chip_row, 256), :]
    for y in range(4):
        up_ref[64 * y : 64 * y + 64, :] = po_ref[256 * y + 192 : 256 * y + 256, :]
        down_ref[64 * y : 64 * y + 64, :] = po_ref[256 * y : 256 * y + 64, :]


def smem():
    return pl.BlockSpec(memory_space=pltpu.SMEM)


def vmem():
    return pl.BlockSpec(memory_space=pltpu.VMEM)


def place(core, inv, tiles):
    edge = jax.ShapeDtypeStruct((256, 768), BF16)
    return pl.pallas_call(
        place_kernel,
        out_shape=(jax.ShapeDtypeStruct((1024, 768), BF16), edge, edge, edge, edge),
        in_specs=[smem(), smem(), vmem()],
        out_specs=(vmem(),) * 5,
        name="place",
    )(core, inv, tiles)


SLOTS = (
    ((1, 2), (None, None), (0, None)),
    ((0, 1), (2, None), (None, None)),
    ((None, 0), (1, 2), (None, None)),
    ((None, None), (0, 1), (None, 2)),
)


def reverse3(v):
    return (v & 1) * 4 + (v & 2) + (v >> 2)


def product_kernel(
    pos_ref, aidx_ref, a_ref, po_ref, cross_ref, chip_ref, up_ref, down_ref, upc_ref, downc_ref,
    keep_ref, swap_ref, same_ref, other_ref, ad_ref, pe_ref, im_ref, res_ref,
):
    core = pos_ref[0]
    r = pos_ref[1]

    def fill(b, carry):
        y = b // 4

        def tile(x, c):
            if c is None:
                return jnp.zeros((B, B), BF16)
            k = aidx_ref[(y * 4 + x) * 9 + c]
            value = a_ref[(x * 4 + y) * 9 + jnp.maximum(k, 0)]
            return jnp.where(k >= 0, value, jnp.zeros_like(value))

        for x in range(4):
            @pl.when(b % 4 == x)
            def _():
                for dy in range(3):
                    for m in range(3):
                        left, right = SLOTS[x][m]
                        left = None if left is None else left * 3 + dy
                        right = None if right is None else right * 3 + dy
                        pair = jnp.concatenate([tile(x, left), tile(x, right)], axis=1)
                        lane = 384 * dy + 128 * m
                        ad_ref[y, 64 * x : 64 * x + 64, lane : lane + 128] = pair
        return carry

    lax.fori_loop(0, 16, fill, 0)
    for y in range(4):
        pe_ref[y + 1, 0:256, :] = po_ref[256 * y : 256 * y + 256, :]
        pe_ref[y + 1, 256:320, :] = up_ref[64 * y : 64 * y + 64, :]
        pe_ref[y + 1, 320:384, :] = down_ref[64 * y : 64 * y + 64, :]
    cross_at = core * 5
    chip_at = 5 - core * 5
    pe_ref[cross_at, 0:256, :] = cross_ref[...]
    pe_ref[chip_at, 0:256, :] = chip_ref[...]
    pe_ref[cross_at, 256:320, :] = upc_ref[0:64, :]
    pe_ref[chip_at, 256:320, :] = upc_ref[64:128, :]
    pe_ref[cross_at, 320:384, :] = downc_ref[0:64, :]
    pe_ref[chip_at, 320:384, :] = downc_ref[64:128, :]

    def dot(a, b):
        return jnp.dot(a, b, preferred_element_type=F32)

    for y in range(4):
        rows = slice(256 * y, 256 * y + 256)
        if y in (1, 2):
            total = None
            for dy in range(3):
                part = dot(ad_ref[y, :, 384 * dy : 384 * dy + 384], pe_ref[y + dy])
                total = part if total is None else total + part
            im_ref[rows, 256:1024] = total.astype(BF16)
        else:
            edge_dy = 0 if y == 0 else 2
            edge = dot(ad_ref[y, :, 384 * edge_dy : 384 * edge_dy + 384], pe_ref[y + edge_dy])
            first, second = (1, 2) if y == 0 else (0, 1)
            total = dot(ad_ref[y, :, 384 * first : 384 * first + 384], pe_ref[y + first])
            total = total + dot(ad_ref[y, :, 384 * second : 384 * second + 384], pe_ref[y + second])
            if y == 0:
                im_ref[rows, 0:256] = edge[:, 0:256].astype(BF16)
                im_ref[rows, 256:768] = (edge[:, 256:768] + total[:, 0:512]).astype(BF16)
                im_ref[rows, 768:1024] = total[:, 512:768].astype(BF16)
            else:
                im_ref[rows, 256:512] = total[:, 0:256].astype(BF16)
                im_ref[rows, 512:1024] = (edge[:, 0:512] + total[:, 256:768]).astype(BF16)
                im_ref[rows, 1024:1280] = edge[:, 512:768].astype(BF16)

    def piece(window, kind, store):
        lanes = pl.ds(pl.multiple_of(window * 256, 256), 256)
        for chunk in range(5):
            rows = slice(0, 256) if chunk == 0 else slice(768, 1024) if chunk == 4 else slice(0, 1024)
            cols = slice(256 * chunk, 256 * chunk + 256)
            out = lax.dot_general(
                po_ref[rows, lanes], im_ref[rows, cols], (((0,), (0,)), ((), ())),
                preferred_element_type=F32,
            )
            for o in range(16):
                shifted = (o - r - kind + 32) % 16
                flow = shifted // 8
                near = jnp.where(flow == 0, shifted, 15 - shifted)
                half = (flow + core) % 2
                row = pl.multiple_of((half * 8 + reverse3(near)) * 16, 16)
                res_ref[pl.ds(row, 16), :] = out[16 * o : 16 * o + 16, :]
            store(cols)

    def store_outer(cols):
        same_ref[:, cols] = res_ref[0:128, :].astype(BF16)
        other_ref[:, cols] = res_ref[128:256, :].astype(BF16)

    def store_own(cols):
        keep_ref[0:128, cols] = res_ref[0:128, :]
        swap_ref[0:128, cols] = res_ref[128:256, :].astype(BF16)

    def store_partner(cols):
        keep_ref[128:256, cols] = res_ref[0:128, :]
        swap_ref[128:256, cols] = res_ref[128:256, :].astype(BF16)

    piece(core * 2, 1 - core, store_outer)
    piece(1 + core * 0, core, store_own)
    piece(2 - core * 2, 1 - core, store_partner)


def products(pos, aidx, a, po, cross, chip, up, down, upc, downc):
    half = jax.ShapeDtypeStruct((128, 1280), BF16)
    return pl.pallas_call(
        product_kernel,
        out_shape=(
            jax.ShapeDtypeStruct((256, 1280), F32),
            jax.ShapeDtypeStruct((256, 1280), BF16),
            half,
            half,
        ),
        in_specs=[smem(), smem()] + [vmem()] * 8,
        out_specs=(vmem(),) * 4,
        scratch_shapes=[
            pltpu.VMEM((4, 256, 1152), BF16),
            pltpu.VMEM((6, 384, 768), BF16),
            pltpu.VMEM((1024, 1280), BF16),
            pltpu.VMEM((256, 256), F32),
        ],
        name="products",
    )(pos, aidx, a, po, cross, chip, up, down, upc, downc)


def merge_kernel(pos_ref, keep_ref, swap_ref, same_ref, other_ref, acc_ref, msg_ref, sum_ref):
    def merge(low, high):
        sum_ref[...] = jnp.zeros_like(sum_ref)
        sum_ref[0, :, 256:1536] = keep_ref[0:128, :]
        sum_ref[0, :, high : high + 1280] += swap_ref[128:256, :].astype(F32)
        sum_ref[0, :, low : low + 1280] += other_ref[...].astype(F32)
        sum_ref[1, :, low : low + 1280] = keep_ref[128:256, :]
        sum_ref[1, :, 256:1536] += swap_ref[0:128, :].astype(F32)
        sum_ref[1, :, high : high + 1280] += same_ref[...].astype(F32)

    @pl.when(pos_ref[0] == 0)
    def _():
        merge(0, 512)

    @pl.when(pos_ref[0] == 1)
    def _():
        merge(512, 0)

    acc_ref[...] = sum_ref[:, 0:64, :]
    msg_ref[...] = sum_ref[:, 64:128, :].astype(BF16)


def merged(pos, keep, swap, same, other):
    return pl.pallas_call(
        merge_kernel,
        out_shape=(
            jax.ShapeDtypeStruct((2, 64, 1792), F32),
            jax.ShapeDtypeStruct((2, 64, 1792), BF16),
        ),
        in_specs=[smem()] + [vmem()] * 4,
        out_specs=(vmem(), vmem()),
        scratch_shapes=[pltpu.VMEM((2, 128, 1792), F32)],
        name="merge",
    )(pos, keep, swap, same, other)


def per_device(operator_tiles, neighbour_codes, live_slots, prolong_tiles, coarse_blocks):
    r = lax.axis_index("row")
    s = lax.axis_index("col")
    core = s % 2
    pos = jnp.stack([core, r]).astype(jnp.int32)

    place_of = jnp.mod(coarse_blocks // CB - s + 1, COLS) * CB + coarse_blocks % CB
    hit = place_of[..., None] == jnp.arange(12)
    number = jnp.arange(1, 7, dtype=jnp.int32)[:, None]
    inv = jnp.sum(jnp.where(hit, number, 0), axis=2).transpose(1, 0, 2).reshape(-1)
    code_hit = neighbour_codes[..., None] == jnp.arange(9)
    slot = jnp.sum(jnp.where(code_hit, jnp.arange(9, dtype=jnp.int32)[:, None], 0), axis=2)
    slot = jnp.where(slot < live_slots[..., None], slot, -1)
    aidx = slot.transpose(1, 0, 2).reshape(-1)

    po, cross, chip, up, down = place(pos, inv, prolong_tiles.reshape(96, B, B))
    up_in = send(up, lambda r, s: (r + 1, s))
    down_in = send(down, lambda r, s: (r - 1, s))
    cross_in = send(cross, lambda r, s: (r, s - sign(s)))
    chip_in = send(chip, lambda r, s: (r, s + sign(s)))
    upc = jnp.concatenate([cross_in[192:256], chip_in[192:256]], axis=0)
    downc = jnp.concatenate([cross_in[0:64], chip_in[0:64]], axis=0)
    upc_in = send(upc, lambda r, s: (r + 1, s))
    downc_in = send(downc, lambda r, s: (r - 1, s))

    keep, swap, same, other = products(
        pos, aidx, operator_tiles.reshape(144, B, B), po,
        cross_in, chip_in, up_in, down_in, upc_in, downc_in,
    )
    other_in = send(other, lambda r, s: (r, s - sign(s)))
    same_in = send(same, lambda r, s: (r, s - 2 * sign(s)))
    swap_in = send(swap, lambda r, s: (r, s + sign(s)))
    acc, msg = merged(pos, keep, swap_in, same_in, other_in)
    for step, size in ((1, 32), (2, 16)):
        got = send(msg, lambda r, s: (r + step * sign(s), s)).astype(F32)
        msg = (acc[:, size:] + got[:, size:]).astype(BF16)
        acc = acc[:, :size] + got[:, :size]
    acc = acc + send(msg, lambda r, s: (r + 4 * sign(s), s)).astype(F32)
    last = send(acc[1], lambda r, s: (r + sign(s), s + sign(s)))
    return (acc[0] + last)[None]


def solution(mesh):
    in_specs = (
        P("row", "col", None, None, None),
        P("row", "col", None),
        P("row", "col"),
        P("row", "col", None, None, None),
        P("row", "col", None),
    )
    out_specs = P("col", "row", None)
    return jax.shard_map(
        per_device, mesh=mesh, in_specs=in_specs, out_specs=out_specs, check_vma=False
    )
```

time: 462 us -> 121 us (0.26); the launches traced: 455 us -> 120 us
  waiting for transfers between devices: 163 us -> 30.3 us
  other arithmetic: 102 us -> 2.56 us
  local copies, waits for them, and re-layouts: 96.8 us -> 3.27 us
  matrix products: 30.3 us -> 0 us
  Pallas kernels: 0 us -> 18.6 us
  starting transfers between devices: 47.9 us -> 65.1 us
  between operations: 14.3 us -> 0.28 us
    unnamed x2 -> x0, waiting for transfers between devices: 155 us -> none
    scatter-add x4 -> x0, other arithmetic: 92.6 us -> none  [image_row(): jax.ops.segment_sum(products.reshape(-1, tile_size, tile_size), segment_i...]
    reshape x5 -> x2, local copies, waits for them, and re-layouts: 41.3 us -> 1.32 us  [the longest x1 0.66 us: per_device(): aidx = slot.transpose(1, 0, 2).reshape(-1)]
    dot_general x6 -> x0, matrix products: 30.3 us -> none  [the longest x4 20.3 us: image_row(): jnp.einsum('mkab,mklbc->mklac', tiles_row, flat_tiles[index_row], preferr...]
    ppermute x10 -> x13, waiting for transfers between devices: 8.02 us -> 30.3 us  [send(): return lax.ppermute(value, ('row', 'col'), joint(rule))]
    pallas_call x0 -> x3, Pallas kernels: none -> 18.6 us  [the longest x1 10.8 us: products(): pl.pallas_call(product_kernel, out_shape=(jax.ShapeDtypeStruct((256, 1280...]
    convert_element_type x2 -> x0, local copies, waits for them, and re-layouts: 17.7 us -> none  [per_device(): image_panel.reshape(block_count * tile_size, window_cols * tile_size)]
    ppermute x10 -> x13, starting transfers between devices: 47.9 us -> 65.1 us  [send(): return lax.ppermute(value, ('row', 'col'), joint(rule))]
  transfers between devices with their start and end apart: 11 -> 13, of which waited for: 5 -> 10; matrix products, arithmetic and copies ran while one was open for 4% -> 1% of each run, Pallas kernels for 0% -> 0%
where the time goes in v1:
time: 121 us; the launch traced here: 120 us
  starting transfers between devices  65.1 us (54%)
  waiting for transfers between devices  30.3 us (25%)
  Pallas kernels  18.6 us (15%)
  local copies, waits for them, and re-layouts  3.27 us (3%)
  other arithmetic  2.56 us (2%)
    ppermute x13, starting transfers between devices, send(): return lax.ppermute(value, ('row', 'col'), joint(rule))  65.1 us
    ppermute x13, waiting for transfers between devices, send(): return lax.ppermute(value, ('row', 'col'), joint(rule))  30.3 us
    pallas_call x1, Pallas kernels, products(): pl.pallas_call(product_kernel, out_shape=(jax.ShapeDtypeStruct((256, 1280...  10.8 us
    pallas_call x1, Pallas kernels, place(): pl.pallas_call(place_kernel, out_shape=(jax.ShapeDtypeStruct((1024, 768),...  4.71 us
    pallas_call x1, Pallas kernels, merged(): pl.pallas_call(merge_kernel, out_shape=(jax.ShapeDtypeStruct((2, 64, 1792...  3.1 us
  transfers between devices with their start and end apart: 13, of which 10 were waited for; matrix products, arithmetic and copies ran while one was open for 1% of the time, Pallas kernels for 0%

profile of v1, /device:TPU:1, one launch (start us, length us, event | category | flops | bytes accessed | tf_op | source)
XLA Modules:
  0.0 120.1 jit_solution(17778140585884554043)
XLA Ops:
  0.0 0.7 fusion.9
  0.7 0.1 copy.9
  0.9 0.1 select_reduce_fusion.1
  1.0 0.7 reshape.17.inv_ref
  1.6 0.6 pad_add_fusion.core_ref.pos_ref
  2.2 4.7 %place.1 = (bf16[1024,768]{1,0:T(8,128)(2,1)}, bf16[256,768]{1,0:T(8,128)(2,1)}, bf16[256,768]{1,0:T(8,128)(2,1)}, bf16[256,768]{1,0:T(8,128)(2,1)}, bf16[256,768]{1,0:T(8,128)(2,1)}) custom-call(s32[2]{0:T(128)} %pad_add_fusion.core_ref.pos_ref, s32[192]{0:T(256)} %reshape.17.inv_ref, bf16[96,64,64]{2,1,0:T(8,128)(2,1)} %bitcast.19), custom_call_target="tpu_custom_call" | custom-call | tf_op jit(solution)/shard_map/place/pallas_call | solution.py:70
  6.9 4.6 %collective-permute-start = (bf16[256,768]{1,0:T(8,128)(2,1)}, bf16[256,768]{1,0:T(8,128)(2,1)S(1)}, u32[]{:S(2)}, u32[]{:S(2)}) collective-permute-start(bf16[256,768]{1,0:T(8,128)(2,1)} %get-tuple-element.17), channel_id=1, source_target_pairs={{0,31},{1,2},{2,1},{3,4},{4,3},{5,6},{6,5},{7,8},{8,7},{9,10},{10,... | collective-permute-start | bytes 1179656 | tf_op jit(solution)/shard_map/ppermute | solution.py:26
  11.5 6.1 %collective-permute-start.1 = (bf16[256,768]{1,0:T(8,128)(2,1)}, bf16[256,768]{1,0:T(8,128)(2,1)S(1)}, u32[]{:S(2)}, u32[]{:S(2)}) collective-permute-start(bf16[256,768]{1,0:T(8,128)(2,1)} %get-tuple-element.18), channel_id=1, source_target_pairs={{0,1},{1,0},{2,3},{3,2},{4,5},{5,4},{6,7},{7,6},{8,9},{9,8},{10,11... | collective-permute-start | bytes 1179656 | tf_op jit(solution)/shard_map/ppermute | solution.py:26
  17.6 2.8 %collective-permute-start.2 = (bf16[256,768]{1,0:T(8,128)(2,1)}, bf16[256,768]{1,0:T(8,128)(2,1)S(1)}, u32[]{:S(2)}, u32[]{:S(2)}) collective-permute-start(bf16[256,768]{1,0:T(8,128)(2,1)} %get-tuple-element.19), channel_id=1, source_target_pairs={{0,32},{1,33},{2,34},{3,35},{4,36},{5,37},{6,38},{7,39},{8,40},{9,... | collective-permute-start | bytes 1179656 | tf_op jit(solution)/shard_map/ppermute | solution.py:26
  20.5 9.5 %collective-permute-start.3 = (bf16[256,768]{1,0:T(8,128)(2,1)}, bf16[256,768]{1,0:T(8,128)(2,1)S(1)}, u32[]{:S(2)}, u32[]{:S(2)}) collective-permute-start(bf16[256,768]{1,0:T(8,128)(2,1)} %get-tuple-element.20), channel_id=1, source_target_pairs={{0,480},{1,481},{2,482},{3,483},{4,484},{5,485},{6,486},{7,487},{8... | collective-permute-start | bytes 1179656 | tf_op jit(solution)/shard_map/ppermute | solution.py:26
  30.0 0.1 copy.7
  30.1 0.1 select_reduce_fusion
  30.2 0.0 collective-permute-done.cross_ref
  30.2 0.0 copy-start.1
  30.2 0.0 collective-permute-done.1.chip_ref
  30.2 0.0 copy-start.2
  30.3 1.9 %collective-permute-start.4 = (bf16[128,768]{1,0:T(8,128)(2,1)S(1)}, bf16[128,768]{1,0:T(8,128)(2,1)S(1)}, u32[]{:S(2)}, u32[]{:S(2)}) collective-permute-start(bf16[128,768]{1,0:T(8,128)(2,1)S(1)} %pad_maximum_fusion), channel_id=1, source_target_pairs={{0,32},{1,33},{2,34},{3,35},{4,36},{5,37},{6,38},{7,39},{8,40},{9,... | collective-permute-start | bytes 589832 | tf_op jit(solution)/shard_map/ppermute | solution.py:26
  32.3 4.6 %collective-permute-start.5 = (bf16[128,768]{1,0:T(8,128)(2,1)S(1)}, bf16[128,768]{1,0:T(8,128)(2,1)S(1)}, u32[]{:S(2)}, u32[]{:S(2)}) collective-permute-start(bf16[128,768]{1,0:T(8,128)(2,1)S(1)} %pad_maximum_fusion.1), channel_id=1, source_target_pairs={{0,480},{1,481},{2,482},{3,483},{4,484},{5,485},{6,486},{7,487},{8... | collective-permute-start | bytes 589832 | tf_op jit(solution)/shard_map/ppermute | solution.py:26
  36.8 0.1 compare_select_fusion
  36.9 0.7 reshape.15.aidx_ref
  37.6 0.1 collective-permute-done.2.up_ref
  37.7 1.0 collective-permute-done.3.down_ref
  38.7 3.2 %collective-permute-done.4.upc_ref = bf16[128,768]{1,0:T(8,128)(2,1)S(1)} collective-permute-done((bf16[128,768]{1,0:T(8,128)(2,1)S(1)}, bf16[128,768]{1,0:T(8,128)(2,1)S(1)}, u32[]{:S(2)}, u32[]{:S(2)}) %collective-permute-start.4) | collective-permute-done | bytes 196640 | tf_op jit(solution)/shard_map/ppermute | solution.py:26
  41.9 0.9 collective-permute-done.5.downc_ref
  42.8 0.0 copy-done.4
  42.8 0.0 copy-done.5
  42.8 0.7 copy-done.9
  43.5 10.8 %products.1 = (f32[256,1280]{1,0:T(8,128)}, bf16[256,1280]{1,0:T(8,128)(2,1)}, bf16[128,1280]{1,0:T(8,128)(2,1)}, bf16[128,1280]{1,0:T(8,128)(2,1)}) custom-call(s32[2]{0:T(128)} %pad_add_fusion.core_ref.pos_ref, s32[144]{0:T(256)} %reshape.15.aidx_ref, bf16[144,64,64]{2,1,0:T(8,128)(2,1)} %bitcast.18, bf16[1024,768]{1,0:T(8,128)(2,1)} %get-tuple-element.16.po_ref, ...), custom_call_target="tpu_custom_call" | custom-call | tf_op jit(solution)/shard_map/products/pallas_call | solution.py:198
  54.3 2.8 %collective-permute-start.6 = (bf16[256,1280]{1,0:T(8,128)(2,1)}, bf16[256,1280]{1,0:T(8,128)(2,1)S(1)}, u32[]{:S(2)}, u32[]{:S(2)}) collective-permute-start(bf16[256,1280]{1,0:T(8,128)(2,1)} %get-tuple-element.22), channel_id=1, source_target_pairs={{0,1},{1,0},{2,3},{3,2},{4,5},{5,4},{6,7},{7,6},{8,9},{9,8},{10,11... | collective-permute-start | bytes 1966088 | tf_op jit(solution)/shard_map/ppermute | solution.py:26
  57.1 1.9 %collective-permute-start.7 = (bf16[128,1280]{1,0:T(8,128)(2,1)}, bf16[128,1280]{1,0:T(8,128)(2,1)S(1)}, u32[]{:S(2)}, u32[]{:S(2)}) collective-permute-start(bf16[128,1280]{1,0:T(8,128)(2,1)} %get-tuple-element.23), channel_id=1, source_target_pairs={{0,30},{1,3},{2,0},{3,5},{4,2},{5,7},{6,4},{7,9},{8,6},{9,11},{10,... | collective-permute-start | bytes 983048 | tf_op jit(solution)/shard_map/ppermute | solution.py:26
  59.0 3.5 %collective-permute-start.8 = (bf16[128,1280]{1,0:T(8,128)(2,1)}, bf16[128,1280]{1,0:T(8,128)(2,1)S(1)}, u32[]{:S(2)}, u32[]{:S(2)}) collective-permute-start(bf16[128,1280]{1,0:T(8,128)(2,1)} %get-tuple-element.24), channel_id=1, source_target_pairs={{0,31},{1,2},{2,1},{3,4},{4,3},{5,6},{6,5},{7,8},{8,7},{9,10},{10,... | collective-permute-start | bytes 983048 | tf_op jit(solution)/shard_map/ppermute | solution.py:26
  62.6 5.9 %collective-permute-done.7.same_ref = bf16[128,1280]{1,0:T(8,128)(2,1)S(1)} collective-permute-done((bf16[128,1280]{1,0:T(8,128)(2,1)}, bf16[128,1280]{1,0:T(8,128)(2,1)S(1)}, u32[]{:S(2)}, u32[]{:S(2)}) %collective-permute-start.7) | collective-permute-done | bytes 327712 | tf_op jit(solution)/shard_map/ppermute | solution.py:26
  68.4 1.0 collective-permute-done.8.other_ref
  69.4 0.0 collective-permute-done.6.swap_ref
  69.4 0.7 copy-done.7
  70.1 0.3 copy-done.3
  70.4 3.1 %merge.1 = (f32[2,64,1792]{2,1,0:T(8,128)}, bf16[2,64,1792]{2,1,0:T(8,128)(2,1)}) custom-call(s32[2]{0:T(128)} %pad_add_fusion.core_ref.pos_ref, f32[256,1280]{1,0:T(8,128)} %get-tuple-element.21.keep_ref, bf16[256,1280]{1,0:T(8,128)(2,1)} %copy-done.3, bf16[128,1280]{1,0:T(8,128)(2,1)} %copy-done.6, bf16[128,1280]{1,0:T(8,128)(2,1)} %copy-done.7), custom_call_target="tpu_custom_call" | custom-call | tf_op jit(solution)/shard_map/merge/pallas_call | solution.py:241
  73.5 5.4 %collective-permute-start.9 = (bf16[2,64,1792]{2,1,0:T(8,128)(2,1)}, bf16[2,64,1792]{2,1,0:T(8,128)(2,1)S(1)}, u32[]{:S(2)}, u32[]{:S(2)}) collective-permute-start(bf16[2,64,1792]{2,1,0:T(8,128)(2,1)} %get-tuple-element.26), channel_id=1, source_target_pairs={{0,32},{1,481},{2,34},{3,483},{4,36},{5,485},{6,38},{7,487},{8,40}... | collective-permute-start | bytes 1376264 | tf_op jit(solution)/shard_map/ppermute | solution.py:26
  78.9 5.7 %collective-permute-done.9 = bf16[2,64,1792]{2,1,0:T(8,128)(2,1)S(1)} collective-permute-done((bf16[2,64,1792]{2,1,0:T(8,128)(2,1)}, bf16[2,64,1792]{2,1,0:T(8,128)(2,1)S(1)}, u32[]{:S(2)}, u32[]{:S(2)}) %collective-permute-start.9) | collective-permute-done | bytes 458784 | tf_op jit(solution)/shard_map/ppermute | solution.py:26
  84.7 0.1 convert_element_type.15
  84.7 0.1 slice_add_fusion.1
  84.8 4.0 %collective-permute-start.10 = (bf16[2,32,1792]{2,1,0:T(8,128)(2,1)S(1)}, bf16[2,32,1792]{2,1,0:T(8,128)(2,1)S(1)}, u32[]{:S(2)}, u32[]{:S(2)}) collective-permute-start(bf16[2,32,1792]{2,1,0:T(8,128)(2,1)S(1)} %get-tuple-element.28), channel_id=1, source_target_pairs={{0,64},{1,449},{2,66},{3,451},{4,68},{5,453},{6,70},{7,455},{8,72}... | collective-permute-start | bytes 688136 | tf_op jit(solution)/shard_map/ppermute | solution.py:26
  88.8 4.9 %collective-permute-done.10 = bf16[2,32,1792]{2,1,0:T(8,128)(2,1)S(1)} collective-permute-done((bf16[2,32,1792]{2,1,0:T(8,128)(2,1)S(1)}, bf16[2,32,1792]{2,1,0:T(8,128)(2,1)S(1)}, u32[]{:S(2)}, u32[]{:S(2)}) %collective-permute-start.10) | collective-permute-done | bytes 229408 | tf_op jit(solution)/shard_map/ppermute | solution.py:26
  93.8 6.9 %collective-permute-start.11 = (bf16[2,16,1792]{2,1,0:T(8,128)(2,1)S(1)}, bf16[2,16,1792]{2,1,0:T(8,128)(2,1)S(1)}, u32[]{:S(2)}, u32[]{:S(2)}) collective-permute-start(bf16[2,16,1792]{2,1,0:T(8,128)(2,1)S(1)} %fusion.1), channel_id=1, source_target_pairs={{0,128},{1,385},{2,130},{3,387},{4,132},{5,389},{6,134},{7,391},{8... | collective-permute-start | bytes 344072 | tf_op jit(solution)/shard_map/ppermute | solution.py:26
  100.7 5.1 %collective-permute-done.11 = bf16[2,16,1792]{2,1,0:T(8,128)(2,1)S(1)} collective-permute-done((bf16[2,16,1792]{2,1,0:T(8,128)(2,1)S(1)}, bf16[2,16,1792]{2,1,0:T(8,128)(2,1)S(1)}, u32[]{:S(2)}, u32[]{:S(2)}) %collective-permute-start.11) | collective-permute-done | bytes 114720 | tf_op jit(solution)/shard_map/ppermute | solution.py:26
  105.9 11.1 %collective-permute-start.12 = (f32[16,1792]{1,0:T(8,128)S(1)}, f32[16,1792]{1,0:T(8,128)S(1)}, u32[]{:S(2)}, u32[]{:S(2)}) collective-permute-start(f32[16,1792]{1,0:T(8,128)S(1)} %slice_bitcast_fusion), channel_id=1, source_target_pairs={{0,33},{1,480},{2,35},{3,482},{4,37},{5,484},{6,39},{7,486},{8,41}... | collective-permute-start | bytes 344072 | tf_op jit(solution)/shard_map/ppermute | solution.py:26
  117.0 2.5 %collective-permute-done.12 = f32[16,1792]{1,0:T(8,128)S(1)} collective-permute-done((f32[16,1792]{1,0:T(8,128)S(1)}, f32[16,1792]{1,0:T(8,128)S(1)}, u32[]{:S(2)}, u32[]{:S(2)}) %collective-permute-start.12) | collective-permute-done | bytes 114720 | tf_op jit(solution)/shard_map/ppermute | solution.py:26
  119.4 0.7 fusion.4
  (28 shorter events, 0.2 us)
Async XLA Ops:
  0.0 30.0 %copy-start.10 = (s32[4,4,9]{2,1,0:T(4,128)S(1)}, s32[4,4,9]{2,1,0:T(4,128)}, u32[]{:S(2)}) copy-start(s32[4,4,9]{2,1,0:T(4,128)} %param.6) | copy-start | bytes 1732
  2.2 34.6 %copy-start.11 = (s32[4,4]{1,0:T(4,128)S(1)}, s32[4,4]{1,0:T(4,128)}, u32[]{:S(2)}) copy-start(s32[4,4]{1,0:T(4,128)} %param.7) | copy-start | bytes 196
  6.9 23.3 %collective-permute-start = (bf16[256,768]{1,0:T(8,128)(2,1)}, bf16[256,768]{1,0:T(8,128)(2,1)S(1)}, u32[]{:S(2)}, u32[]{:S(2)}) collective-permute-start(bf16[256,768]{1,0:T(8,128)(2,1)} %get-tuple-element.17), channel_id=1, source_target_pairs={{0,31},{1,2},{2,1},{3,4},{4,3},{5,6},{6,5},{7,8},{8,7},{9,10},{10,... | collective-permute-start | bytes 1179656 | tf_op jit(solution)/shard_map/ppermute | solution.py:26
  11.5 18.7 %collective-permute-start.1 = (bf16[256,768]{1,0:T(8,128)(2,1)}, bf16[256,768]{1,0:T(8,128)(2,1)S(1)}, u32[]{:S(2)}, u32[]{:S(2)}) collective-permute-start(bf16[256,768]{1,0:T(8,128)(2,1)} %get-tuple-element.18), channel_id=1, source_target_pairs={{0,1},{1,0},{2,3},{3,2},{4,5},{5,4},{6,7},{7,6},{8,9},{9,8},{10,11... | collective-permute-start | bytes 1179656 | tf_op jit(solution)/shard_map/ppermute | solution.py:26
  17.6 20.1 %collective-permute-start.2 = (bf16[256,768]{1,0:T(8,128)(2,1)}, bf16[256,768]{1,0:T(8,128)(2,1)S(1)}, u32[]{:S(2)}, u32[]{:S(2)}) collective-permute-start(bf16[256,768]{1,0:T(8,128)(2,1)} %get-tuple-element.19), channel_id=1, source_target_pairs={{0,32},{1,33},{2,34},{3,35},{4,36},{5,37},{6,38},{7,39},{8,40},{9,... | collective-permute-start | bytes 1179656 | tf_op jit(solution)/shard_map/ppermute | solution.py:26
  20.5 18.3 %collective-permute-start.3 = (bf16[256,768]{1,0:T(8,128)(2,1)}, bf16[256,768]{1,0:T(8,128)(2,1)S(1)}, u32[]{:S(2)}, u32[]{:S(2)}) collective-permute-start(bf16[256,768]{1,0:T(8,128)(2,1)} %get-tuple-element.20), channel_id=1, source_target_pairs={{0,480},{1,481},{2,482},{3,483},{4,484},{5,485},{6,486},{7,487},{8... | collective-permute-start | bytes 1179656 | tf_op jit(solution)/shard_map/ppermute | solution.py:26
  30.2 12.6 %copy-start.1 = (bf16[256,768]{1,0:T(8,128)(2,1)}, bf16[256,768]{1,0:T(8,128)(2,1)S(1)}, u32[]{:S(2)}) copy-start(bf16[256,768]{1,0:T(8,128)(2,1)S(1)} %collective-permute-done.cross_ref) | copy-start | bytes 1179652
  30.2 12.6 %copy-start.2 = (bf16[256,768]{1,0:T(8,128)(2,1)}, bf16[256,768]{1,0:T(8,128)(2,1)S(1)}, u32[]{:S(2)}) copy-start(bf16[256,768]{1,0:T(8,128)(2,1)S(1)} %collective-permute-done.1.chip_ref) | copy-start | bytes 1179652
  30.3 11.6 %collective-permute-start.4 = (bf16[128,768]{1,0:T(8,128)(2,1)S(1)}, bf16[128,768]{1,0:T(8,128)(2,1)S(1)}, u32[]{:S(2)}, u32[]{:S(2)}) collective-permute-start(bf16[128,768]{1,0:T(8,128)(2,1)S(1)} %pad_maximum_fusion), channel_id=1, source_target_pairs={{0,32},{1,33},{2,34},{3,35},{4,36},{5,37},{6,38},{7,39},{8,40},{9,... | collective-permute-start | bytes 589832 | tf_op jit(solution)/shard_map/ppermute | solution.py:26
  32.3 10.6 %collective-permute-start.5 = (bf16[128,768]{1,0:T(8,128)(2,1)S(1)}, bf16[128,768]{1,0:T(8,128)(2,1)S(1)}, u32[]{:S(2)}, u32[]{:S(2)}) collective-permute-start(bf16[128,768]{1,0:T(8,128)(2,1)S(1)} %pad_maximum_fusion.1), channel_id=1, source_target_pairs={{0,480},{1,481},{2,482},{3,483},{4,484},{5,485},{6,486},{7,487},{8... | collective-permute-start | bytes 589832 | tf_op jit(solution)/shard_map/ppermute | solution.py:26
  37.7 5.1 %copy-start.4 = (bf16[256,768]{1,0:T(8,128)(2,1)}, bf16[256,768]{1,0:T(8,128)(2,1)S(1)}, u32[]{:S(2)}) copy-start(bf16[256,768]{1,0:T(8,128)(2,1)S(1)} %collective-permute-done.2.up_ref) | copy-start | bytes 1179652
  38.7 4.1 %copy-start.5 = (bf16[256,768]{1,0:T(8,128)(2,1)}, bf16[256,768]{1,0:T(8,128)(2,1)S(1)}, u32[]{:S(2)}) copy-start(bf16[256,768]{1,0:T(8,128)(2,1)S(1)} %collective-permute-done.3.down_ref) | copy-start | bytes 1179652
  41.9 0.9 copy-start.8
  42.8 0.7 copy-start.9
  54.3 15.1 %collective-permute-start.6 = (bf16[256,1280]{1,0:T(8,128)(2,1)}, bf16[256,1280]{1,0:T(8,128)(2,1)S(1)}, u32[]{:S(2)}, u32[]{:S(2)}) collective-permute-start(bf16[256,1280]{1,0:T(8,128)(2,1)} %get-tuple-element.22), channel_id=1, source_target_pairs={{0,1},{1,0},{2,3},{3,2},{4,5},{5,4},{6,7},{7,6},{8,9},{9,8},{10,11... | collective-permute-start | bytes 1966088 | tf_op jit(solution)/shard_map/ppermute | solution.py:26
  57.1 11.3 %collective-permute-start.7 = (bf16[128,1280]{1,0:T(8,128)(2,1)}, bf16[128,1280]{1,0:T(8,128)(2,1)S(1)}, u32[]{:S(2)}, u32[]{:S(2)}) collective-permute-start(bf16[128,1280]{1,0:T(8,128)(2,1)} %get-tuple-element.23), channel_id=1, source_target_pairs={{0,30},{1,3},{2,0},{3,5},{4,2},{5,7},{6,4},{7,9},{8,6},{9,11},{10,... | collective-permute-start | bytes 983048 | tf_op jit(solution)/shard_map/ppermute | solution.py:26
  59.0 10.4 %collective-permute-start.8 = (bf16[128,1280]{1,0:T(8,128)(2,1)}, bf16[128,1280]{1,0:T(8,128)(2,1)S(1)}, u32[]{:S(2)}, u32[]{:S(2)}) collective-permute-start(bf16[128,1280]{1,0:T(8,128)(2,1)} %get-tuple-element.24), channel_id=1, source_target_pairs={{0,31},{1,2},{2,1},{3,4},{4,3},{5,6},{6,5},{7,8},{8,7},{9,10},{10,... | collective-permute-start | bytes 983048 | tf_op jit(solution)/shard_map/ppermute | solution.py:26
  68.4 1.0 copy-start.6
  69.4 0.7 copy-start.7
  69.4 1.0 copy-start.3
  73.5 11.2 %copy-start = (f32[2,64,1792]{2,1,0:T(8,128)S(1)}, f32[2,64,1792]{2,1,0:T(8,128)}, u32[]{:S(2)}) copy-start(f32[2,64,1792]{2,1,0:T(8,128)} %get-tuple-element.25) | copy-start | bytes 2752516
  73.5 11.2 %collective-permute-start.9 = (bf16[2,64,1792]{2,1,0:T(8,128)(2,1)}, bf16[2,64,1792]{2,1,0:T(8,128)(2,1)S(1)}, u32[]{:S(2)}, u32[]{:S(2)}) collective-permute-start(bf16[2,64,1792]{2,1,0:T(8,128)(2,1)} %get-tuple-element.26), channel_id=1, source_target_pairs={{0,32},{1,481},{2,34},{3,483},{4,36},{5,485},{6,38},{7,487},{8,40}... | collective-permute-start | bytes 1376264 | tf_op jit(solution)/shard_map/ppermute | solution.py:26
  84.8 8.9 %collective-permute-start.10 = (bf16[2,32,1792]{2,1,0:T(8,128)(2,1)S(1)}, bf16[2,32,1792]{2,1,0:T(8,128)(2,1)S(1)}, u32[]{:S(2)}, u32[]{:S(2)}) collective-permute-start(bf16[2,32,1792]{2,1,0:T(8,128)(2,1)S(1)} %get-tuple-element.28), channel_id=1, source_target_pairs={{0,64},{1,449},{2,66},{3,451},{4,68},{5,453},{6,70},{7,455},{8,72}... | collective-permute-start | bytes 688136 | tf_op jit(solution)/shard_map/ppermute | solution.py:26
  93.8 12.0 %collective-permute-start.11 = (bf16[2,16,1792]{2,1,0:T(8,128)(2,1)S(1)}, bf16[2,16,1792]{2,1,0:T(8,128)(2,1)S(1)}, u32[]{:S(2)}, u32[]{:S(2)}) collective-permute-start(bf16[2,16,1792]{2,1,0:T(8,128)(2,1)S(1)} %fusion.1), channel_id=1, source_target_pairs={{0,128},{1,385},{2,130},{3,387},{4,132},{5,389},{6,134},{7,391},{8... | collective-permute-start | bytes 344072 | tf_op jit(solution)/shard_map/ppermute | solution.py:26
  105.9 13.5 %collective-permute-start.12 = (f32[16,1792]{1,0:T(8,128)S(1)}, f32[16,1792]{1,0:T(8,128)S(1)}, u32[]{:S(2)}, u32[]{:S(2)}) collective-permute-start(f32[16,1792]{1,0:T(8,128)S(1)} %slice_bitcast_fusion), channel_id=1, source_target_pairs={{0,33},{1,480},{2,35},{3,482},{4,37},{5,484},{6,39},{7,486},{8,41}... | collective-permute-start | bytes 344072 | tf_op jit(solution)/shard_map/ppermute | solution.py:26

commit v2 on v1

v2 whole, which is shorter than its diff:
```python
import jax
import jax.numpy as jnp
from jax import lax
from jax.experimental import pallas as pl
from jax.experimental.pallas import tpu as pltpu
from jax.sharding import PartitionSpec as P


CB = 4
B = 64
ROWS = 16
COLS = 32
F32 = jnp.float32
BF16 = jnp.bfloat16


def joint(rule):
    pairs = []
    for r in range(ROWS):
        for s in range(COLS):
            r2, s2 = rule(r, s)
            pairs.append((r * COLS + s, (r2 % ROWS) * COLS + s2 % COLS))
    return pairs


def send(value, rule):
    return lax.ppermute(value, ("row", "col"), joint(rule))


def sign(s):
    return 1 if s % 2 == 0 else -1


def place_kernel(core_ref, inv_ref, p_ref, po_ref, cross_ref, chip_ref, up_ref, down_ref):
    def block(b, carry):
        y = b // 4
        x = b % 4
        row = pl.multiple_of(b * B, B)

        def tile(r):
            j = inv_ref[b * 12 + r]
            value = p_ref[(x * 4 + y) * 6 + jnp.maximum(j - 1, 0)]
            return jnp.where(j > 0, value, jnp.zeros_like(value))

        for m in range(6):
            pair = jnp.concatenate([tile(2 * m), tile(2 * m + 1)], axis=1)
            po_ref[pl.ds(row, B), 128 * m : 128 * (m + 1)] = pair
        return carry

    lax.fori_loop(0, 16, block, 0)
    core = core_ref[0]
    cross_row = pl.multiple_of(core * 768, 256)
    chip_row = pl.multiple_of(768 - core * 768, 256)
    cross_ref[...] = po_ref[pl.ds(cross_row, 256), :]
    chip_ref[...] = po_ref[pl.ds(chip_row, 256), :]
    for y in range(4):
        up_ref[64 * y : 64 * y + 64, :] = po_ref[256 * y + 192 : 256 * y + 256, :]
        down_ref[64 * y : 64 * y + 64, :] = po_ref[256 * y : 256 * y + 64, :]


def smem():
    return pl.BlockSpec(memory_space=pltpu.SMEM)


def vmem():
    return pl.BlockSpec(memory_space=pltpu.VMEM)


def budget(mib, flops, moved):
    return dict(
        compiler_params=pltpu.CompilerParams(vmem_limit_bytes=mib << 20),
        cost_estimate=pl.CostEstimate(flops=flops, bytes_accessed=moved, transcendentals=0),
    )


def place(core, inv, tiles):
    edge = jax.ShapeDtypeStruct((256, 768), BF16)
    return pl.pallas_call(
        place_kernel,
        out_shape=(jax.ShapeDtypeStruct((1024, 768), BF16), edge, edge, edge, edge),
        in_specs=[smem(), smem(), vmem()],
        out_specs=(vmem(),) * 5,
        name="place",
        **budget(6, 0, 6000000),
    )(core, inv, tiles)


SLOTS = (
    ((1, 2), (None, None), (0, None)),
    ((0, 1), (2, None), (None, None)),
    ((None, 0), (1, 2), (None, None)),
    ((None, None), (0, 1), (None, 2)),
)


def dot(a, b):
    return jnp.dot(a, b, preferred_element_type=F32)


def local_kernel(pos_ref, aidx_ref, a_ref, po_ref, ad_ref, outer_ref, rest_ref, im_ref):
    core = pos_ref[0]
    r = pos_ref[1]

    def fill(b, carry):
        y = b // 4

        def tile(x, c):
            if c is None:
                return jnp.zeros((B, B), BF16)
            k = aidx_ref[(y * 4 + x) * 9 + c]
            value = a_ref[(x * 4 + y) * 9 + jnp.maximum(k, 0)]
            return jnp.where(k >= 0, value, jnp.zeros_like(value))

        for x in range(4):
            @pl.when(b % 4 == x)
            def _():
                for dy in range(3):
                    for m in range(3):
                        left, right = SLOTS[x][m]
                        left = None if left is None else left * 3 + dy
                        right = None if right is None else right * 3 + dy
                        pair = jnp.concatenate([tile(x, left), tile(x, right)], axis=1)
                        lane = 256 * dy + 128 * m if m < 2 else 768 + 128 * dy
                        ad_ref[y, 64 * x : 64 * x + 64, lane : lane + 128] = pair
        return carry

    lax.fori_loop(0, 16, fill, 0)

    for y in range(4):
        first = 1 if y == 0 else 0
        last = 1 if y == 3 else 2
        im_ref[256 * y : 256 * y + 256, :] = dot(
            ad_ref[y, :, 256 * first : 256 * last + 256],
            po_ref[256 * (y + first - 1) : 256 * (y + last), :],
        )

    windows = ((core * 2, 1 - core), (1 + core * 0, core), (2 - core * 2, 1 - core))
    for n, (window, kind) in enumerate(windows):
        lanes = pl.ds(pl.multiple_of(window * 256, 256), 256)
        for y in range(4):
            flipped = po_ref[256 * y : 256 * y + 256, lanes].T
            for o in range(16):
                shifted = (o - r - kind + 32) % 16
                flow = shifted // 8
                near = jnp.where(flow == 0, shifted, 15 - shifted)
                half = (flow + core) % 2
                spot = half * 8 + (near % 4) * 2 + near // 4
                row = pl.multiple_of(max(n - 1, 0) * 256 + spot * 16, 16)
                pt_ref = rest_ref if n else outer_ref
                pt_ref[pl.ds(row, 16), 256 * y : 256 * y + 256] = flipped[16 * o : 16 * o + 16, :]


def local_products(pos, aidx, a, po):
    return pl.pallas_call(
        local_kernel,
        out_shape=(
            jax.ShapeDtypeStruct((4, 256, 1152), BF16),
            jax.ShapeDtypeStruct((256, 1024), BF16),
            jax.ShapeDtypeStruct((512, 1024), BF16),
            jax.ShapeDtypeStruct((1024, 768), F32),
        ),
        in_specs=[smem(), smem(), vmem(), vmem()],
        out_specs=(vmem(),) * 4,
        name="local_products",
        **budget(12, 1000000000, 12000000),
    )(pos, aidx, a, po)


def pieces(pt_ref, base, im_ref, store):
    for chunk in range(5):
        k = slice(0, 256) if chunk == 0 else slice(768, 1024) if chunk == 4 else slice(0, 1024)
        cols = slice(256 * chunk, 256 * chunk + 256)
        store(cols, dot(pt_ref[base : base + 256, k], im_ref[k, cols]))


def halo_kernel(
    pos_ref, ad_ref, pt_ref, part_ref, cross_ref, chip_ref, up_ref, down_ref, upc_ref, downc_ref,
    im_ref, same_ref, other_ref, side_ref, hr_ref,
):
    core = pos_ref[0]
    for y in range(4):
        hr_ref[y + 1, 0:64, :] = up_ref[64 * y : 64 * y + 64, :]
        hr_ref[y + 1, 64:128, :] = down_ref[64 * y : 64 * y + 64, :]
    side_ref[core] = cross_ref[...]
    side_ref[1 - core] = chip_ref[...]
    hr_ref[core * 5, 0:64, :] = upc_ref[0:64, :]
    hr_ref[core * 5, 64:128, :] = downc_ref[0:64, :]
    hr_ref[5 - core * 5, 0:64, :] = upc_ref[64:128, :]
    hr_ref[5 - core * 5, 64:128, :] = downc_ref[64:128, :]

    for y in range(4):
        rows = slice(256 * y, 256 * y + 256)
        first = 1 if y == 0 else 0
        last = 1 if y == 3 else 2
        count = last - first + 1
        total = part_ref[rows, :] + dot(
            ad_ref[y, :, 768 + 128 * first : 896 + 128 * last],
            hr_ref[y + first : y + last + 1].reshape(128 * count, 768),
        )
        if count == 3:
            im_ref[rows, 256:1024] = total.astype(BF16)
            continue
        dy, side, at = (0, 0, 0) if y == 0 else (2, 1, 5)
        edge = dot(ad_ref[y, :, 256 * dy : 256 * dy + 256], side_ref[side])
        edge = edge + dot(ad_ref[y, :, 768 + 128 * dy : 896 + 128 * dy], hr_ref[at])
        if y == 0:
            im_ref[rows, 0:256] = edge[:, 0:256].astype(BF16)
            im_ref[rows, 256:768] = (edge[:, 256:768] + total[:, 0:512]).astype(BF16)
            im_ref[rows, 768:1024] = total[:, 512:768].astype(BF16)
        else:
            im_ref[rows, 256:512] = total[:, 0:256].astype(BF16)
            im_ref[rows, 512:1024] = (edge[:, 0:512] + total[:, 256:768]).astype(BF16)
            im_ref[rows, 1024:1280] = edge[:, 512:768].astype(BF16)

    def store(cols, out):
        same_ref[:, cols] = out[0:128].astype(BF16)
        other_ref[:, cols] = out[128:256].astype(BF16)

    pieces(pt_ref, 0, im_ref, store)


def halo_products(pos, ad, pt, part, *halo):
    half = jax.ShapeDtypeStruct((128, 1280), BF16)
    return pl.pallas_call(
        halo_kernel,
        out_shape=(jax.ShapeDtypeStruct((1024, 1280), BF16), half, half),
        in_specs=[smem()] + [vmem()] * 9,
        out_specs=(vmem(),) * 3,
        scratch_shapes=[pltpu.VMEM((2, 256, 768), BF16), pltpu.VMEM((6, 128, 768), BF16)],
        name="halo_products",
        **budget(12, 1500000000, 12000000),
    )(pos, ad, pt, part, *halo)


def own_kernel(pt_ref, im_ref, keep_ref, swap_ref):
    for n in range(2):
        def store(cols, out):
            keep_ref[128 * n : 128 * n + 128, cols] = out[0:128]
            swap_ref[128 * n : 128 * n + 128, cols] = out[128:256].astype(BF16)

        pieces(pt_ref, 256 * n, im_ref, store)


def own_pieces(pt, im):
    return pl.pallas_call(
        own_kernel,
        out_shape=(
            jax.ShapeDtypeStruct((256, 1280), F32),
            jax.ShapeDtypeStruct((256, 1280), BF16),
        ),
        in_specs=[vmem(), vmem()],
        out_specs=(vmem(), vmem()),
        name="own_pieces",
        **budget(8, 1400000000, 6000000),
    )(pt, im)


def merge_kernel(
    pos_ref, keep_own, keep_partner, swap_own, swap_partner, same_ref, other_ref, out_ref, sum_ref
):
    def merge(low, high):
        def add(n, at, ref):
            sum_ref[n, :, at : at + 1280] += ref[...].astype(F32)

        zero = jnp.zeros((32, 256), F32)
        for n in range(2):
            for at in (0, 256, 1280, 1536):
                sum_ref[n, :, at : at + 256] = zero
        sum_ref[0, :, 256:1536] = keep_own[...]
        sum_ref[1, :, 256:1536] = swap_own[...].astype(F32)
        add(0, high, swap_partner)
        add(0, low, other_ref)
        add(1, low, keep_partner)
        add(1, high, same_ref)

    @pl.when(pos_ref[0] == 0)
    def _():
        merge(0, 512)

    @pl.when(pos_ref[0] == 1)
    def _():
        merge(512, 0)

    out_ref[...] = sum_ref[...].astype(out_ref.dtype)


def merged(pos, keep, swap, same, other, group):
    def rows(at):
        return pl.BlockSpec((32, 1280), lambda i: (at, 0))

    return pl.pallas_call(
        merge_kernel,
        grid=(1,),
        out_shape=jax.ShapeDtypeStruct((2, 32, 1792), F32 if group == 0 else BF16),
        in_specs=[smem()] + [rows(group), rows(group + 4)] * 2 + [rows(group)] * 2,
        out_specs=pl.BlockSpec((2, 32, 1792), lambda i: (0, 0, 0)),
        scratch_shapes=[pltpu.VMEM((2, 32, 1792), F32)],
        **budget(4, 0, 1000000),
    )(pos, keep, keep, swap, swap, same, other)


def body(operator_tiles, neighbour_codes, live_slots, prolong_tiles, coarse_blocks):
    r = lax.axis_index("row")
    s = lax.axis_index("col")
    core = s % 2
    pos = jnp.stack([core, r]).astype(jnp.int32)

    place_of = jnp.mod(coarse_blocks // CB - s + 1, COLS) * CB + coarse_blocks % CB
    hit = place_of[..., None] == jnp.arange(12)
    number = jnp.arange(1, 7, dtype=jnp.int32)[:, None]
    inv = jnp.sum(jnp.where(hit, number, 0), axis=2).transpose(1, 0, 2).reshape(-1)
    code_hit = neighbour_codes[..., None] == jnp.arange(9)
    slot = jnp.sum(jnp.where(code_hit, jnp.arange(9, dtype=jnp.int32)[:, None], 0), axis=2)
    slot = jnp.where(slot < live_slots[..., None], slot, -1)
    aidx = slot.transpose(1, 0, 2).reshape(-1)

    po, cross, chip, up, down = place(pos, inv, prolong_tiles.reshape(96, B, B))
    cross_in = send(cross, lambda r, s: (r, s - sign(s)))
    chip_in = send(chip, lambda r, s: (r, s + sign(s)))
    up_in = send(up, lambda r, s: (r + 1, s))
    down_in = send(down, lambda r, s: (r - 1, s))
    upc = jnp.concatenate([cross_in[192:256], chip_in[192:256]], axis=0)
    downc = jnp.concatenate([cross_in[0:64], chip_in[0:64]], axis=0)
    upc_in = send(upc, lambda r, s: (r + 1, s))
    downc_in = send(downc, lambda r, s: (r - 1, s))

    ad, outer, rest, part = local_products(pos, aidx, operator_tiles.reshape(144, B, B), po)
    im, same, other = halo_products(
        pos, ad, outer, part, cross_in, chip_in, up_in, down_in, upc_in, downc_in
    )
    other_in = send(other, lambda r, s: (r, s - sign(s)))
    same_in = send(same, lambda r, s: (r, s - 2 * sign(s)))
    keep, swap = own_pieces(rest, im)
    swap_in = send(swap, lambda r, s: (r, s + sign(s)))
    moved = {}
    for step in (3, 2, 1):
        msg = merged(pos, keep, swap_in, same_in, other_in, step)
        moved[step] = send(msg, lambda r, s: (r + step * sign(s), s))
    acc = merged(pos, keep, swap_in, same_in, other_in, 0)
    for step in (1, 2, 3):
        acc = acc + moved[step].astype(F32)
    msg = acc[:, 16:].astype(BF16)
    acc = acc[:, :16] + send(msg, lambda r, s: (r + 4 * sign(s), s)).astype(F32)
    last = send(acc[1], lambda r, s: (r + sign(s), s + sign(s)))
    return (acc[0] + last)[None]


def solution(mesh):
    in_specs = (
        P("row", "col", None, None, None),
        P("row", "col", None),
        P("row", "col"),
        P("row", "col", None, None, None),
        P("row", "col", None),
    )
    out_specs = P("col", "row", None)
    return jax.shard_map(body, mesh=mesh, in_specs=in_specs, out_specs=out_specs, check_vma=False)
```

time: 121 us -> 113 us (0.934)
  waiting for transfers between devices: 30.3 us -> 21.5 us
  Pallas kernels: 18.6 us -> 14.1 us
  local copies, waits for them, and re-layouts: 3.27 us -> 5.77 us
  other arithmetic: 2.56 us -> 4.16 us
  starting transfers between devices: 65.1 us -> 66.5 us
    ppermute x13 -> x14, waiting for transfers between devices: 30.3 us -> 21.5 us  [send(): return lax.ppermute(value, ('row', 'col'), joint(rule))]
    unnamed x25 -> x11, local copies, waits for them, and re-layouts: 1.79 us -> 5.41 us
    pallas_call x2 -> x7, Pallas kernels: 13.9 us -> 10.7 us  [the longest x1 4.15 us: local_products(): pl.pallas_call(local_kernel, out_shape=(jax.ShapeDtypeStruct((4, 256, 115...]
    ppermute x13 -> x14, starting transfers between devices: 65.1 us -> 66.5 us  [send(): return lax.ppermute(value, ('row', 'col'), joint(rule))]
    concatenate x2, other arithmetic: 0.03 us -> 1.39 us  [the longest x1 0.7 us: body(): downc = jnp.concatenate([cross_in[0:64], chip_in[0:64]], axis=0)]
    pallas_call x1, Pallas kernels: 4.71 us -> 3.44 us  [place(): pl.pallas_call(place_kernel, out_shape=(jax.ShapeDtypeStruct((1024, 768),...]
  transfers between devices with their start and end apart: 13 -> 14, of which waited for: 10 -> 6; matrix products, arithmetic and copies ran while one was open for 1% -> 3% of each run, Pallas kernels for 0% -> 5%
where the time goes in v2:
time: 113 us; the launch traced here: 112 us
  starting transfers between devices  66.5 us (59%)
  waiting for transfers between devices  21.5 us (19%)
  Pallas kernels  14.1 us (12%)
  local copies, waits for them, and re-layouts  5.77 us (5%)
  other arithmetic  4.16 us (4%)
    ppermute x14, starting transfers between devices, send(): return lax.ppermute(value, ('row', 'col'), joint(rule))  66.5 us
    ppermute x14, waiting for transfers between devices, send(): return lax.ppermute(value, ('row', 'col'), joint(rule))  21.5 us
    unnamed x11, local copies, waits for them, and re-layouts  5.41 us
    pallas_call x1, Pallas kernels, local_products(): pl.pallas_call(local_kernel, out_shape=(jax.ShapeDtypeStruct((4, 256, 115...  4.15 us
    pallas_call x1, Pallas kernels, place(): pl.pallas_call(place_kernel, out_shape=(jax.ShapeDtypeStruct((1024, 768),...  3.44 us
    pallas_call x1, Pallas kernels, halo_products(): pl.pallas_call(halo_kernel, out_shape=(jax.ShapeDtypeStruct((1024, 1280),...  2.88 us
    pallas_call x4, Pallas kernels, merged(): pl.pallas_call(merge_kernel, grid=(1,), out_shape=jax.ShapeDtypeStruct((2...  2.55 us
  transfers between devices with their start and end apart: 14, of which 6 were waited for; matrix products, arithmetic and copies ran while one was open for 3% of the time, Pallas kernels for 5%

profile of v2, /device:TPU:1, one launch (start us, length us, event | category | flops | bytes accessed | tf_op | source)
XLA Modules:
  0.0 112.4 jit_solution(9312988928267499272)
XLA Ops:
  0.0 0.9 fusion.6
  0.9 0.1 copy.9
  1.0 0.1 select_reduce_fusion.1
  1.1 0.1 reshape.17.inv_ref
  1.2 0.1 pad_add_fusion.core_ref.pos_ref
  1.3 1.4 %copy-done.1 = bf16[4,4,6,64,64]{4,3,2,1,0:T(8,128)(2,1)S(1)} copy-done((bf16[4,4,6,64,64]{4,3,2,1,0:T(8,128)(2,1)S(1)}, bf16[4,4,6,64,64]{4,3,2,1,0:T(8,128)(2,1)}, u32[]{:S(2)}) %copy-start.1) | copy-done | bytes 786456
  2.7 3.4 %place.1 = (bf16[1024,768]{1,0:T(8,128)(2,1)S(1)}, bf16[256,768]{1,0:T(8,128)(2,1)}, bf16[256,768]{1,0:T(8,128)(2,1)}, bf16[256,768]{1,0:T(8,128)(2,1)}, bf16[256,768]{1,0:T(8,128)(2,1)}) custom-call(s32[2]{0:T(128)S(1)} %pad_add_fusion.core_ref.pos_ref, s32[192]{0:T(256)S(1)} %reshape.17.inv_ref, bf16[96,64,64]{2,1,0:T(8,128)(2,1)S(1)} %bitcast.19), custom_call_target="tpu_custom_call" | custom-call | bytes 6000000 | tf_op jit(solution)/shard_map/place/pallas_call | solution.py:78
  6.2 1.2 %copy-done.2 = bf16[1024,768]{1,0:T(8,128)(2,1)} copy-done((bf16[1024,768]{1,0:T(8,128)(2,1)}, bf16[1024,768]{1,0:T(8,128)(2,1)S(1)}, u32[]{:S(2)}) %copy-start.2) | copy-done | bytes 1572888
  7.3 4.6 %collective-permute-start = (bf16[256,768]{1,0:T(8,128)(2,1)}, bf16[256,768]{1,0:T(8,128)(2,1)S(1)}, u32[]{:S(2)}, u32[]{:S(2)}) collective-permute-start(bf16[256,768]{1,0:T(8,128)(2,1)} %get-tuple-element.24), channel_id=1, source_target_pairs={{0,31},{1,2},{2,1},{3,4},{4,3},{5,6},{6,5},{7,8},{8,7},{9,10},{10,... | collective-permute-start | bytes 1179656 | tf_op jit(solution)/shard_map/ppermute | solution.py:27
  11.9 6.1 %collective-permute-start.1 = (bf16[256,768]{1,0:T(8,128)(2,1)}, bf16[256,768]{1,0:T(8,128)(2,1)S(1)}, u32[]{:S(2)}, u32[]{:S(2)}) collective-permute-start(bf16[256,768]{1,0:T(8,128)(2,1)} %get-tuple-element.25), channel_id=1, source_target_pairs={{0,1},{1,0},{2,3},{3,2},{4,5},{5,4},{6,7},{7,6},{8,9},{9,8},{10,11... | collective-permute-start | bytes 1179656 | tf_op jit(solution)/shard_map/ppermute | solution.py:27
  18.0 2.8 %collective-permute-start.2 = (bf16[256,768]{1,0:T(8,128)(2,1)}, bf16[256,768]{1,0:T(8,128)(2,1)S(1)}, u32[]{:S(2)}, u32[]{:S(2)}) collective-permute-start(bf16[256,768]{1,0:T(8,128)(2,1)} %get-tuple-element.26), channel_id=1, source_target_pairs={{0,32},{1,33},{2,34},{3,35},{4,36},{5,37},{6,38},{7,39},{8,40},{9,... | collective-permute-start | bytes 1179656 | tf_op jit(solution)/shard_map/ppermute | solution.py:27
  20.8 9.5 %collective-permute-start.3 = (bf16[256,768]{1,0:T(8,128)(2,1)}, bf16[256,768]{1,0:T(8,128)(2,1)}, u32[]{:S(2)}, u32[]{:S(2)}) collective-permute-start(bf16[256,768]{1,0:T(8,128)(2,1)} %get-tuple-element.27), channel_id=1, source_target_pairs={{0,480},{1,481},{2,482},{3,483},{4,484},{5,485},{6,486},{7,487},{8... | collective-permute-start | bytes 1179656 | tf_op jit(solution)/shard_map/ppermute | solution.py:27
  30.4 1.4 %copy.7 = s32[4,4,9]{1,2,0:T(8,128)} copy(s32[4,4,9]{2,1,0:T(4,128)} %param.6) | data formatting | bytes 1152 | tf_op args[1]
  31.8 0.9 select_reduce_fusion
  32.7 0.0 collective-permute-done.1.chip_ref
  32.7 0.7 pad_maximum_fusion
  33.4 1.9 %collective-permute-start.4 = (bf16[128,768]{1,0:T(8,128)(2,1)}, bf16[128,768]{1,0:T(8,128)(2,1)}, u32[]{:S(2)}, u32[]{:S(2)}) collective-permute-start(bf16[128,768]{1,0:T(8,128)(2,1)} %pad_maximum_fusion), channel_id=1, source_target_pairs={{0,32},{1,33},{2,34},{3,35},{4,36},{5,37},{6,38},{7,39},{8,40},{9,... | collective-permute-start | bytes 589832 | tf_op jit(solution)/shard_map/ppermute | solution.py:27
  35.3 0.7 pad_maximum_fusion.1
  36.0 4.6 %collective-permute-start.5 = (bf16[128,768]{1,0:T(8,128)(2,1)}, bf16[128,768]{1,0:T(8,128)(2,1)}, u32[]{:S(2)}, u32[]{:S(2)}) collective-permute-start(bf16[128,768]{1,0:T(8,128)(2,1)} %pad_maximum_fusion.1), channel_id=1, source_target_pairs={{0,480},{1,481},{2,482},{3,483},{4,484},{5,485},{6,486},{7,487},{8... | collective-permute-start | bytes 589832 | tf_op jit(solution)/shard_map/ppermute | solution.py:27
  40.6 0.1 compare_select_fusion
  40.7 0.1 reshape.15.aidx_ref
  40.8 1.4 %copy-done.3 = bf16[1024,768]{1,0:T(8,128)(2,1)S(1)} copy-done((bf16[1024,768]{1,0:T(8,128)(2,1)S(1)}, bf16[1024,768]{1,0:T(8,128)(2,1)}, u32[]{:S(2)}) %copy-start.3) | copy-done | bytes 1572888
  42.2 4.2 %local_products.1 = (bf16[4,256,1152]{2,1,0:T(8,128)(2,1)S(1)}, bf16[256,1024]{1,0:T(8,128)(2,1)S(1)}, bf16[512,1024]{1,0:T(8,128)(2,1)S(1)}, f32[1024,768]{1,0:T(8,128)S(1)}) custom-call(s32[2]{0:T(128)S(1)} %pad_add_fusion.core_ref.pos_ref, s32[144]{0:T(256)S(1)} %reshape.15.aidx_ref, bf16[144,64,64]{2,1,0:T(8,128)(2,1)S(1)} %bitcast.18, ...), custom_call_target="tpu_custom_call" | custom-call | flops 1000000000 | bytes 12000000 | tf_op jit(solution)/shard_map/local_products/pallas_call | solution.py:154
  46.3 0.0 collective-permute-done.2.up_ref
  46.4 0.0 collective-permute-done.4.upc_ref
  46.4 0.0 collective-permute-done.5.downc_ref
  46.4 2.9 %halo_products.1 = (bf16[1024,1280]{1,0:T(8,128)(2,1)S(1)}, bf16[128,1280]{1,0:T(8,128)(2,1)S(1)}, bf16[128,1280]{1,0:T(8,128)(2,1)S(1)}) custom-call(s32[2]{0:T(128)S(1)} %pad_add_fusion.core_ref.pos_ref, bf16[4,256,1152]{2,1,0:T(8,128)(2,1)S(1)} %get-tuple-element.21.ad_ref, bf16[256,1024]{1,0:T(8,128)(2,1)S(1)} %get-tuple-element.22.pt_ref, ...), custom_call_target="tpu_custom_call" | custom-call | flops 1500000000 | bytes 12000000 | tf_op jit(solution)/shard_map/halo_products/pallas_call | solution.py:224
  49.3 1.1 own_pieces.1
  50.4 2.8 %collective-permute-start.6 = (bf16[256,1280]{1,0:T(8,128)(2,1)S(1)}, bf16[256,1280]{1,0:T(8,128)(2,1)S(1)}, u32[]{:S(2)}, u32[]{:S(2)}) collective-permute-start(bf16[256,1280]{1,0:T(8,128)(2,1)S(1)} %get-tuple-element.30), channel_id=1, source_target_pairs={{0,1},{1,0},{2,3},{3,2},{4,5},{5,4},{6,7},{7,6},{8,9},{9,8},{10,11... | collective-permute-start | bytes 1966088 | tf_op jit(solution)/shard_map/ppermute | solution.py:27
  53.2 1.9 %collective-permute-start.7 = (bf16[128,1280]{1,0:T(8,128)(2,1)S(1)}, bf16[128,1280]{1,0:T(8,128)(2,1)S(1)}, u32[]{:S(2)}, u32[]{:S(2)}) collective-permute-start(bf16[128,1280]{1,0:T(8,128)(2,1)S(1)} %get-tuple-element.31), channel_id=1, source_target_pairs={{0,30},{1,3},{2,0},{3,5},{4,2},{5,7},{6,4},{7,9},{8,6},{9,11},{10,... | collective-permute-start | bytes 983048 | tf_op jit(solution)/shard_map/ppermute | solution.py:27
  55.1 3.5 %collective-permute-start.8 = (bf16[128,1280]{1,0:T(8,128)(2,1)S(1)}, bf16[128,1280]{1,0:T(8,128)(2,1)S(1)}, u32[]{:S(2)}, u32[]{:S(2)}) collective-permute-start(bf16[128,1280]{1,0:T(8,128)(2,1)S(1)} %get-tuple-element.32), channel_id=1, source_target_pairs={{0,31},{1,2},{2,1},{3,4},{4,3},{5,6},{6,5},{7,8},{8,7},{9,10},{10,... | collective-permute-start | bytes 983048 | tf_op jit(solution)/shard_map/ppermute | solution.py:27
  58.6 5.7 %collective-permute-done.7.same_ref = bf16[128,1280]{1,0:T(8,128)(2,1)S(1)} collective-permute-done((bf16[128,1280]{1,0:T(8,128)(2,1)S(1)}, bf16[128,1280]{1,0:T(8,128)(2,1)S(1)}, u32[]{:S(2)}, u32[]{:S(2)}) %collective-permute-start.7) | collective-permute-done | bytes 327712 | tf_op jit(solution)/shard_map/ppermute | solution.py:27
  64.3 1.0 collective-permute-done.8.other_ref
  65.3 0.6 shard_map.56
  65.9 4.1 %collective-permute-start.9 = (bf16[2,32,1792]{2,1,0:T(8,128)(2,1)S(1)}, bf16[2,32,1792]{2,1,0:T(8,128)(2,1)S(1)}, u32[]{:S(2)}, u32[]{:S(2)}) collective-permute-start(bf16[2,32,1792]{2,1,0:T(8,128)(2,1)S(1)} %shard_map.56), channel_id=1, source_target_pairs={{0,32},{1,481},{2,34},{3,483},{4,36},{5,485},{6,38},{7,487},{8,40}... | collective-permute-start | bytes 688136 | tf_op jit(solution)/shard_map/ppermute | solution.py:27
  70.0 0.6 shard_map.57
  70.6 1.9 %collective-permute-start.10 = (bf16[2,32,1792]{2,1,0:T(8,128)(2,1)S(1)}, bf16[2,32,1792]{2,1,0:T(8,128)(2,1)S(1)}, u32[]{:S(2)}, u32[]{:S(2)}) collective-permute-start(bf16[2,32,1792]{2,1,0:T(8,128)(2,1)S(1)} %shard_map.57), channel_id=1, source_target_pairs={{0,64},{1,449},{2,66},{3,451},{4,68},{5,453},{6,70},{7,455},{8,72}... | collective-permute-start | bytes 688136 | tf_op jit(solution)/shard_map/ppermute | solution.py:27
  72.6 0.6 shard_map.58
  73.2 5.9 %collective-permute-start.11 = (bf16[2,32,1792]{2,1,0:T(8,128)(2,1)S(1)}, bf16[2,32,1792]{2,1,0:T(8,128)(2,1)S(1)}, u32[]{:S(2)}, u32[]{:S(2)}) collective-permute-start(bf16[2,32,1792]{2,1,0:T(8,128)(2,1)S(1)} %shard_map.58), channel_id=1, source_target_pairs={{0,96},{1,417},{2,98},{3,419},{4,100},{5,421},{6,102},{7,423},{8,1... | collective-permute-start | bytes 688136 | tf_op jit(solution)/shard_map/ppermute | solution.py:27
  79.1 0.6 shard_map.55
  79.8 4.0 %collective-permute-done.10 = bf16[2,32,1792]{2,1,0:T(8,128)(2,1)S(1)} collective-permute-done((bf16[2,32,1792]{2,1,0:T(8,128)(2,1)S(1)}, bf16[2,32,1792]{2,1,0:T(8,128)(2,1)S(1)}, u32[]{:S(2)}, u32[]{:S(2)}) %collective-permute-start.10) | collective-permute-done | bytes 229408 | tf_op jit(solution)/shard_map/ppermute | solution.py:27
  83.8 3.3 %collective-permute-done.11 = bf16[2,32,1792]{2,1,0:T(8,128)(2,1)S(1)} collective-permute-done((bf16[2,32,1792]{2,1,0:T(8,128)(2,1)S(1)}, bf16[2,32,1792]{2,1,0:T(8,128)(2,1)S(1)}, u32[]{:S(2)}, u32[]{:S(2)}) %collective-permute-start.11) | collective-permute-done | bytes 229408 | tf_op jit(solution)/shard_map/ppermute | solution.py:27
  87.0 0.1 convert_add_fusion
  87.1 5.9 %collective-permute-start.12 = (bf16[2,16,1792]{2,1,0:T(8,128)(2,1)S(1)}, bf16[2,16,1792]{2,1,0:T(8,128)(2,1)S(1)}, u32[]{:S(2)}, u32[]{:S(2)}) collective-permute-start(bf16[2,16,1792]{2,1,0:T(8,128)(2,1)S(1)} %slice.49), channel_id=1, source_target_pairs={{0,128},{1,385},{2,130},{3,387},{4,132},{5,389},{6,134},{7,391},{8... | collective-permute-start | bytes 344072 | tf_op jit(solution)/shard_map/ppermute | solution.py:27
  93.1 5.2 %collective-permute-done.12 = bf16[2,16,1792]{2,1,0:T(8,128)(2,1)S(1)} collective-permute-done((bf16[2,16,1792]{2,1,0:T(8,128)(2,1)S(1)}, bf16[2,16,1792]{2,1,0:T(8,128)(2,1)S(1)}, u32[]{:S(2)}, u32[]{:S(2)}) %collective-permute-start.12) | collective-permute-done | bytes 114720 | tf_op jit(solution)/shard_map/ppermute | solution.py:27
  98.3 11.0 %collective-permute-start.13 = (f32[16,1792]{1,0:T(8,128)S(1)}, f32[16,1792]{1,0:T(8,128)S(1)}, u32[]{:S(2)}, u32[]{:S(2)}) collective-permute-start(f32[16,1792]{1,0:T(8,128)S(1)} %slice_bitcast_fusion), channel_id=1, source_target_pairs={{0,33},{1,480},{2,35},{3,482},{4,37},{5,484},{6,39},{7,486},{8,41}... | collective-permute-start | bytes 344072 | tf_op jit(solution)/shard_map/ppermute | solution.py:27
  109.2 2.5 %collective-permute-done.13 = f32[16,1792]{1,0:T(8,128)S(1)} collective-permute-done((f32[16,1792]{1,0:T(8,128)S(1)}, f32[16,1792]{1,0:T(8,128)S(1)}, u32[]{:S(2)}, u32[]{:S(2)}) %collective-permute-start.13) | collective-permute-done | bytes 114720 | tf_op jit(solution)/shard_map/ppermute | solution.py:27
  111.7 0.7 fusion.1
  (19 shorter events, 0.1 us)
Async XLA Ops:
  0.0 40.8 %copy-start = (bf16[4,4,9,64,64]{4,3,2,1,0:T(8,128)(2,1)S(1)}, bf16[4,4,9,64,64]{4,3,2,1,0:T(8,128)(2,1)}, u32[]{:S(2)}) copy-start(bf16[4,4,9,64,64]{4,3,2,1,0:T(8,128)(2,1)} %param.5) | copy-start | bytes 3538948
  1.3 1.4 %copy-start.1 = (bf16[4,4,6,64,64]{4,3,2,1,0:T(8,128)(2,1)S(1)}, bf16[4,4,6,64,64]{4,3,2,1,0:T(8,128)(2,1)}, u32[]{:S(2)}) copy-start(bf16[4,4,6,64,64]{4,3,2,1,0:T(8,128)(2,1)} %param.8) | copy-start | bytes 2359300
  2.7 37.9 %copy-start.4 = (s32[4,4]{1,0:T(4,128)S(1)}, s32[4,4]{1,0:T(4,128)}, u32[]{:S(2)}) copy-start(s32[4,4]{1,0:T(4,128)} %param.7) | copy-start | bytes 196
  6.2 1.2 %copy-start.2 = (bf16[1024,768]{1,0:T(8,128)(2,1)}, bf16[1024,768]{1,0:T(8,128)(2,1)S(1)}, u32[]{:S(2)}) copy-start(bf16[1024,768]{1,0:T(8,128)(2,1)S(1)} %get-tuple-element.19.po_ref) | copy-start | bytes 4718596
  7.3 25.3 %collective-permute-start = (bf16[256,768]{1,0:T(8,128)(2,1)}, bf16[256,768]{1,0:T(8,128)(2,1)S(1)}, u32[]{:S(2)}, u32[]{:S(2)}) collective-permute-start(bf16[256,768]{1,0:T(8,128)(2,1)} %get-tuple-element.24), channel_id=1, source_target_pairs={{0,31},{1,2},{2,1},{3,4},{4,3},{5,6},{6,5},{7,8},{8,7},{9,10},{10,... | collective-permute-start | bytes 1179656 | tf_op jit(solution)/shard_map/ppermute | solution.py:27
  11.9 20.8 %collective-permute-start.1 = (bf16[256,768]{1,0:T(8,128)(2,1)}, bf16[256,768]{1,0:T(8,128)(2,1)S(1)}, u32[]{:S(2)}, u32[]{:S(2)}) collective-permute-start(bf16[256,768]{1,0:T(8,128)(2,1)} %get-tuple-element.25), channel_id=1, source_target_pairs={{0,1},{1,0},{2,3},{3,2},{4,5},{5,4},{6,7},{7,6},{8,9},{9,8},{10,11... | collective-permute-start | bytes 1179656 | tf_op jit(solution)/shard_map/ppermute | solution.py:27
  18.0 28.3 %collective-permute-start.2 = (bf16[256,768]{1,0:T(8,128)(2,1)}, bf16[256,768]{1,0:T(8,128)(2,1)S(1)}, u32[]{:S(2)}, u32[]{:S(2)}) collective-permute-start(bf16[256,768]{1,0:T(8,128)(2,1)} %get-tuple-element.26), channel_id=1, source_target_pairs={{0,32},{1,33},{2,34},{3,35},{4,36},{5,37},{6,38},{7,39},{8,40},{9,... | collective-permute-start | bytes 1179656 | tf_op jit(solution)/shard_map/ppermute | solution.py:27
  20.8 25.5 %collective-permute-start.3 = (bf16[256,768]{1,0:T(8,128)(2,1)}, bf16[256,768]{1,0:T(8,128)(2,1)}, u32[]{:S(2)}, u32[]{:S(2)}) collective-permute-start(bf16[256,768]{1,0:T(8,128)(2,1)} %get-tuple-element.27), channel_id=1, source_target_pairs={{0,480},{1,481},{2,482},{3,483},{4,484},{5,485},{6,486},{7,487},{8... | collective-permute-start | bytes 1179656 | tf_op jit(solution)/shard_map/ppermute | solution.py:27
  33.4 13.0 %collective-permute-start.4 = (bf16[128,768]{1,0:T(8,128)(2,1)}, bf16[128,768]{1,0:T(8,128)(2,1)}, u32[]{:S(2)}, u32[]{:S(2)}) collective-permute-start(bf16[128,768]{1,0:T(8,128)(2,1)} %pad_maximum_fusion), channel_id=1, source_target_pairs={{0,32},{1,33},{2,34},{3,35},{4,36},{5,37},{6,38},{7,39},{8,40},{9,... | collective-permute-start | bytes 589832 | tf_op jit(solution)/shard_map/ppermute | solution.py:27
  36.0 10.4 %collective-permute-start.5 = (bf16[128,768]{1,0:T(8,128)(2,1)}, bf16[128,768]{1,0:T(8,128)(2,1)}, u32[]{:S(2)}, u32[]{:S(2)}) collective-permute-start(bf16[128,768]{1,0:T(8,128)(2,1)} %pad_maximum_fusion.1), channel_id=1, source_target_pairs={{0,480},{1,481},{2,482},{3,483},{4,484},{5,485},{6,486},{7,487},{8... | collective-permute-start | bytes 589832 | tf_op jit(solution)/shard_map/ppermute | solution.py:27
  40.8 1.4 %copy-start.3 = (bf16[1024,768]{1,0:T(8,128)(2,1)S(1)}, bf16[1024,768]{1,0:T(8,128)(2,1)}, u32[]{:S(2)}) copy-start(bf16[1024,768]{1,0:T(8,128)(2,1)} %copy-done.2) | copy-start | bytes 4718596
  50.4 14.9 %collective-permute-start.6 = (bf16[256,1280]{1,0:T(8,128)(2,1)S(1)}, bf16[256,1280]{1,0:T(8,128)(2,1)S(1)}, u32[]{:S(2)}, u32[]{:S(2)}) collective-permute-start(bf16[256,1280]{1,0:T(8,128)(2,1)S(1)} %get-tuple-element.30), channel_id=1, source_target_pairs={{0,1},{1,0},{2,3},{3,2},{4,5},{5,4},{6,7},{7,6},{8,9},{9,8},{10,11... | collective-permute-start | bytes 1966088 | tf_op jit(solution)/shard_map/ppermute | solution.py:27
  53.2 11.1 %collective-permute-start.7 = (bf16[128,1280]{1,0:T(8,128)(2,1)S(1)}, bf16[128,1280]{1,0:T(8,128)(2,1)S(1)}, u32[]{:S(2)}, u32[]{:S(2)}) collective-permute-start(bf16[128,1280]{1,0:T(8,128)(2,1)S(1)} %get-tuple-element.31), channel_id=1, source_target_pairs={{0,30},{1,3},{2,0},{3,5},{4,2},{5,7},{6,4},{7,9},{8,6},{9,11},{10,... | collective-permute-start | bytes 983048 | tf_op jit(solution)/shard_map/ppermute | solution.py:27
  55.1 10.2 %collective-permute-start.8 = (bf16[128,1280]{1,0:T(8,128)(2,1)S(1)}, bf16[128,1280]{1,0:T(8,128)(2,1)S(1)}, u32[]{:S(2)}, u32[]{:S(2)}) collective-permute-start(bf16[128,1280]{1,0:T(8,128)(2,1)S(1)} %get-tuple-element.32), channel_id=1, source_target_pairs={{0,31},{1,2},{2,1},{3,4},{4,3},{5,6},{6,5},{7,8},{8,7},{9,10},{10,... | collective-permute-start | bytes 983048 | tf_op jit(solution)/shard_map/ppermute | solution.py:27
  65.9 13.9 %collective-permute-start.9 = (bf16[2,32,1792]{2,1,0:T(8,128)(2,1)S(1)}, bf16[2,32,1792]{2,1,0:T(8,128)(2,1)S(1)}, u32[]{:S(2)}, u32[]{:S(2)}) collective-permute-start(bf16[2,32,1792]{2,1,0:T(8,128)(2,1)S(1)} %shard_map.56), channel_id=1, source_target_pairs={{0,32},{1,481},{2,34},{3,483},{4,36},{5,485},{6,38},{7,487},{8,40}... | collective-permute-start | bytes 688136 | tf_op jit(solution)/shard_map/ppermute | solution.py:27
  70.6 13.1 %collective-permute-start.10 = (bf16[2,32,1792]{2,1,0:T(8,128)(2,1)S(1)}, bf16[2,32,1792]{2,1,0:T(8,128)(2,1)S(1)}, u32[]{:S(2)}, u32[]{:S(2)}) collective-permute-start(bf16[2,32,1792]{2,1,0:T(8,128)(2,1)S(1)} %shard_map.57), channel_id=1, source_target_pairs={{0,64},{1,449},{2,66},{3,451},{4,68},{5,453},{6,70},{7,455},{8,72}... | collective-permute-start | bytes 688136 | tf_op jit(solution)/shard_map/ppermute | solution.py:27
  73.2 13.8 %collective-permute-start.11 = (bf16[2,32,1792]{2,1,0:T(8,128)(2,1)S(1)}, bf16[2,32,1792]{2,1,0:T(8,128)(2,1)S(1)}, u32[]{:S(2)}, u32[]{:S(2)}) collective-permute-start(bf16[2,32,1792]{2,1,0:T(8,128)(2,1)S(1)} %shard_map.58), channel_id=1, source_target_pairs={{0,96},{1,417},{2,98},{3,419},{4,100},{5,421},{6,102},{7,423},{8,1... | collective-permute-start | bytes 688136 | tf_op jit(solution)/shard_map/ppermute | solution.py:27
  87.1 11.1 %collective-permute-start.12 = (bf16[2,16,1792]{2,1,0:T(8,128)(2,1)S(1)}, bf16[2,16,1792]{2,1,0:T(8,128)(2,1)S(1)}, u32[]{:S(2)}, u32[]{:S(2)}) collective-permute-start(bf16[2,16,1792]{2,1,0:T(8,128)(2,1)S(1)} %slice.49), channel_id=1, source_target_pairs={{0,128},{1,385},{2,130},{3,387},{4,132},{5,389},{6,134},{7,391},{8... | collective-permute-start | bytes 344072 | tf_op jit(solution)/shard_map/ppermute | solution.py:27
  98.3 13.4 %collective-permute-start.13 = (f32[16,1792]{1,0:T(8,128)S(1)}, f32[16,1792]{1,0:T(8,128)S(1)}, u32[]{:S(2)}, u32[]{:S(2)}) collective-permute-start(f32[16,1792]{1,0:T(8,128)S(1)} %slice_bitcast_fusion), channel_id=1, source_target_pairs={{0,33},{1,480},{2,35},{3,482},{4,37},{5,484},{6,39},{7,486},{8,41}... | collective-permute-start | bytes 344072 | tf_op jit(solution)/shard_map/ppermute | solution.py:27

commit v3 on v2

--- a/solution.py
+++ b/solution.py
@@ -6,7 +6,6 @@
 from jax.sharding import PartitionSpec as P
 
 
-CB = 4
 B = 64
 ROWS = 16
 COLS = 32
@@ -31,33 +30,6 @@
     return 1 if s % 2 == 0 else -1
 
 
-def place_kernel(core_ref, inv_ref, p_ref, po_ref, cross_ref, chip_ref, up_ref, down_ref):
-    def block(b, carry):
-        y = b // 4
-        x = b % 4
-        row = pl.multiple_of(b * B, B)
-
-        def tile(r):
-            j = inv_ref[b * 12 + r]
-            value = p_ref[(x * 4 + y) * 6 + jnp.maximum(j - 1, 0)]
-            return jnp.where(j > 0, value, jnp.zeros_like(value))
-
-        for m in range(6):
-            pair = jnp.concatenate([tile(2 * m), tile(2 * m + 1)], axis=1)
-            po_ref[pl.ds(row, B), 128 * m : 128 * (m + 1)] = pair
-        return carry
-
-    lax.fori_loop(0, 16, block, 0)
-    core = core_ref[0]
-    cross_row = pl.multiple_of(core * 768, 256)
-    chip_row = pl.multiple_of(768 - core * 768, 256)
-    cross_ref[...] = po_ref[pl.ds(cross_row, 256), :]
-    chip_ref[...] = po_ref[pl.ds(chip_row, 256), :]
-    for y in range(4):
-        up_ref[64 * y : 64 * y + 64, :] = po_ref[256 * y + 192 : 256 * y + 256, :]
-        down_ref[64 * y : 64 * y + 64, :] = po_ref[256 * y : 256 * y + 64, :]
-
-
 def smem():
     return pl.BlockSpec(memory_space=pltpu.SMEM)
 
@@ -73,16 +45,82 @@
     )
 
 
-def place(core, inv, tiles):
-    edge = jax.ShapeDtypeStruct((256, 768), BF16)
-    return pl.pallas_call(
-        place_kernel,
-        out_shape=(jax.ShapeDtypeStruct((1024, 768), BF16), edge, edge, edge, edge),
-        in_specs=[smem(), smem(), vmem()],
-        out_specs=(vmem(),) * 5,
-        name="place",
-        **budget(6, 0, 6000000),
-    )(core, inv, tiles)
+def place_blocks(ys, pos_ref, blocks_ref, p_ref, po_refs, buf_ref, inv_ref, sems):
+    spots = [(n, y, x) for n, y in enumerate(ys) for x in range(4)]
+    copies = [
+        pltpu.make_async_copy(p_ref.at[x, y], buf_ref.at[i], sems.at[i])
+        for i, (_, y, x) in enumerate(spots)
+    ]
+    for copy in copies:
+        copy.start()
+    slab = pos_ref[2]
+    for i, (_, y, x) in enumerate(spots):
+        for column in range(12):
+            inv_ref[i * 12 + column] = 0
+        for j in range(6):
+            g = blocks_ref[x, y, j]
+            inv_ref[i * 12 + ((g // 4 - slab + 33) % 32) * 4 + g % 4] = j + 1
+    for i, (n, _, x) in enumerate(spots):
+        copies[i].wait()
+
+        def tile(column):
+            j = inv_ref[i * 12 + column]
+            value = buf_ref[i, jnp.maximum(j - 1, 0)]
+            return jnp.where(j > 0, value, jnp.zeros_like(value))
+
+        for m in range(6):
+            pair = jnp.concatenate([tile(2 * m), tile(2 * m + 1)], axis=1)
+            po_refs[n][64 * x : 64 * x + 64, 128 * m : 128 * m + 128] = pair
+
+
+def edge_kernel(pos_ref, blocks_ref, p_ref, low_ref, high_ref, cross_ref, chip_ref, *scratch):
+    place_blocks((0, 3), pos_ref, blocks_ref, p_ref, (low_ref, high_ref), *scratch)
+
+    @pl.when(pos_ref[0] == 0)
+    def _():
+        cross_ref[...] = low_ref[...]
+        chip_ref[...] = high_ref[...]
+
+    @pl.when(pos_ref[0] == 1)
+    def _():
+        cross_ref[...] = high_ref[...]
+        chip_ref[...] = low_ref[...]
+
+
+def middle_kernel(pos_ref, blocks_ref, p_ref, one_ref, two_ref, *scratch):
+    place_blocks((1, 2), pos_ref, blocks_ref, p_ref, (one_ref, two_ref), *scratch)
+
+
+def place(kernel, count, pos, blocks, tiles):
+    return pl.pallas_call(
+        kernel,
+        out_shape=(jax.ShapeDtypeStruct((256, 768), BF16),) * count,
+        in_specs=[smem(), smem(), pl.BlockSpec(memory_space=pltpu.HBM)],
+        out_specs=(vmem(),) * count,
+        scratch_shapes=[
+            pltpu.VMEM((8, 6, B, B), BF16),
+            pltpu.SMEM((96,), jnp.int32),
+            pltpu.SemaphoreType.DMA((8,)),
+        ],
+        **budget(6, 0, 2000000),
+    )(pos, blocks, tiles)
+
+
+def rim_kernel(p0, p1, p2, p3, cross_ref, chip_ref, up_ref, down_ref):
+    for n, ref in enumerate((p0, p1, p2, p3, cross_ref, chip_ref)):
+        up_ref[64 * n : 64 * n + 64, :] = ref[192:256, :]
+        down_ref[64 * n : 64 * n + 64, :] = ref[0:64, :]
+
+
+def rims(*parts):
+    return pl.pallas_call(
+        rim_kernel,
+        out_shape=(jax.ShapeDtypeStruct((384, 768), BF16),) * 2,
+        in_specs=[vmem()] * 6,
+        out_specs=(vmem(),) * 2,
+        name="rims",
+        **budget(4, 0, 2000000),
+    )(*parts)
 
 
 SLOTS = (
@@ -97,22 +135,31 @@
     return jnp.dot(a, b, preferred_element_type=F32)
 
 
-def local_kernel(pos_ref, aidx_ref, a_ref, po_ref, ad_ref, outer_ref, rest_ref, im_ref):
+def local_kernel(
+    pos_ref, codes_ref, live_ref, a_ref, p0, p1, p2, p3,
+    ad_ref, outer_ref, rest_ref, im_ref, po_ref, aidx_ref,
+):
     core = pos_ref[0]
     r = pos_ref[1]
 
+    for y, part in enumerate((p0, p1, p2, p3)):
+        po_ref[256 * y : 256 * y + 256, :] = part[...]
+
     def fill(b, carry):
         y = b // 4
+        at = b % 4
+        for k in range(9):
+            aidx_ref[codes_ref[at, y, k]] = jnp.where(k < live_ref[at, y], k, -1)
 
         def tile(x, c):
             if c is None:
                 return jnp.zeros((B, B), BF16)
-            k = aidx_ref[(y * 4 + x) * 9 + c]
+            k = aidx_ref[c]
             value = a_ref[(x * 4 + y) * 9 + jnp.maximum(k, 0)]
             return jnp.where(k >= 0, value, jnp.zeros_like(value))
 
         for x in range(4):
-            @pl.when(b % 4 == x)
+            @pl.when(at == x)
             def _():
                 for dy in range(3):
                     for m in range(3):
@@ -150,7 +197,7 @@
                 pt_ref[pl.ds(row, 16), 256 * y : 256 * y + 256] = flipped[16 * o : 16 * o + 16, :]
 
 
-def local_products(pos, aidx, a, po):
+def local_products(pos, codes, live, a, *parts):
     return pl.pallas_call(
         local_kernel,
         out_shape=(
@@ -159,11 +206,12 @@
             jax.ShapeDtypeStruct((512, 1024), BF16),
             jax.ShapeDtypeStruct((1024, 768), F32),
         ),
-        in_specs=[smem(), smem(), vmem(), vmem()],
+        in_specs=[smem(), smem(), smem()] + [vmem()] * 5,
         out_specs=(vmem(),) * 4,
+        scratch_shapes=[pltpu.VMEM((1024, 768), BF16), pltpu.SMEM((9,), jnp.int32)],
         name="local_products",
         **budget(12, 1000000000, 12000000),
-    )(pos, aidx, a, po)
+    )(pos, codes, live, a, *parts)
 
 
 def pieces(pt_ref, base, im_ref, store):
@@ -174,7 +222,7 @@
 
 
 def halo_kernel(
-    pos_ref, ad_ref, pt_ref, part_ref, cross_ref, chip_ref, up_ref, down_ref, upc_ref, downc_ref,
+    pos_ref, ad_ref, pt_ref, part_ref, cross_ref, chip_ref, up_ref, down_ref,
     im_ref, same_ref, other_ref, side_ref, hr_ref,
 ):
     core = pos_ref[0]
@@ -183,10 +231,10 @@
         hr_ref[y + 1, 64:128, :] = down_ref[64 * y : 64 * y + 64, :]
     side_ref[core] = cross_ref[...]
     side_ref[1 - core] = chip_ref[...]
-    hr_ref[core * 5, 0:64, :] = upc_ref[0:64, :]
-    hr_ref[core * 5, 64:128, :] = downc_ref[0:64, :]
-    hr_ref[5 - core * 5, 0:64, :] = upc_ref[64:128, :]
-    hr_ref[5 - core * 5, 64:128, :] = downc_ref[64:128, :]
+    hr_ref[core * 5, 0:64, :] = up_ref[256:320, :]
+    hr_ref[core * 5, 64:128, :] = down_ref[256:320, :]
+    hr_ref[5 - core * 5, 0:64, :] = up_ref[320:384, :]
+    hr_ref[5 - core * 5, 64:128, :] = down_ref[320:384, :]
 
     for y in range(4):
         rows = slice(256 * y, 256 * y + 256)
@@ -224,7 +272,7 @@
     return pl.pallas_call(
         halo_kernel,
         out_shape=(jax.ShapeDtypeStruct((1024, 1280), BF16), half, half),
-        in_specs=[smem()] + [vmem()] * 9,
+        in_specs=[smem()] + [vmem()] * 7,
         out_specs=(vmem(),) * 3,
         scratch_shapes=[pltpu.VMEM((2, 256, 768), BF16), pltpu.VMEM((6, 128, 768), BF16)],
         name="halo_products",
@@ -303,30 +351,21 @@
     r = lax.axis_index("row")
     s = lax.axis_index("col")
     core = s % 2
-    pos = jnp.stack([core, r]).astype(jnp.int32)
-
-    place_of = jnp.mod(coarse_blocks // CB - s + 1, COLS) * CB + coarse_blocks % CB
-    hit = place_of[..., None] == jnp.arange(12)
-    number = jnp.arange(1, 7, dtype=jnp.int32)[:, None]
-    inv = jnp.sum(jnp.where(hit, number, 0), axis=2).transpose(1, 0, 2).reshape(-1)
-    code_hit = neighbour_codes[..., None] == jnp.arange(9)
-    slot = jnp.sum(jnp.where(code_hit, jnp.arange(9, dtype=jnp.int32)[:, None], 0), axis=2)
-    slot = jnp.where(slot < live_slots[..., None], slot, -1)
-    aidx = slot.transpose(1, 0, 2).reshape(-1)
-
-    po, cross, chip, up, down = place(pos, inv, prolong_tiles.reshape(96, B, B))
+    pos = jnp.stack([core, r, s]).astype(jnp.int32)
+
+    low, high, cross, chip = place(edge_kernel, 4, pos, coarse_blocks, prolong_tiles)
     cross_in = send(cross, lambda r, s: (r, s - sign(s)))
     chip_in = send(chip, lambda r, s: (r, s + sign(s)))
+    one, two = place(middle_kernel, 2, pos, coarse_blocks, prolong_tiles)
+    parts = (low, one, two, high)
+    up, down = rims(*parts, cross_in, chip_in)
     up_in = send(up, lambda r, s: (r + 1, s))
     down_in = send(down, lambda r, s: (r - 1, s))
-    upc = jnp.concatenate([cross_in[192:256], chip_in[192:256]], axis=0)
-    downc = jnp.concatenate([cross_in[0:64], chip_in[0:64]], axis=0)
-    upc_in = send(upc, lambda r, s: (r + 1, s))
-    downc_in = send(downc, lambda r, s: (r - 1, s))
-
-    ad, outer, rest, part = local_products(pos, aidx, operator_tiles.reshape(144, B, B), po)
+    ad, outer, rest, part = local_products(
+        pos, neighbour_codes, live_slots, operator_tiles.reshape(144, B, B), *parts
+    )
     im, same, other = halo_products(
-        pos, ad, outer, part, cross_in, chip_in, up_in, down_in, upc_in, downc_in
+        pos, ad, outer, part, cross_in, chip_in, up_in, down_in
     )
     other_in = send(other, lambda r, s: (r, s - sign(s)))
     same_in = send(same, lambda r, s: (r, s - 2 * sign(s)))
@@ -354,4 +393,6 @@
         P("row", "col", None),
     )
     out_specs = P("col", "row", None)
-    return jax.shard_map(body, mesh=mesh, in_specs=in_specs, out_specs=out_specs, check_vma=False)
+    return jax.shard_map(
+        body, mesh=mesh, in_specs=in_specs, out_specs=out_specs, check_vma=False
+    )

time: 113 us -> 112 us (level)
  local copies, waits for them, and re-layouts: 5.77 us -> 2.15 us
  starting transfers between devices: 66.5 us -> 69.9 us
  other arithmetic: 4.16 us -> 0.85 us
  Pallas kernels: 14.1 us -> 16.9 us
    ppermute x14 -> x12, starting transfers between devices: 66.5 us -> 69.9 us  [send(): return lax.ppermute(value, ('row', 'col'), joint(rule))]
    unnamed x11 -> x10, local copies, waits for them, and re-layouts: 5.41 us -> 2.12 us
    pallas_call x1 -> x3, Pallas kernels: 3.44 us -> 6.19 us  [the longest x2 6.11 us: place(): pl.pallas_call(kernel, out_shape=(jax.ShapeDtypeStruct((256, 768), BF16),...]
    concatenate x2 -> x0, other arithmetic: 1.39 us -> none  [the longest x1 0.7 us: body(): downc = jnp.concatenate([cross_in[0:64], chip_in[0:64]], axis=0)]
    ppermute x14 -> x12, waiting for transfers between devices: 21.5 us -> 21.9 us  [send(): return lax.ppermute(value, ('row', 'col'), joint(rule))]
  transfers between devices with their start and end apart: 14 -> 12, of which waited for: 6 -> 7; matrix products, arithmetic and copies ran while one was open for 3% -> 0% of each run, Pallas kernels for 5% -> 9%
where the time goes in v3:
time: 112 us
  starting transfers between devices  69.9 us (62%)
  waiting for transfers between devices  21.9 us (20%)
  Pallas kernels  16.9 us (15%)
  local copies, waits for them, and re-layouts  2.15 us (2%)
    ppermute x12, starting transfers between devices, send(): return lax.ppermute(value, ('row', 'col'), joint(rule))  69.9 us
    ppermute x12, waiting for transfers between devices, send(): return lax.ppermute(value, ('row', 'col'), joint(rule))  21.9 us
    pallas_call x2, Pallas kernels, place(): pl.pallas_call(kernel, out_shape=(jax.ShapeDtypeStruct((256, 768), BF16),...  6.11 us
    pallas_call x1, Pallas kernels, local_products(): pl.pallas_call(local_kernel, out_shape=(jax.ShapeDtypeStruct((4, 256, 115...  4.73 us
    pallas_call x4, Pallas kernels, merged(): pl.pallas_call(merge_kernel, grid=(1,), out_shape=jax.ShapeDtypeStruct((2...  2.55 us
    pallas_call x1, Pallas kernels, halo_products(): pl.pallas_call(halo_kernel, out_shape=(jax.ShapeDtypeStruct((1024, 1280),...  2.32 us
  transfers between devices with their start and end apart: 12, of which 7 were waited for; matrix products, arithmetic and copies ran while one was open for 0% of the time, Pallas kernels for 9%

profile of v3, /device:TPU:1, one launch (start us, length us, event | category | flops | bytes accessed | tf_op | source)
XLA Modules:
  0.0 112.0 jit_solution(1410248916828211047)
XLA Ops:
  0.0 0.1 pad_add_fusion.pos_ref
  0.1 0.0 copy-start
  0.1 1.4 %copy-done = bf16[4,4,6,64,64]{4,3,2,1,0:T(8,128)(2,1)S(1)} copy-done((bf16[4,4,6,64,64]{4,3,2,1,0:T(8,128)(2,1)S(1)}, bf16[4,4,6,64,64]{4,3,2,1,0:T(8,128)(2,1)}, u32[]{:S(2)}) %copy-start) | copy-done | bytes 786456
  1.5 0.0 copy-start.2
  1.5 0.7 copy-done.2
  2.2 3.1 %shard_map.55 = (bf16[256,768]{1,0:T(8,128)(2,1)S(1)}, bf16[256,768]{1,0:T(8,128)(2,1)S(1)}, bf16[256,768]{1,0:T(8,128)(2,1)S(1)}, bf16[256,768]{1,0:T(8,128)(2,1)S(1)}) custom-call(s32[3]{0:T(128)S(1)} %pad_add_fusion.pos_ref, s32[4,4,6]{2,1,0:T(4,128)S(1)} %copy-done.2, bf16[4,4,6,64,64]{4,3,2,1,0:T(8,128)(2,1)S(1)} %copy-done), custom_call_target="tpu_custom_call" | custom-call | bytes 2000000 | tf_op jit(solution)/shard_map/pallas_call | solution.py:95
  5.3 0.0 copy-start.1
  5.3 0.0 copy-start.3
  5.3 0.0 copy-start.4
  5.3 4.7 %collective-permute-start = (bf16[256,768]{1,0:T(8,128)(2,1)S(1)}, bf16[256,768]{1,0:T(8,128)(2,1)S(1)}, u32[]{:S(2)}, u32[]{:S(2)}) collective-permute-start(bf16[256,768]{1,0:T(8,128)(2,1)S(1)} %get-tuple-element.30), channel_id=1, source_target_pairs={{0,31},{1,2},{2,1},{3,4},{4,3},{5,6},{6,5},{7,8},{8,7},{9,10},{10,... | collective-permute-start | bytes 1179656 | tf_op jit(solution)/shard_map/ppermute | solution.py:26
  10.0 6.1 %collective-permute-start.1 = (bf16[256,768]{1,0:T(8,128)(2,1)S(1)}, bf16[256,768]{1,0:T(8,128)(2,1)S(1)}, u32[]{:S(2)}, u32[]{:S(2)}) collective-permute-start(bf16[256,768]{1,0:T(8,128)(2,1)S(1)} %get-tuple-element.31), channel_id=1, source_target_pairs={{0,1},{1,0},{2,3},{3,2},{4,5},{5,4},{6,7},{7,6},{8,9},{9,8},{10,11... | collective-permute-start | bytes 1179656 | tf_op jit(solution)/shard_map/ppermute | solution.py:26
  16.1 3.0 %shard_map.56 = (bf16[256,768]{1,0:T(8,128)(2,1)S(1)}, bf16[256,768]{1,0:T(8,128)(2,1)S(1)}) custom-call(s32[3]{0:T(128)S(1)} %pad_add_fusion.pos_ref, s32[4,4,6]{2,1,0:T(4,128)S(1)} %copy-done.2, bf16[4,4,6,64,64]{4,3,2,1,0:T(8,128)(2,1)S(1)} %copy-done), custom_call_target="tpu_custom_call" | custom-call | bytes 2000000 | tf_op jit(solution)/shard_map/pallas_call | solution.py:95
  19.2 0.0 collective-permute-done.cross_ref
  19.2 0.0 collective-permute-done.1.chip_ref
  19.2 0.1 rims.1
  19.3 2.8 %collective-permute-start.2 = (bf16[384,768]{1,0:T(8,128)(2,1)S(1)}, bf16[384,768]{1,0:T(8,128)(2,1)S(1)}, u32[]{:S(2)}, u32[]{:S(2)}) collective-permute-start(bf16[384,768]{1,0:T(8,128)(2,1)S(1)} %get-tuple-element.32), channel_id=1, source_target_pairs={{0,32},{1,33},{2,34},{3,35},{4,36},{5,37},{6,38},{7,39},{8,40},{9,... | collective-permute-start | bytes 1769480 | tf_op jit(solution)/shard_map/ppermute | solution.py:26
  22.1 9.5 %collective-permute-start.3 = (bf16[384,768]{1,0:T(8,128)(2,1)S(1)}, bf16[384,768]{1,0:T(8,128)(2,1)S(1)}, u32[]{:S(2)}, u32[]{:S(2)}) collective-permute-start(bf16[384,768]{1,0:T(8,128)(2,1)S(1)} %get-tuple-element.33), channel_id=1, source_target_pairs={{0,480},{1,481},{2,482},{3,483},{4,484},{5,485},{6,486},{7,487},{8... | collective-permute-start | bytes 1769480 | tf_op jit(solution)/shard_map/ppermute | solution.py:26
  31.6 0.0 copy-done.1
  31.6 0.0 copy-done.3
  31.6 0.0 copy-done.4
  31.7 4.7 %local_products.1 = (bf16[4,256,1152]{2,1,0:T(8,128)(2,1)S(1)}, bf16[256,1024]{1,0:T(8,128)(2,1)S(1)}, bf16[512,1024]{1,0:T(8,128)(2,1)S(1)}, f32[1024,768]{1,0:T(8,128)S(1)}) custom-call(s32[3]{0:T(128)S(1)} %pad_add_fusion.pos_ref, s32[4,4,9]{2,1,0:T(4,128)S(1)} %copy-done.3, s32[4,4]{1,0:T(4,128)S(1)} %copy-done.4, bf16[144,64,64]{2,1,0:T(8,128)(2,1)S(1)} %bitcast.14, ...), custom_call_target="tpu_custom_call" | custom-call | flops 1000000000 | bytes 12000000 | tf_op jit(solution)/shard_map/local_products/pallas_call | solution.py:201
  36.4 6.1 %collective-permute-done.2.up_ref = bf16[384,768]{1,0:T(8,128)(2,1)S(1)} collective-permute-done((bf16[384,768]{1,0:T(8,128)(2,1)S(1)}, bf16[384,768]{1,0:T(8,128)(2,1)S(1)}, u32[]{:S(2)}, u32[]{:S(2)}) %collective-permute-start.2) | collective-permute-done | bytes 589856 | tf_op jit(solution)/shard_map/ppermute | solution.py:26
  42.5 0.9 collective-permute-done.3.down_ref
  43.4 2.3 %halo_products.1 = (bf16[1024,1280]{1,0:T(8,128)(2,1)S(1)}, bf16[128,1280]{1,0:T(8,128)(2,1)S(1)}, bf16[128,1280]{1,0:T(8,128)(2,1)S(1)}) custom-call(s32[3]{0:T(128)S(1)} %pad_add_fusion.pos_ref, bf16[4,256,1152]{2,1,0:T(8,128)(2,1)S(1)} %get-tuple-element.27.ad_ref, bf16[256,1024]{1,0:T(8,128)(2,1)S(1)} %get-tuple-element.28.pt_ref, ...), custom_call_target="tpu_custom_call" | custom-call | flops 1500000000 | bytes 12000000 | tf_op jit(solution)/shard_map/halo_products/pallas_call | solution.py:272
  45.7 1.1 own_pieces.1
  46.9 3.6 %collective-permute-start.4 = (bf16[256,1280]{1,0:T(8,128)(2,1)S(1)}, bf16[256,1280]{1,0:T(8,128)(2,1)S(1)}, u32[]{:S(2)}, u32[]{:S(2)}) collective-permute-start(bf16[256,1280]{1,0:T(8,128)(2,1)S(1)} %get-tuple-element.36), channel_id=1, source_target_pairs={{0,1},{1,0},{2,3},{3,2},{4,5},{5,4},{6,7},{7,6},{8,9},{9,8},{10,11... | collective-permute-start | bytes 1966088 | tf_op jit(solution)/shard_map/ppermute | solution.py:26
  50.5 1.9 %collective-permute-start.5 = (bf16[128,1280]{1,0:T(8,128)(2,1)S(1)}, bf16[128,1280]{1,0:T(8,128)(2,1)S(1)}, u32[]{:S(2)}, u32[]{:S(2)}) collective-permute-start(bf16[128,1280]{1,0:T(8,128)(2,1)S(1)} %get-tuple-element.37), channel_id=1, source_target_pairs={{0,30},{1,3},{2,0},{3,5},{4,2},{5,7},{6,4},{7,9},{8,6},{9,11},{10,... | collective-permute-start | bytes 983048 | tf_op jit(solution)/shard_map/ppermute | solution.py:26
  52.4 3.5 %collective-permute-start.6 = (bf16[128,1280]{1,0:T(8,128)(2,1)S(1)}, bf16[128,1280]{1,0:T(8,128)(2,1)S(1)}, u32[]{:S(2)}, u32[]{:S(2)}) collective-permute-start(bf16[128,1280]{1,0:T(8,128)(2,1)S(1)} %get-tuple-element.38), channel_id=1, source_target_pairs={{0,31},{1,2},{2,1},{3,4},{4,3},{5,6},{6,5},{7,8},{8,7},{9,10},{10,... | collective-permute-start | bytes 983048 | tf_op jit(solution)/shard_map/ppermute | solution.py:26
  56.0 5.7 %collective-permute-done.5.same_ref = bf16[128,1280]{1,0:T(8,128)(2,1)S(1)} collective-permute-done((bf16[128,1280]{1,0:T(8,128)(2,1)S(1)}, bf16[128,1280]{1,0:T(8,128)(2,1)S(1)}, u32[]{:S(2)}, u32[]{:S(2)}) %collective-permute-start.5) | collective-permute-done | bytes 327712 | tf_op jit(solution)/shard_map/ppermute | solution.py:26
  61.6 0.7 collective-permute-done.6.other_ref
  62.3 0.0 collective-permute-done.4.swap_own.swap_partner
  62.3 0.6 shard_map.58
  63.0 5.3 %collective-permute-start.7 = (bf16[2,32,1792]{2,1,0:T(8,128)(2,1)S(1)}, bf16[2,32,1792]{2,1,0:T(8,128)(2,1)S(1)}, u32[]{:S(2)}, u32[]{:S(2)}) collective-permute-start(bf16[2,32,1792]{2,1,0:T(8,128)(2,1)S(1)} %shard_map.58), channel_id=1, source_target_pairs={{0,32},{1,481},{2,34},{3,483},{4,36},{5,485},{6,38},{7,487},{8,40}... | collective-permute-start | bytes 688136 | tf_op jit(solution)/shard_map/ppermute | solution.py:26
  68.3 0.6 shard_map.59
  68.9 2.6 %collective-permute-start.8 = (bf16[2,32,1792]{2,1,0:T(8,128)(2,1)S(1)}, bf16[2,32,1792]{2,1,0:T(8,128)(2,1)S(1)}, u32[]{:S(2)}, u32[]{:S(2)}) collective-permute-start(bf16[2,32,1792]{2,1,0:T(8,128)(2,1)S(1)} %shard_map.59), channel_id=1, source_target_pairs={{0,64},{1,449},{2,66},{3,451},{4,68},{5,453},{6,70},{7,455},{8,72}... | collective-permute-start | bytes 688136 | tf_op jit(solution)/shard_map/ppermute | solution.py:26
  71.5 0.6 shard_map.60
  72.2 5.2 %collective-permute-start.9 = (bf16[2,32,1792]{2,1,0:T(8,128)(2,1)S(1)}, bf16[2,32,1792]{2,1,0:T(8,128)(2,1)S(1)}, u32[]{:S(2)}, u32[]{:S(2)}) collective-permute-start(bf16[2,32,1792]{2,1,0:T(8,128)(2,1)S(1)} %shard_map.60), channel_id=1, source_target_pairs={{0,96},{1,417},{2,98},{3,419},{4,100},{5,421},{6,102},{7,423},{8,1... | collective-permute-start | bytes 688136 | tf_op jit(solution)/shard_map/ppermute | solution.py:26
  77.4 0.6 shard_map.57
  78.1 0.0 collective-permute-done.7
  78.1 0.0 collective-permute-done.8
  78.1 4.3 %collective-permute-done.9 = bf16[2,32,1792]{2,1,0:T(8,128)(2,1)S(1)} collective-permute-done((bf16[2,32,1792]{2,1,0:T(8,128)(2,1)S(1)}, bf16[2,32,1792]{2,1,0:T(8,128)(2,1)S(1)}, u32[]{:S(2)}, u32[]{:S(2)}) %collective-permute-start.9) | collective-permute-done | bytes 229408 | tf_op jit(solution)/shard_map/ppermute | solution.py:26
  82.3 0.1 convert_add_fusion
  82.5 8.0 %collective-permute-start.10 = (bf16[2,16,1792]{2,1,0:T(8,128)(2,1)S(1)}, bf16[2,16,1792]{2,1,0:T(8,128)(2,1)S(1)}, u32[]{:S(2)}, u32[]{:S(2)}) collective-permute-start(bf16[2,16,1792]{2,1,0:T(8,128)(2,1)S(1)} %slice.29), channel_id=1, source_target_pairs={{0,128},{1,385},{2,130},{3,387},{4,132},{5,389},{6,134},{7,391},{8... | collective-permute-start | bytes 344072 | tf_op jit(solution)/shard_map/ppermute | solution.py:26
  90.5 1.8 %collective-permute-done.10 = bf16[2,16,1792]{2,1,0:T(8,128)(2,1)S(1)} collective-permute-done((bf16[2,16,1792]{2,1,0:T(8,128)(2,1)S(1)}, bf16[2,16,1792]{2,1,0:T(8,128)(2,1)S(1)}, u32[]{:S(2)}, u32[]{:S(2)}) %collective-permute-start.10) | collective-permute-done | bytes 114720 | tf_op jit(solution)/shard_map/ppermute | solution.py:26
  92.3 16.5 %collective-permute-start.11 = (f32[16,1792]{1,0:T(8,128)S(1)}, f32[16,1792]{1,0:T(8,128)S(1)}, u32[]{:S(2)}, u32[]{:S(2)}) collective-permute-start(f32[16,1792]{1,0:T(8,128)S(1)} %slice_bitcast_fusion), channel_id=1, source_target_pairs={{0,33},{1,480},{2,35},{3,482},{4,37},{5,484},{6,39},{7,486},{8,41}... | collective-permute-start | bytes 344072 | tf_op jit(solution)/shard_map/ppermute | solution.py:26
  108.8 2.5 %collective-permute-done.11 = f32[16,1792]{1,0:T(8,128)S(1)} collective-permute-done((f32[16,1792]{1,0:T(8,128)S(1)}, f32[16,1792]{1,0:T(8,128)S(1)}, u32[]{:S(2)}, u32[]{:S(2)}) %collective-permute-start.11) | collective-permute-done | bytes 114720 | tf_op jit(solution)/shard_map/ppermute | solution.py:26
  111.3 0.7 fusion.1
  (3 shorter events, 0.1 us)
Async XLA Ops:
  0.1 1.4 %copy-start = (bf16[4,4,6,64,64]{4,3,2,1,0:T(8,128)(2,1)S(1)}, bf16[4,4,6,64,64]{4,3,2,1,0:T(8,128)(2,1)}, u32[]{:S(2)}) copy-start(bf16[4,4,6,64,64]{4,3,2,1,0:T(8,128)(2,1)} %p_ref.3) | copy-start | bytes 2359300
  1.5 0.7 copy-start.2
  5.3 26.4 %copy-start.1 = (bf16[4,4,9,64,64]{4,3,2,1,0:T(8,128)(2,1)S(1)}, bf16[4,4,9,64,64]{4,3,2,1,0:T(8,128)(2,1)}, u32[]{:S(2)}) copy-start(bf16[4,4,9,64,64]{4,3,2,1,0:T(8,128)(2,1)} %param.5) | copy-start | bytes 3538948
  5.3 26.3 %copy-start.3 = (s32[4,4,9]{2,1,0:T(4,128)S(1)}, s32[4,4,9]{2,1,0:T(4,128)}, u32[]{:S(2)}) copy-start(s32[4,4,9]{2,1,0:T(4,128)} %codes_ref.1) | copy-start | bytes 1732
  5.3 26.3 %copy-start.4 = (s32[4,4]{1,0:T(4,128)S(1)}, s32[4,4]{1,0:T(4,128)}, u32[]{:S(2)}) copy-start(s32[4,4]{1,0:T(4,128)} %live_ref.1) | copy-start | bytes 196
  5.3 13.9 %collective-permute-start = (bf16[256,768]{1,0:T(8,128)(2,1)S(1)}, bf16[256,768]{1,0:T(8,128)(2,1)S(1)}, u32[]{:S(2)}, u32[]{:S(2)}) collective-permute-start(bf16[256,768]{1,0:T(8,128)(2,1)S(1)} %get-tuple-element.30), channel_id=1, source_target_pairs={{0,31},{1,2},{2,1},{3,4},{4,3},{5,6},{6,5},{7,8},{8,7},{9,10},{10,... | collective-permute-start | bytes 1179656 | tf_op jit(solution)/shard_map/ppermute | solution.py:26
  10.0 9.1 %collective-permute-start.1 = (bf16[256,768]{1,0:T(8,128)(2,1)S(1)}, bf16[256,768]{1,0:T(8,128)(2,1)S(1)}, u32[]{:S(2)}, u32[]{:S(2)}) collective-permute-start(bf16[256,768]{1,0:T(8,128)(2,1)S(1)} %get-tuple-element.31), channel_id=1, source_target_pairs={{0,1},{1,0},{2,3},{3,2},{4,5},{5,4},{6,7},{7,6},{8,9},{9,8},{10,11... | collective-permute-start | bytes 1179656 | tf_op jit(solution)/shard_map/ppermute | solution.py:26
  19.3 23.2 %collective-permute-start.2 = (bf16[384,768]{1,0:T(8,128)(2,1)S(1)}, bf16[384,768]{1,0:T(8,128)(2,1)S(1)}, u32[]{:S(2)}, u32[]{:S(2)}) collective-permute-start(bf16[384,768]{1,0:T(8,128)(2,1)S(1)} %get-tuple-element.32), channel_id=1, source_target_pairs={{0,32},{1,33},{2,34},{3,35},{4,36},{5,37},{6,38},{7,39},{8,40},{9,... | collective-permute-start | bytes 1769480 | tf_op jit(solution)/shard_map/ppermute | solution.py:26
  22.1 21.3 %collective-permute-start.3 = (bf16[384,768]{1,0:T(8,128)(2,1)S(1)}, bf16[384,768]{1,0:T(8,128)(2,1)S(1)}, u32[]{:S(2)}, u32[]{:S(2)}) collective-permute-start(bf16[384,768]{1,0:T(8,128)(2,1)S(1)} %get-tuple-element.33), channel_id=1, source_target_pairs={{0,480},{1,481},{2,482},{3,483},{4,484},{5,485},{6,486},{7,487},{8... | collective-permute-start | bytes 1769480 | tf_op jit(solution)/shard_map/ppermute | solution.py:26
  46.9 15.4 %collective-permute-start.4 = (bf16[256,1280]{1,0:T(8,128)(2,1)S(1)}, bf16[256,1280]{1,0:T(8,128)(2,1)S(1)}, u32[]{:S(2)}, u32[]{:S(2)}) collective-permute-start(bf16[256,1280]{1,0:T(8,128)(2,1)S(1)} %get-tuple-element.36), channel_id=1, source_target_pairs={{0,1},{1,0},{2,3},{3,2},{4,5},{5,4},{6,7},{7,6},{8,9},{9,8},{10,11... | collective-permute-start | bytes 1966088 | tf_op jit(solution)/shard_map/ppermute | solution.py:26
  50.5 11.1 %collective-permute-start.5 = (bf16[128,1280]{1,0:T(8,128)(2,1)S(1)}, bf16[128,1280]{1,0:T(8,128)(2,1)S(1)}, u32[]{:S(2)}, u32[]{:S(2)}) collective-permute-start(bf16[128,1280]{1,0:T(8,128)(2,1)S(1)} %get-tuple-element.37), channel_id=1, source_target_pairs={{0,30},{1,3},{2,0},{3,5},{4,2},{5,7},{6,4},{7,9},{8,6},{9,11},{10,... | collective-permute-start | bytes 983048 | tf_op jit(solution)/shard_map/ppermute | solution.py:26
  52.4 9.9 %collective-permute-start.6 = (bf16[128,1280]{1,0:T(8,128)(2,1)S(1)}, bf16[128,1280]{1,0:T(8,128)(2,1)S(1)}, u32[]{:S(2)}, u32[]{:S(2)}) collective-permute-start(bf16[128,1280]{1,0:T(8,128)(2,1)S(1)} %get-tuple-element.38), channel_id=1, source_target_pairs={{0,31},{1,2},{2,1},{3,4},{4,3},{5,6},{6,5},{7,8},{8,7},{9,10},{10,... | collective-permute-start | bytes 983048 | tf_op jit(solution)/shard_map/ppermute | solution.py:26
  63.0 15.1 %collective-permute-start.7 = (bf16[2,32,1792]{2,1,0:T(8,128)(2,1)S(1)}, bf16[2,32,1792]{2,1,0:T(8,128)(2,1)S(1)}, u32[]{:S(2)}, u32[]{:S(2)}) collective-permute-start(bf16[2,32,1792]{2,1,0:T(8,128)(2,1)S(1)} %shard_map.58), channel_id=1, source_target_pairs={{0,32},{1,481},{2,34},{3,483},{4,36},{5,485},{6,38},{7,487},{8,40}... | collective-permute-start | bytes 688136 | tf_op jit(solution)/shard_map/ppermute | solution.py:26
  68.9 9.1 %collective-permute-start.8 = (bf16[2,32,1792]{2,1,0:T(8,128)(2,1)S(1)}, bf16[2,32,1792]{2,1,0:T(8,128)(2,1)S(1)}, u32[]{:S(2)}, u32[]{:S(2)}) collective-permute-start(bf16[2,32,1792]{2,1,0:T(8,128)(2,1)S(1)} %shard_map.59), channel_id=1, source_target_pairs={{0,64},{1,449},{2,66},{3,451},{4,68},{5,453},{6,70},{7,455},{8,72}... | collective-permute-start | bytes 688136 | tf_op jit(solution)/shard_map/ppermute | solution.py:26
  72.2 10.2 %collective-permute-start.9 = (bf16[2,32,1792]{2,1,0:T(8,128)(2,1)S(1)}, bf16[2,32,1792]{2,1,0:T(8,128)(2,1)S(1)}, u32[]{:S(2)}, u32[]{:S(2)}) collective-permute-start(bf16[2,32,1792]{2,1,0:T(8,128)(2,1)S(1)} %shard_map.60), channel_id=1, source_target_pairs={{0,96},{1,417},{2,98},{3,419},{4,100},{5,421},{6,102},{7,423},{8,1... | collective-permute-start | bytes 688136 | tf_op jit(solution)/shard_map/ppermute | solution.py:26
  82.5 9.8 %collective-permute-start.10 = (bf16[2,16,1792]{2,1,0:T(8,128)(2,1)S(1)}, bf16[2,16,1792]{2,1,0:T(8,128)(2,1)S(1)}, u32[]{:S(2)}, u32[]{:S(2)}) collective-permute-start(bf16[2,16,1792]{2,1,0:T(8,128)(2,1)S(1)} %slice.29), channel_id=1, source_target_pairs={{0,128},{1,385},{2,130},{3,387},{4,132},{5,389},{6,134},{7,391},{8... | collective-permute-start | bytes 344072 | tf_op jit(solution)/shard_map/ppermute | solution.py:26
  92.3 19.0 %collective-permute-start.11 = (f32[16,1792]{1,0:T(8,128)S(1)}, f32[16,1792]{1,0:T(8,128)S(1)}, u32[]{:S(2)}, u32[]{:S(2)}) collective-permute-start(f32[16,1792]{1,0:T(8,128)S(1)} %slice_bitcast_fusion), channel_id=1, source_target_pairs={{0,33},{1,480},{2,35},{3,482},{4,37},{5,484},{6,39},{7,486},{8,41}... | collective-permute-start | bytes 344072 | tf_op jit(solution)/shard_map/ppermute | solution.py:26

commit v4 on v3

--- a/solution.py
+++ b/solution.py
@@ -45,78 +45,126 @@
     )
 
 
-def place_blocks(ys, pos_ref, blocks_ref, p_ref, po_refs, buf_ref, inv_ref, sems):
-    spots = [(n, y, x) for n, y in enumerate(ys) for x in range(4)]
-    copies = [
-        pltpu.make_async_copy(p_ref.at[x, y], buf_ref.at[i], sems.at[i])
-        for i, (_, y, x) in enumerate(spots)
-    ]
-    for copy in copies:
-        copy.start()
-    slab = pos_ref[2]
-    for i, (_, y, x) in enumerate(spots):
+PART4 = 4 * 192 + 4 * 16
+PART6 = 6 * 192 + 6 * 16
+
+
+def column_of(pos_ref, blocks_ref, x, y, j):
+    g = blocks_ref[x, y, j]
+    return ((g // 4 - pos_ref[2] + 33) % 32) * 4 + g % 4
+
+
+def pack(pos_ref, blocks_ref, p_ref, out_ref, n, x, y):
+    for t in range(3):
+        left = p_ref[(x * 4 + y) * 6 + 2 * t]
+        right = p_ref[(x * 4 + y) * 6 + 2 * t + 1]
+        at = 192 * n + 64 * t
+        out_ref[at : at + 64, :] = jnp.concatenate([left, right], axis=1)
+    row = lax.broadcasted_iota(jnp.int32, (16, 128), 0)
+    table = jnp.zeros((16, 128), jnp.int32)
+    for j in range(6):
+        table = jnp.where(row == j, column_of(pos_ref, blocks_ref, x, y, j), table)
+    out_ref[768 + 16 * n : 784 + 16 * n, :] = table.astype(F32).astype(BF16)
+
+
+def expand(message_ref, n, tables_at, store):
+    tables = message_ref[pl.ds(pl.multiple_of(tables_at + 16 * n, 16), 16), :]
+    tiles = []
+    for t in range(3):
+        pair = message_ref[pl.ds(pl.multiple_of(192 * n + 64 * t, 64), 64), :]
+        left, right = pair[:, 0:64], pair[:, 64:128]
+        tiles.append(jnp.concatenate([left, left], axis=1))
+        tiles.append(jnp.concatenate([right, right], axis=1))
+    spots = [jnp.broadcast_to(tables[j : j + 1, :], (64, 128)) for j in range(6)]
+    odd = (lax.broadcasted_iota(jnp.int32, (64, 128), 1) // 64).astype(F32)
+    for m in range(6):
+        column = (odd + 2.0 * m).astype(BF16)
+        out = jnp.zeros((64, 128), BF16)
+        for j in range(6):
+            out = jnp.where(spots[j] == column, tiles[j], out)
+        store(slice(128 * m, 128 * m + 128), out)
+
+
+def pack_kernel(pos_ref, blocks_ref, p_ref, cross_ref, chip_ref):
+    core = pos_ref[0]
+    for x in range(4):
+        pack(pos_ref, blocks_ref, p_ref, cross_ref, x, x, core * 3)
+        pack(pos_ref, blocks_ref, p_ref, chip_ref, x, x, 3 - core * 3)
+
+
+def packed(pos, blocks, tiles):
+    return pl.pallas_call(
+        pack_kernel,
+        out_shape=(jax.ShapeDtypeStruct((PART4, 128), BF16),) * 2,
+        in_specs=[smem(), smem(), vmem()],
+        out_specs=(vmem(),) * 2,
+        name="packed",
+        **budget(4, 0, 2000000),
+    )(pos, blocks, tiles)
+
+
+def place_kernel(pos_ref, blocks_ref, p_ref, po_ref, up_ref, down_ref, inv_ref):
+    for y in range(4):
+        pack(pos_ref, blocks_ref, p_ref, up_ref, y, 3, y)
+        pack(pos_ref, blocks_ref, p_ref, down_ref, y, 0, y)
+
+    def prepare(b, carry):
+        y, x = b // 4, b % 4
         for column in range(12):
-            inv_ref[i * 12 + column] = 0
+            inv_ref[b * 12 + column] = 0
         for j in range(6):
-            g = blocks_ref[x, y, j]
-            inv_ref[i * 12 + ((g // 4 - slab + 33) % 32) * 4 + g % 4] = j + 1
-    for i, (n, _, x) in enumerate(spots):
-        copies[i].wait()
+            inv_ref[b * 12 + column_of(pos_ref, blocks_ref, x, y, j)] = j + 1
+        return carry
+
+    lax.fori_loop(0, 16, prepare, 0)
+
+    def block(b, carry):
+        y, x = b // 4, b % 4
+        row = pl.multiple_of(b * B, B)
 
         def tile(column):
-            j = inv_ref[i * 12 + column]
-            value = buf_ref[i, jnp.maximum(j - 1, 0)]
+            j = inv_ref[b * 12 + column]
+            value = p_ref[(x * 4 + y) * 6 + jnp.maximum(j - 1, 0)]
             return jnp.where(j > 0, value, jnp.zeros_like(value))
 
         for m in range(6):
             pair = jnp.concatenate([tile(2 * m), tile(2 * m + 1)], axis=1)
-            po_refs[n][64 * x : 64 * x + 64, 128 * m : 128 * m + 128] = pair
-
-
-def edge_kernel(pos_ref, blocks_ref, p_ref, low_ref, high_ref, cross_ref, chip_ref, *scratch):
-    place_blocks((0, 3), pos_ref, blocks_ref, p_ref, (low_ref, high_ref), *scratch)
-
-    @pl.when(pos_ref[0] == 0)
-    def _():
-        cross_ref[...] = low_ref[...]
-        chip_ref[...] = high_ref[...]
-
-    @pl.when(pos_ref[0] == 1)
-    def _():
-        cross_ref[...] = high_ref[...]
-        chip_ref[...] = low_ref[...]
-
-
-def middle_kernel(pos_ref, blocks_ref, p_ref, one_ref, two_ref, *scratch):
-    place_blocks((1, 2), pos_ref, blocks_ref, p_ref, (one_ref, two_ref), *scratch)
-
-
-def place(kernel, count, pos, blocks, tiles):
-    return pl.pallas_call(
-        kernel,
-        out_shape=(jax.ShapeDtypeStruct((256, 768), BF16),) * count,
-        in_specs=[smem(), smem(), pl.BlockSpec(memory_space=pltpu.HBM)],
-        out_specs=(vmem(),) * count,
-        scratch_shapes=[
-            pltpu.VMEM((8, 6, B, B), BF16),
-            pltpu.SMEM((96,), jnp.int32),
-            pltpu.SemaphoreType.DMA((8,)),
-        ],
-        **budget(6, 0, 2000000),
+            po_ref[pl.ds(row, B), 128 * m : 128 * m + 128] = pair
+        return carry
+
+    lax.fori_loop(0, 16, block, 0)
+
+
+def place(pos, blocks, tiles):
+    return pl.pallas_call(
+        place_kernel,
+        out_shape=(
+            jax.ShapeDtypeStruct((1024, 768), BF16),
+            jax.ShapeDtypeStruct((PART4, 128), BF16),
+            jax.ShapeDtypeStruct((PART4, 128), BF16),
+        ),
+        in_specs=[smem(), smem(), vmem()],
+        out_specs=(vmem(),) * 3,
+        scratch_shapes=[pltpu.SMEM((192,), jnp.int32)],
+        name="place",
+        **budget(4, 0, 2000000),
     )(pos, blocks, tiles)
 
 
-def rim_kernel(p0, p1, p2, p3, cross_ref, chip_ref, up_ref, down_ref):
-    for n, ref in enumerate((p0, p1, p2, p3, cross_ref, chip_ref)):
-        up_ref[64 * n : 64 * n + 64, :] = ref[192:256, :]
-        down_ref[64 * n : 64 * n + 64, :] = ref[0:64, :]
+def rim_kernel(up_own, down_own, cross_ref, chip_ref, up_ref, down_ref):
+    for own, out, x in ((up_own, up_ref, 3), (down_own, down_ref, 0)):
+        out[0:768, :] = own[0:768, :]
+        out[1152:1216, :] = own[768:832, :]
+        for n, ref in ((4, cross_ref), (5, chip_ref)):
+            out[192 * n : 192 * n + 192, :] = ref[192 * x : 192 * x + 192, :]
+            out[1152 + 16 * n : 1168 + 16 * n, :] = ref[768 + 16 * x : 784 + 16 * x, :]
 
 
 def rims(*parts):
     return pl.pallas_call(
         rim_kernel,
-        out_shape=(jax.ShapeDtypeStruct((384, 768), BF16),) * 2,
-        in_specs=[vmem()] * 6,
+        out_shape=(jax.ShapeDtypeStruct((PART6, 128), BF16),) * 2,
+        in_specs=[vmem()] * 4,
         out_specs=(vmem(),) * 2,
         name="rims",
         **budget(4, 0, 2000000),
@@ -136,14 +184,22 @@
 
 
 def local_kernel(
-    pos_ref, codes_ref, live_ref, a_ref, p0, p1, p2, p3,
-    ad_ref, outer_ref, rest_ref, im_ref, po_ref, aidx_ref,
+    pos_ref, codes_ref, live_ref, a_ref, po_ref, cross_ref, chip_ref,
+    ad_ref, outer_ref, rest_ref, im_ref, side_ref, aidx_ref,
 ):
     core = pos_ref[0]
     r = pos_ref[1]
 
-    for y, part in enumerate((p0, p1, p2, p3)):
-        po_ref[256 * y : 256 * y + 256, :] = part[...]
+    def widen(x, carry):
+        rows = pl.ds(pl.multiple_of(64 * x, 64), 64)
+        for side, ref in ((core, cross_ref), (1 - core, chip_ref)):
+            def store(cols, value):
+                side_ref[side, rows, cols] = value
+
+            expand(ref, x, 768, store)
+        return carry
+
+    lax.fori_loop(0, 4, widen, 0)
 
     def fill(b, carry):
         y = b // 4
@@ -197,7 +253,7 @@
                 pt_ref[pl.ds(row, 16), 256 * y : 256 * y + 256] = flipped[16 * o : 16 * o + 16, :]
 
 
-def local_products(pos, codes, live, a, *parts):
+def local_products(pos, codes, live, a, po, cross, chip):
     return pl.pallas_call(
         local_kernel,
         out_shape=(
@@ -205,13 +261,14 @@
             jax.ShapeDtypeStruct((256, 1024), BF16),
             jax.ShapeDtypeStruct((512, 1024), BF16),
             jax.ShapeDtypeStruct((1024, 768), F32),
+            jax.ShapeDtypeStruct((2, 256, 768), BF16),
         ),
-        in_specs=[smem(), smem(), smem()] + [vmem()] * 5,
-        out_specs=(vmem(),) * 4,
-        scratch_shapes=[pltpu.VMEM((1024, 768), BF16), pltpu.SMEM((9,), jnp.int32)],
+        in_specs=[smem(), smem(), smem()] + [vmem()] * 4,
+        out_specs=(vmem(),) * 5,
+        scratch_shapes=[pltpu.SMEM((9,), jnp.int32)],
         name="local_products",
         **budget(12, 1000000000, 12000000),
-    )(pos, codes, live, a, *parts)
+    )(pos, codes, live, a, po, cross, chip)
 
 
 def pieces(pt_ref, base, im_ref, store):
@@ -222,19 +279,21 @@
 
 
 def halo_kernel(
-    pos_ref, ad_ref, pt_ref, part_ref, cross_ref, chip_ref, up_ref, down_ref,
-    im_ref, same_ref, other_ref, side_ref, hr_ref,
+    pos_ref, ad_ref, pt_ref, part_ref, side_ref, up_ref, down_ref,
+    im_ref, same_ref, other_ref, hr_ref,
 ):
     core = pos_ref[0]
-    for y in range(4):
-        hr_ref[y + 1, 0:64, :] = up_ref[64 * y : 64 * y + 64, :]
-        hr_ref[y + 1, 64:128, :] = down_ref[64 * y : 64 * y + 64, :]
-    side_ref[core] = cross_ref[...]
-    side_ref[1 - core] = chip_ref[...]
-    hr_ref[core * 5, 0:64, :] = up_ref[256:320, :]
-    hr_ref[core * 5, 64:128, :] = down_ref[256:320, :]
-    hr_ref[5 - core * 5, 0:64, :] = up_ref[320:384, :]
-    hr_ref[5 - core * 5, 64:128, :] = down_ref[320:384, :]
+
+    def widen(n, carry):
+        to = jnp.where(n < 4, n + 1, jnp.where(n == 4, core * 5, 5 - core * 5))
+        for at, ref in ((0, up_ref), (64, down_ref)):
+            def store(cols, value):
+                hr_ref[to, at : at + 64, cols] = value
+
+            expand(ref, n, 1152, store)
+        return carry
+
+    lax.fori_loop(0, 6, widen, 0)
 
     for y in range(4):
         rows = slice(256 * y, 256 * y + 256)
@@ -272,9 +331,9 @@
     return pl.pallas_call(
         halo_kernel,
         out_shape=(jax.ShapeDtypeStruct((1024, 1280), BF16), half, half),
-        in_specs=[smem()] + [vmem()] * 7,
+        in_specs=[smem()] + [vmem()] * 6,
         out_specs=(vmem(),) * 3,
-        scratch_shapes=[pltpu.VMEM((2, 256, 768), BF16), pltpu.VMEM((6, 128, 768), BF16)],
+        scratch_shapes=[pltpu.VMEM((6, 128, 768), BF16)],
         name="halo_products",
         **budget(12, 1500000000, 12000000),
     )(pos, ad, pt, part, *halo)
@@ -353,20 +412,18 @@
     core = s % 2
     pos = jnp.stack([core, r, s]).astype(jnp.int32)
 
-    low, high, cross, chip = place(edge_kernel, 4, pos, coarse_blocks, prolong_tiles)
+    tiles = prolong_tiles.reshape(96, B, B)
+    cross, chip = packed(pos, coarse_blocks, tiles)
     cross_in = send(cross, lambda r, s: (r, s - sign(s)))
     chip_in = send(chip, lambda r, s: (r, s + sign(s)))
-    one, two = place(middle_kernel, 2, pos, coarse_blocks, prolong_tiles)
-    parts = (low, one, two, high)
-    up, down = rims(*parts, cross_in, chip_in)
+    po, up_own, down_own = place(pos, coarse_blocks, tiles)
+    up, down = rims(up_own, down_own, cross_in, chip_in)
     up_in = send(up, lambda r, s: (r + 1, s))
     down_in = send(down, lambda r, s: (r - 1, s))
-    ad, outer, rest, part = local_products(
-        pos, neighbour_codes, live_slots, operator_tiles.reshape(144, B, B), *parts
+    ad, outer, rest, part, side = local_products(
+        pos, neighbour_codes, live_slots, operator_tiles.reshape(144, B, B), po, cross_in, chip_in
     )
-    im, same, other = halo_products(
-        pos, ad, outer, part, cross_in, chip_in, up_in, down_in
-    )
+    im, same, other = halo_products(pos, ad, outer, part, side, up_in, down_in)
     other_in = send(other, lambda r, s: (r, s - sign(s)))
     same_in = send(same, lambda r, s: (r, s - 2 * sign(s)))
     keep, swap = own_pieces(rest, im)

time: 112 us -> 102 us (0.911); the launches traced: 112 us -> 101 us
  starting transfers between devices: 69.9 us -> 63.6 us
  waiting for transfers between devices: 21.9 us -> 16.6 us
    ppermute x12, starting transfers between devices: 69.9 us -> 63.6 us  [send(): return lax.ppermute(value, ('row', 'col'), joint(rule))]
    ppermute x12, waiting for transfers between devices: 21.9 us -> 16.6 us  [send(): return lax.ppermute(value, ('row', 'col'), joint(rule))]
  transfers between devices with their start and end apart: 12 -> 12, of which waited for: 7 -> 7; matrix products, arithmetic and copies ran while one was open for 0% -> 0% of each run, Pallas kernels for 9% -> 11%
where the time goes in v4:
time: 102 us; the launch traced here: 101 us
  starting transfers between devices  63.6 us (62%)
  Pallas kernels  17.4 us (17%)
  waiting for transfers between devices  16.6 us (16%)
  local copies, waits for them, and re-layouts  2.14 us (2%)
    ppermute x12, starting transfers between devices, send(): return lax.ppermute(value, ('row', 'col'), joint(rule))  63.6 us
    ppermute x12, waiting for transfers between devices, send(): return lax.ppermute(value, ('row', 'col'), joint(rule))  16.6 us
    pallas_call x1, Pallas kernels, local_products(): pl.pallas_call(local_kernel, out_shape=(jax.ShapeDtypeStruct((4, 256, 115...  5.19 us
    pallas_call x1, Pallas kernels, place(): pl.pallas_call(place_kernel, out_shape=(jax.ShapeDtypeStruct((1024, 768),...  4.09 us
    pallas_call x1, Pallas kernels, halo_products(): pl.pallas_call(halo_kernel, out_shape=(jax.ShapeDtypeStruct((1024, 1280),...  3.14 us
    pallas_call x4, Pallas kernels, merged(): pl.pallas_call(merge_kernel, grid=(1,), out_shape=jax.ShapeDtypeStruct((2...  2.55 us
    unnamed x10, local copies, waits for them, and re-layouts  2.12 us
  transfers between devices with their start and end apart: 12, of which 7 were waited for; matrix products, arithmetic and copies ran while one was open for 0% of the time, Pallas kernels for 11%

profile of v4, /device:TPU:1, one launch (start us, length us, event | category | flops | bytes accessed | tf_op | source)
XLA Modules:
  0.0 100.7 jit_solution(13256220835991835594)
XLA Ops:
  0.0 0.0 copy-start.4
  0.0 0.0 copy-start.3
  0.0 0.1 pad_add_fusion.pos_ref
  0.1 0.0 copy-start
  0.1 1.4 %copy-done = bf16[4,4,6,64,64]{4,3,2,1,0:T(8,128)(2,1)S(1)} copy-done((bf16[4,4,6,64,64]{4,3,2,1,0:T(8,128)(2,1)S(1)}, bf16[4,4,6,64,64]{4,3,2,1,0:T(8,128)(2,1)}, u32[]{:S(2)}) %copy-start) | copy-done | bytes 786456
  1.5 0.0 copy-start.2
  1.5 0.7 copy-done.2
  2.2 0.0 copy-start.1
  2.2 1.2 %packed.1 = (bf16[832,128]{1,0:T(8,128)(2,1)S(1)}, bf16[832,128]{1,0:T(8,128)(2,1)S(1)}) custom-call(s32[3]{0:T(128)S(1)} %pad_add_fusion.pos_ref, s32[4,4,6]{2,1,0:T(4,128)S(1)} %copy-done.2, bf16[96,64,64]{2,1,0:T(8,128)(2,1)S(1)} %bitcast.15), custom_call_target="tpu_custom_call" | custom-call | bytes 2000000 | tf_op jit(solution)/shard_map/packed/pallas_call | solution.py:96
  3.4 4.6 %collective-permute-start = (bf16[832,128]{1,0:T(8,128)(2,1)S(1)}, bf16[832,128]{1,0:T(8,128)(2,1)S(1)}, u32[]{:S(2)}, u32[]{:S(2)}) collective-permute-start(bf16[832,128]{1,0:T(8,128)(2,1)S(1)} %get-tuple-element.23), channel_id=1, source_target_pairs={{0,31},{1,2},{2,1},{3,4},{4,3},{5,6},{6,5},{7,8},{8,7},{9,10},{10,... | collective-permute-start | bytes 638984 | tf_op jit(solution)/shard_map/ppermute | solution.py:26
  8.0 6.1 %collective-permute-start.1 = (bf16[832,128]{1,0:T(8,128)(2,1)S(1)}, bf16[832,128]{1,0:T(8,128)(2,1)S(1)}, u32[]{:S(2)}, u32[]{:S(2)}) collective-permute-start(bf16[832,128]{1,0:T(8,128)(2,1)S(1)} %get-tuple-element.24), channel_id=1, source_target_pairs={{0,1},{1,0},{2,3},{3,2},{4,5},{5,4},{6,7},{7,6},{8,9},{9,8},{10,11... | collective-permute-start | bytes 638984 | tf_op jit(solution)/shard_map/ppermute | solution.py:26
  14.1 4.1 %place.1 = (bf16[1024,768]{1,0:T(8,128)(2,1)S(1)}, bf16[832,128]{1,0:T(8,128)(2,1)S(1)}, bf16[832,128]{1,0:T(8,128)(2,1)S(1)}) custom-call(s32[3]{0:T(128)S(1)} %pad_add_fusion.pos_ref, s32[4,4,6]{2,1,0:T(4,128)S(1)} %copy-done.2, bf16[96,64,64]{2,1,0:T(8,128)(2,1)S(1)} %bitcast.16), custom_call_target="tpu_custom_call" | custom-call | bytes 2000000 | tf_op jit(solution)/shard_map/place/pallas_call | solution.py:139
  18.2 0.0 collective-permute-done.cross_ref
  18.2 0.0 collective-permute-done.1.chip_ref
  18.3 2.8 %collective-permute-start.2 = (bf16[1248,128]{1,0:T(8,128)(2,1)S(1)}, bf16[1248,128]{1,0:T(8,128)(2,1)S(1)}, u32[]{:S(2)}, u32[]{:S(2)}) collective-permute-start(bf16[1248,128]{1,0:T(8,128)(2,1)S(1)} %get-tuple-element.32), channel_id=1, source_target_pairs={{0,32},{1,33},{2,34},{3,35},{4,36},{5,37},{6,38},{7,39},{8,40},{9,... | collective-permute-start | bytes 958472 | tf_op jit(solution)/shard_map/ppermute | solution.py:26
  21.1 9.5 %collective-permute-start.3 = (bf16[1248,128]{1,0:T(8,128)(2,1)S(1)}, bf16[1248,128]{1,0:T(8,128)(2,1)S(1)}, u32[]{:S(2)}, u32[]{:S(2)}) collective-permute-start(bf16[1248,128]{1,0:T(8,128)(2,1)S(1)} %get-tuple-element.33), channel_id=1, source_target_pairs={{0,480},{1,481},{2,482},{3,483},{4,484},{5,485},{6,486},{7,487},{8... | collective-permute-start | bytes 958472 | tf_op jit(solution)/shard_map/ppermute | solution.py:26
  30.6 0.0 copy-done.4
  30.6 0.0 copy-done.3
  30.7 0.0 copy-done.1
  30.7 5.2 %local_products.1 = (bf16[4,256,1152]{2,1,0:T(8,128)(2,1)S(1)}, bf16[256,1024]{1,0:T(8,128)(2,1)S(1)}, bf16[512,1024]{1,0:T(8,128)(2,1)S(1)}, f32[1024,768]{1,0:T(8,128)S(1)}, bf16[2,256,768]{2,1,0:T(8,128)(2,1)S(1)}) custom-call(s32[3]{0:T(128)S(1)} %pad_add_fusion.pos_ref, s32[4,4,9]{2,1,0:T(4,128)S(1)} %copy-done.3, s32[4,4]{1,0:T(4,128)S(1)} %copy-done.4, ...), custom_call_target="tpu_custom_call" | custom-call | flops 1000000000 | bytes 12000000 | tf_op jit(solution)/shard_map/local_products/pallas_call | solution.py:257
  35.9 0.7 collective-permute-done.2.up_ref
  36.6 0.9 collective-permute-done.3.down_ref
  37.5 3.1 %halo_products.1 = (bf16[1024,1280]{1,0:T(8,128)(2,1)S(1)}, bf16[128,1280]{1,0:T(8,128)(2,1)S(1)}, bf16[128,1280]{1,0:T(8,128)(2,1)S(1)}) custom-call(s32[3]{0:T(128)S(1)} %pad_add_fusion.pos_ref, bf16[4,256,1152]{2,1,0:T(8,128)(2,1)S(1)} %get-tuple-element.26.ad_ref, bf16[256,1024]{1,0:T(8,128)(2,1)S(1)} %get-tuple-element.27.pt_ref, ...), custom_call_target="tpu_custom_call" | custom-call | flops 1500000000 | bytes 12000000 | tf_op jit(solution)/shard_map/halo_products/pallas_call | solution.py:331
  40.6 1.1 %own_pieces.1 = (f32[256,1280]{1,0:T(8,128)S(1)}, bf16[256,1280]{1,0:T(8,128)(2,1)S(1)}) custom-call(bf16[512,1024]{1,0:T(8,128)(2,1)S(1)} %get-tuple-element.25.pt_ref, bf16[1024,1280]{1,0:T(8,128)(2,1)S(1)} %get-tuple-element.34.im_ref), custom_call_target="tpu_custom_call" | custom-call | flops 1400000000 | bytes 6000000 | tf_op jit(solution)/shard_map/own_pieces/pallas_call | solution.py:352
  41.8 2.8 %collective-permute-start.4 = (bf16[256,1280]{1,0:T(8,128)(2,1)S(1)}, bf16[256,1280]{1,0:T(8,128)(2,1)S(1)}, u32[]{:S(2)}, u32[]{:S(2)}) collective-permute-start(bf16[256,1280]{1,0:T(8,128)(2,1)S(1)} %get-tuple-element.36), channel_id=1, source_target_pairs={{0,1},{1,0},{2,3},{3,2},{4,5},{5,4},{6,7},{7,6},{8,9},{9,8},{10,11... | collective-permute-start | bytes 1966088 | tf_op jit(solution)/shard_map/ppermute | solution.py:26
  44.5 1.9 %collective-permute-start.5 = (bf16[128,1280]{1,0:T(8,128)(2,1)S(1)}, bf16[128,1280]{1,0:T(8,128)(2,1)S(1)}, u32[]{:S(2)}, u32[]{:S(2)}) collective-permute-start(bf16[128,1280]{1,0:T(8,128)(2,1)S(1)} %get-tuple-element.37), channel_id=1, source_target_pairs={{0,30},{1,3},{2,0},{3,5},{4,2},{5,7},{6,4},{7,9},{8,6},{9,11},{10,... | collective-permute-start | bytes 983048 | tf_op jit(solution)/shard_map/ppermute | solution.py:26
  46.5 3.5 %collective-permute-start.6 = (bf16[128,1280]{1,0:T(8,128)(2,1)S(1)}, bf16[128,1280]{1,0:T(8,128)(2,1)S(1)}, u32[]{:S(2)}, u32[]{:S(2)}) collective-permute-start(bf16[128,1280]{1,0:T(8,128)(2,1)S(1)} %get-tuple-element.38), channel_id=1, source_target_pairs={{0,31},{1,2},{2,1},{3,4},{4,3},{5,6},{6,5},{7,8},{8,7},{9,10},{10,... | collective-permute-start | bytes 983048 | tf_op jit(solution)/shard_map/ppermute | solution.py:26
  50.0 5.7 %collective-permute-done.5.same_ref = bf16[128,1280]{1,0:T(8,128)(2,1)S(1)} collective-permute-done((bf16[128,1280]{1,0:T(8,128)(2,1)S(1)}, bf16[128,1280]{1,0:T(8,128)(2,1)S(1)}, u32[]{:S(2)}, u32[]{:S(2)}) %collective-permute-start.5) | collective-permute-done | bytes 327712 | tf_op jit(solution)/shard_map/ppermute | solution.py:26
  55.7 1.0 collective-permute-done.6.other_ref
  56.6 0.0 collective-permute-done.4.swap_own.swap_partner
  56.6 0.6 shard_map.56
  57.3 5.3 %collective-permute-start.7 = (bf16[2,32,1792]{2,1,0:T(8,128)(2,1)S(1)}, bf16[2,32,1792]{2,1,0:T(8,128)(2,1)S(1)}, u32[]{:S(2)}, u32[]{:S(2)}) collective-permute-start(bf16[2,32,1792]{2,1,0:T(8,128)(2,1)S(1)} %shard_map.56), channel_id=1, source_target_pairs={{0,32},{1,481},{2,34},{3,483},{4,36},{5,485},{6,38},{7,487},{8,40}... | collective-permute-start | bytes 688136 | tf_op jit(solution)/shard_map/ppermute | solution.py:26
  62.6 0.6 shard_map.57
  63.3 2.6 %collective-permute-start.8 = (bf16[2,32,1792]{2,1,0:T(8,128)(2,1)S(1)}, bf16[2,32,1792]{2,1,0:T(8,128)(2,1)S(1)}, u32[]{:S(2)}, u32[]{:S(2)}) collective-permute-start(bf16[2,32,1792]{2,1,0:T(8,128)(2,1)S(1)} %shard_map.57), channel_id=1, source_target_pairs={{0,64},{1,449},{2,66},{3,451},{4,68},{5,453},{6,70},{7,455},{8,72}... | collective-permute-start | bytes 688136 | tf_op jit(solution)/shard_map/ppermute | solution.py:26
  65.9 0.6 shard_map.58
  66.5 5.2 %collective-permute-start.9 = (bf16[2,32,1792]{2,1,0:T(8,128)(2,1)S(1)}, bf16[2,32,1792]{2,1,0:T(8,128)(2,1)S(1)}, u32[]{:S(2)}, u32[]{:S(2)}) collective-permute-start(bf16[2,32,1792]{2,1,0:T(8,128)(2,1)S(1)} %shard_map.58), channel_id=1, source_target_pairs={{0,96},{1,417},{2,98},{3,419},{4,100},{5,421},{6,102},{7,423},{8,1... | collective-permute-start | bytes 688136 | tf_op jit(solution)/shard_map/ppermute | solution.py:26
  71.7 0.6 shard_map.55
  72.4 0.0 collective-permute-done.7
  72.4 0.0 collective-permute-done.8
  72.4 4.0 %collective-permute-done.9 = bf16[2,32,1792]{2,1,0:T(8,128)(2,1)S(1)} collective-permute-done((bf16[2,32,1792]{2,1,0:T(8,128)(2,1)S(1)}, bf16[2,32,1792]{2,1,0:T(8,128)(2,1)S(1)}, u32[]{:S(2)}, u32[]{:S(2)}) %collective-permute-start.9) | collective-permute-done | bytes 229408 | tf_op jit(solution)/shard_map/ppermute | solution.py:26
  76.5 0.1 convert_add_fusion
  76.6 8.2 %collective-permute-start.10 = (bf16[2,16,1792]{2,1,0:T(8,128)(2,1)S(1)}, bf16[2,16,1792]{2,1,0:T(8,128)(2,1)S(1)}, u32[]{:S(2)}, u32[]{:S(2)}) collective-permute-start(bf16[2,16,1792]{2,1,0:T(8,128)(2,1)S(1)} %slice.29), channel_id=1, source_target_pairs={{0,128},{1,385},{2,130},{3,387},{4,132},{5,389},{6,134},{7,391},{8... | collective-permute-start | bytes 344072 | tf_op jit(solution)/shard_map/ppermute | solution.py:26
  84.8 1.8 %collective-permute-done.10 = bf16[2,16,1792]{2,1,0:T(8,128)(2,1)S(1)} collective-permute-done((bf16[2,16,1792]{2,1,0:T(8,128)(2,1)S(1)}, bf16[2,16,1792]{2,1,0:T(8,128)(2,1)S(1)}, u32[]{:S(2)}, u32[]{:S(2)}) %collective-permute-start.10) | collective-permute-done | bytes 114720 | tf_op jit(solution)/shard_map/ppermute | solution.py:26
  86.6 11.0 %collective-permute-start.11 = (f32[16,1792]{1,0:T(8,128)S(1)}, f32[16,1792]{1,0:T(8,128)S(1)}, u32[]{:S(2)}, u32[]{:S(2)}) collective-permute-start(f32[16,1792]{1,0:T(8,128)S(1)} %slice_bitcast_fusion), channel_id=1, source_target_pairs={{0,33},{1,480},{2,35},{3,482},{4,37},{5,484},{6,39},{7,486},{8,41}... | collective-permute-start | bytes 344072 | tf_op jit(solution)/shard_map/ppermute | solution.py:26
  97.6 2.5 %collective-permute-done.11 = f32[16,1792]{1,0:T(8,128)S(1)} collective-permute-done((f32[16,1792]{1,0:T(8,128)S(1)}, f32[16,1792]{1,0:T(8,128)S(1)}, u32[]{:S(2)}, u32[]{:S(2)}) %collective-permute-start.11) | collective-permute-done | bytes 114720 | tf_op jit(solution)/shard_map/ppermute | solution.py:26
  100.1 0.7 fusion.1
  (4 shorter events, 0.1 us)
Async XLA Ops:
  0.0 30.6 %copy-start.4 = (s32[4,4]{1,0:T(4,128)S(1)}, s32[4,4]{1,0:T(4,128)}, u32[]{:S(2)}) copy-start(s32[4,4]{1,0:T(4,128)} %live_ref.1) | copy-start | bytes 196
  0.0 30.6 %copy-start.3 = (s32[4,4,9]{2,1,0:T(4,128)S(1)}, s32[4,4,9]{2,1,0:T(4,128)}, u32[]{:S(2)}) copy-start(s32[4,4,9]{2,1,0:T(4,128)} %codes_ref.1) | copy-start | bytes 1732
  0.1 1.4 %copy-start = (bf16[4,4,6,64,64]{4,3,2,1,0:T(8,128)(2,1)S(1)}, bf16[4,4,6,64,64]{4,3,2,1,0:T(8,128)(2,1)}, u32[]{:S(2)}) copy-start(bf16[4,4,6,64,64]{4,3,2,1,0:T(8,128)(2,1)} %param.8) | copy-start | bytes 2359300
  1.5 0.7 copy-start.2
  2.2 28.5 %copy-start.1 = (bf16[4,4,9,64,64]{4,3,2,1,0:T(8,128)(2,1)S(1)}, bf16[4,4,9,64,64]{4,3,2,1,0:T(8,128)(2,1)}, u32[]{:S(2)}) copy-start(bf16[4,4,9,64,64]{4,3,2,1,0:T(8,128)(2,1)} %param.5) | copy-start | bytes 3538948
  3.4 14.8 %collective-permute-start = (bf16[832,128]{1,0:T(8,128)(2,1)S(1)}, bf16[832,128]{1,0:T(8,128)(2,1)S(1)}, u32[]{:S(2)}, u32[]{:S(2)}) collective-permute-start(bf16[832,128]{1,0:T(8,128)(2,1)S(1)} %get-tuple-element.23), channel_id=1, source_target_pairs={{0,31},{1,2},{2,1},{3,4},{4,3},{5,6},{6,5},{7,8},{8,7},{9,10},{10,... | collective-permute-start | bytes 638984 | tf_op jit(solution)/shard_map/ppermute | solution.py:26
  8.0 10.2 %collective-permute-start.1 = (bf16[832,128]{1,0:T(8,128)(2,1)S(1)}, bf16[832,128]{1,0:T(8,128)(2,1)S(1)}, u32[]{:S(2)}, u32[]{:S(2)}) collective-permute-start(bf16[832,128]{1,0:T(8,128)(2,1)S(1)} %get-tuple-element.24), channel_id=1, source_target_pairs={{0,1},{1,0},{2,3},{3,2},{4,5},{5,4},{6,7},{7,6},{8,9},{9,8},{10,11... | collective-permute-start | bytes 638984 | tf_op jit(solution)/shard_map/ppermute | solution.py:26
  18.3 18.3 %collective-permute-start.2 = (bf16[1248,128]{1,0:T(8,128)(2,1)S(1)}, bf16[1248,128]{1,0:T(8,128)(2,1)S(1)}, u32[]{:S(2)}, u32[]{:S(2)}) collective-permute-start(bf16[1248,128]{1,0:T(8,128)(2,1)S(1)} %get-tuple-element.32), channel_id=1, source_target_pairs={{0,32},{1,33},{2,34},{3,35},{4,36},{5,37},{6,38},{7,39},{8,40},{9,... | collective-permute-start | bytes 958472 | tf_op jit(solution)/shard_map/ppermute | solution.py:26
  21.1 16.4 %collective-permute-start.3 = (bf16[1248,128]{1,0:T(8,128)(2,1)S(1)}, bf16[1248,128]{1,0:T(8,128)(2,1)S(1)}, u32[]{:S(2)}, u32[]{:S(2)}) collective-permute-start(bf16[1248,128]{1,0:T(8,128)(2,1)S(1)} %get-tuple-element.33), channel_id=1, source_target_pairs={{0,480},{1,481},{2,482},{3,483},{4,484},{5,485},{6,486},{7,487},{8... | collective-permute-start | bytes 958472 | tf_op jit(solution)/shard_map/ppermute | solution.py:26
  41.8 14.9 %collective-permute-start.4 = (bf16[256,1280]{1,0:T(8,128)(2,1)S(1)}, bf16[256,1280]{1,0:T(8,128)(2,1)S(1)}, u32[]{:S(2)}, u32[]{:S(2)}) collective-permute-start(bf16[256,1280]{1,0:T(8,128)(2,1)S(1)} %get-tuple-element.36), channel_id=1, source_target_pairs={{0,1},{1,0},{2,3},{3,2},{4,5},{5,4},{6,7},{7,6},{8,9},{9,8},{10,11... | collective-permute-start | bytes 1966088 | tf_op jit(solution)/shard_map/ppermute | solution.py:26
  44.5 11.1 %collective-permute-start.5 = (bf16[128,1280]{1,0:T(8,128)(2,1)S(1)}, bf16[128,1280]{1,0:T(8,128)(2,1)S(1)}, u32[]{:S(2)}, u32[]{:S(2)}) collective-permute-start(bf16[128,1280]{1,0:T(8,128)(2,1)S(1)} %get-tuple-element.37), channel_id=1, source_target_pairs={{0,30},{1,3},{2,0},{3,5},{4,2},{5,7},{6,4},{7,9},{8,6},{9,11},{10,... | collective-permute-start | bytes 983048 | tf_op jit(solution)/shard_map/ppermute | solution.py:26
  46.5 10.2 %collective-permute-start.6 = (bf16[128,1280]{1,0:T(8,128)(2,1)S(1)}, bf16[128,1280]{1,0:T(8,128)(2,1)S(1)}, u32[]{:S(2)}, u32[]{:S(2)}) collective-permute-start(bf16[128,1280]{1,0:T(8,128)(2,1)S(1)} %get-tuple-element.38), channel_id=1, source_target_pairs={{0,31},{1,2},{2,1},{3,4},{4,3},{5,6},{6,5},{7,8},{8,7},{9,10},{10,... | collective-permute-start | bytes 983048 | tf_op jit(solution)/shard_map/ppermute | solution.py:26
  57.3 15.1 %collective-permute-start.7 = (bf16[2,32,1792]{2,1,0:T(8,128)(2,1)S(1)}, bf16[2,32,1792]{2,1,0:T(8,128)(2,1)S(1)}, u32[]{:S(2)}, u32[]{:S(2)}) collective-permute-start(bf16[2,32,1792]{2,1,0:T(8,128)(2,1)S(1)} %shard_map.56), channel_id=1, source_target_pairs={{0,32},{1,481},{2,34},{3,483},{4,36},{5,485},{6,38},{7,487},{8,40}... | collective-permute-start | bytes 688136 | tf_op jit(solution)/shard_map/ppermute | solution.py:26
  63.3 9.2 %collective-permute-start.8 = (bf16[2,32,1792]{2,1,0:T(8,128)(2,1)S(1)}, bf16[2,32,1792]{2,1,0:T(8,128)(2,1)S(1)}, u32[]{:S(2)}, u32[]{:S(2)}) collective-permute-start(bf16[2,32,1792]{2,1,0:T(8,128)(2,1)S(1)} %shard_map.57), channel_id=1, source_target_pairs={{0,64},{1,449},{2,66},{3,451},{4,68},{5,453},{6,70},{7,455},{8,72}... | collective-permute-start | bytes 688136 | tf_op jit(solution)/shard_map/ppermute | solution.py:26
  66.5 10.0 %collective-permute-start.9 = (bf16[2,32,1792]{2,1,0:T(8,128)(2,1)S(1)}, bf16[2,32,1792]{2,1,0:T(8,128)(2,1)S(1)}, u32[]{:S(2)}, u32[]{:S(2)}) collective-permute-start(bf16[2,32,1792]{2,1,0:T(8,128)(2,1)S(1)} %shard_map.58), channel_id=1, source_target_pairs={{0,96},{1,417},{2,98},{3,419},{4,100},{5,421},{6,102},{7,423},{8,1... | collective-permute-start | bytes 688136 | tf_op jit(solution)/shard_map/ppermute | solution.py:26
  76.6 10.0 %collective-permute-start.10 = (bf16[2,16,1792]{2,1,0:T(8,128)(2,1)S(1)}, bf16[2,16,1792]{2,1,0:T(8,128)(2,1)S(1)}, u32[]{:S(2)}, u32[]{:S(2)}) collective-permute-start(bf16[2,16,1792]{2,1,0:T(8,128)(2,1)S(1)} %slice.29), channel_id=1, source_target_pairs={{0,128},{1,385},{2,130},{3,387},{4,132},{5,389},{6,134},{7,391},{8... | collective-permute-start | bytes 344072 | tf_op jit(solution)/shard_map/ppermute | solution.py:26
  86.6 13.4 %collective-permute-start.11 = (f32[16,1792]{1,0:T(8,128)S(1)}, f32[16,1792]{1,0:T(8,128)S(1)}, u32[]{:S(2)}, u32[]{:S(2)}) collective-permute-start(f32[16,1792]{1,0:T(8,128)S(1)} %slice_bitcast_fusion), channel_id=1, source_target_pairs={{0,33},{1,480},{2,35},{3,482},{4,37},{5,484},{6,39},{7,486},{8,41}... | collective-permute-start | bytes 344072 | tf_op jit(solution)/shard_map/ppermute | solution.py:26

commit v5 on v4

--- a/solution.py
+++ b/solution.py
@@ -92,22 +92,23 @@
         pack(pos_ref, blocks_ref, p_ref, chip_ref, x, x, 3 - core * 3)
 
 
-def packed(pos, blocks, tiles):
-    return pl.pallas_call(
-        pack_kernel,
+def packed(kernel, pos, blocks, tiles):
+    return pl.pallas_call(
+        kernel,
         out_shape=(jax.ShapeDtypeStruct((PART4, 128), BF16),) * 2,
         in_specs=[smem(), smem(), vmem()],
         out_specs=(vmem(),) * 2,
-        name="packed",
         **budget(4, 0, 2000000),
     )(pos, blocks, tiles)
 
 
-def place_kernel(pos_ref, blocks_ref, p_ref, po_ref, up_ref, down_ref, inv_ref):
+def row_kernel(pos_ref, blocks_ref, p_ref, up_ref, down_ref):
     for y in range(4):
         pack(pos_ref, blocks_ref, p_ref, up_ref, y, 3, y)
         pack(pos_ref, blocks_ref, p_ref, down_ref, y, 0, y)
 
+
+def place_kernel(pos_ref, blocks_ref, p_ref, po_ref, inv_ref):
     def prepare(b, carry):
         y, x = b // 4, b % 4
         for column in range(12):
@@ -138,13 +139,9 @@
 def place(pos, blocks, tiles):
     return pl.pallas_call(
         place_kernel,
-        out_shape=(
-            jax.ShapeDtypeStruct((1024, 768), BF16),
-            jax.ShapeDtypeStruct((PART4, 128), BF16),
-            jax.ShapeDtypeStruct((PART4, 128), BF16),
-        ),
+        out_shape=jax.ShapeDtypeStruct((1024, 768), BF16),
         in_specs=[smem(), smem(), vmem()],
-        out_specs=(vmem(),) * 3,
+        out_specs=vmem(),
         scratch_shapes=[pltpu.SMEM((192,), jnp.int32)],
         name="place",
         **budget(4, 0, 2000000),
@@ -247,7 +244,7 @@
                 flow = shifted // 8
                 near = jnp.where(flow == 0, shifted, 15 - shifted)
                 half = (flow + core) % 2
-                spot = half * 8 + (near % 4) * 2 + near // 4
+                spot = half * 8 + (near & 1) * 4 + (near & 2) + (near >> 2)
                 row = pl.multiple_of(max(n - 1, 0) * 256 + spot * 16, 16)
                 pt_ref = rest_ref if n else outer_ref
                 pt_ref[pl.ds(row, 16), 256 * y : 256 * y + 256] = flipped[16 * o : 16 * o + 16, :]
@@ -362,48 +359,42 @@
     )(pt, im)
 
 
-def merge_kernel(
-    pos_ref, keep_own, keep_partner, swap_own, swap_partner, same_ref, other_ref, out_ref, sum_ref
-):
-    def merge(low, high):
-        def add(n, at, ref):
-            sum_ref[n, :, at : at + 1280] += ref[...].astype(F32)
-
-        zero = jnp.zeros((32, 256), F32)
-        for n in range(2):
-            for at in (0, 256, 1280, 1536):
-                sum_ref[n, :, at : at + 256] = zero
-        sum_ref[0, :, 256:1536] = keep_own[...]
-        sum_ref[1, :, 256:1536] = swap_own[...].astype(F32)
-        add(0, high, swap_partner)
-        add(0, low, other_ref)
-        add(1, low, keep_partner)
-        add(1, high, same_ref)
+def merge_kernel(pos_ref, low_ref, middle_ref, high_ref, out_ref, sum_ref):
+    zero = jnp.zeros((64, 256), F32)
+    for at in (0, 1536):
+        sum_ref[:, at : at + 256] = zero
+    sum_ref[:, 256:1536] = middle_ref[...].astype(F32)
+
+    def add(low, high):
+        sum_ref[:, 0:1280] += low[...].astype(F32)
+        sum_ref[:, 512:1792] += high[...].astype(F32)
 
     @pl.when(pos_ref[0] == 0)
     def _():
-        merge(0, 512)
+        add(low_ref, high_ref)
 
     @pl.when(pos_ref[0] == 1)
     def _():
-        merge(512, 0)
+        add(high_ref, low_ref)
 
     out_ref[...] = sum_ref[...].astype(out_ref.dtype)
 
 
-def merged(pos, keep, swap, same, other, group):
+def merged(pos, low, middle, high, dtype):
+    parts = (low, middle, high)
+
     def rows(at):
-        return pl.BlockSpec((32, 1280), lambda i: (at, 0))
+        return pl.BlockSpec((64, 1280), lambda i: (at, 0))
 
     return pl.pallas_call(
         merge_kernel,
         grid=(1,),
-        out_shape=jax.ShapeDtypeStruct((2, 32, 1792), F32 if group == 0 else BF16),
-        in_specs=[smem()] + [rows(group), rows(group + 4)] * 2 + [rows(group)] * 2,
-        out_specs=pl.BlockSpec((2, 32, 1792), lambda i: (0, 0, 0)),
-        scratch_shapes=[pltpu.VMEM((2, 32, 1792), F32)],
+        out_shape=jax.ShapeDtypeStruct((64, 1792), dtype),
+        in_specs=[smem()] + [rows(at) for _, at in parts],
+        out_specs=pl.BlockSpec((64, 1792), lambda i: (0, 0)),
+        scratch_shapes=[pltpu.VMEM((64, 1792), F32)],
         **budget(4, 0, 1000000),
-    )(pos, keep, keep, swap, swap, same, other)
+    )(pos, *(array for array, _ in parts))
 
 
 def body(operator_tiles, neighbour_codes, live_slots, prolong_tiles, coarse_blocks):
@@ -413,13 +404,14 @@
     pos = jnp.stack([core, r, s]).astype(jnp.int32)
 
     tiles = prolong_tiles.reshape(96, B, B)
-    cross, chip = packed(pos, coarse_blocks, tiles)
+    cross, chip = packed(pack_kernel, pos, coarse_blocks, tiles)
     cross_in = send(cross, lambda r, s: (r, s - sign(s)))
     chip_in = send(chip, lambda r, s: (r, s + sign(s)))
-    po, up_own, down_own = place(pos, coarse_blocks, tiles)
+    up_own, down_own = packed(row_kernel, pos, coarse_blocks, tiles)
     up, down = rims(up_own, down_own, cross_in, chip_in)
     up_in = send(up, lambda r, s: (r + 1, s))
     down_in = send(down, lambda r, s: (r - 1, s))
+    po = place(pos, coarse_blocks, tiles)
     ad, outer, rest, part, side = local_products(
         pos, neighbour_codes, live_slots, operator_tiles.reshape(144, B, B), po, cross_in, chip_in
     )
@@ -428,17 +420,32 @@
     same_in = send(same, lambda r, s: (r, s - 2 * sign(s)))
     keep, swap = own_pieces(rest, im)
     swap_in = send(swap, lambda r, s: (r, s + sign(s)))
-    moved = {}
-    for step in (3, 2, 1):
-        msg = merged(pos, keep, swap_in, same_in, other_in, step)
-        moved[step] = send(msg, lambda r, s: (r + step * sign(s), s))
-    acc = merged(pos, keep, swap_in, same_in, other_in, 0)
-    for step in (1, 2, 3):
-        acc = acc + moved[step].astype(F32)
-    msg = acc[:, 16:].astype(BF16)
-    acc = acc[:, :16] + send(msg, lambda r, s: (r + 4 * sign(s), s)).astype(F32)
-    last = send(acc[1], lambda r, s: (r + sign(s), s + sign(s)))
-    return (acc[0] + last)[None]
+    other_slab = ((keep, 2), (swap_in, 0), (same_in, 0))
+    own_slab = ((other_in, 0), (keep, 0), (swap_in, 2))
+
+    def later(parts):
+        return tuple((array, at + 1) for array, at in parts)
+
+    def hop(step, value):
+        return send(value, lambda r, s: (r + step * sign(s), s)).astype(F32)
+
+    first = {}
+    kept = {}
+    for label, parts in (("p", other_slab), ("o", own_slab)):
+        first[label] = hop(1, merged(pos, *later(parts), BF16))
+    for label, parts in (("p", other_slab), ("o", own_slab)):
+        kept[label] = merged(pos, *parts, F32)
+    total = {}
+    for label in ("p", "o"):
+        got = first[label]
+        acc = kept[label]
+        for step, size in ((2, 32), (4, 16)):
+            moved = hop(step, (acc[size:] + got[size:]).astype(BF16))
+            acc = acc[:size] + got[:size]
+            got = moved
+        total[label] = acc + got
+    last = send(total["p"], lambda r, s: (r + sign(s), s + sign(s)))
+    return (total["o"] + last)[None]
 
 
 def solution(mesh):

time: 102 us -> 101 us (level)
  waiting for transfers between devices: 16.6 us -> 13.3 us
  starting transfers between devices: 63.6 us -> 65.1 us
    ppermute x12 -> x14, waiting for transfers between devices: 16.6 us -> 13.3 us  [send(): return lax.ppermute(value, ('row', 'col'), joint(rule))]
    ppermute x12 -> x14, starting transfers between devices: 63.6 us -> 65.1 us  [send(): return lax.ppermute(value, ('row', 'col'), joint(rule))]
    pallas_call x6 -> x7, Pallas kernels: 7.88 us -> 8.66 us  [the longest x1 3.57 us: place(): pl.pallas_call(place_kernel, out_shape=jax.ShapeDtypeStruct((1024, 768),...]
    unnamed x10 -> x12, local copies, waits for them, and re-layouts: 2.12 us -> 2.13 us
  transfers between devices with their start and end apart: 12 -> 14, of which waited for: 7 -> 3; matrix products, arithmetic and copies ran while one was open for 0% -> 0% of each run, Pallas kernels for 11% -> 12%
where the time goes in v5:
time: 101 us; the launch traced here: 100 us
  starting transfers between devices  65.1 us (64%)
  Pallas kernels  18 us (18%)
  waiting for transfers between devices  13.3 us (13%)
  local copies, waits for them, and re-layouts  2.13 us (2%)
  other arithmetic  1.05 us (1%)
    ppermute x14, starting transfers between devices, send(): return lax.ppermute(value, ('row', 'col'), joint(rule))  65.1 us
    ppermute x14, waiting for transfers between devices, send(): return lax.ppermute(value, ('row', 'col'), joint(rule))  13.3 us
    pallas_call x1, Pallas kernels, local_products(): pl.pallas_call(local_kernel, out_shape=(jax.ShapeDtypeStruct((4, 256, 115...  5.06 us
    pallas_call x1, Pallas kernels, place(): pl.pallas_call(place_kernel, out_shape=jax.ShapeDtypeStruct((1024, 768),...  3.57 us
    pallas_call x1, Pallas kernels, halo_products(): pl.pallas_call(halo_kernel, out_shape=(jax.ShapeDtypeStruct((1024, 1280),...  3.15 us
    pallas_call x4, Pallas kernels, merged(): pl.pallas_call(merge_kernel, grid=(1,), out_shape=jax.ShapeDtypeStruct((6...  2.67 us
    pallas_call x2, Pallas kernels, packed(): pl.pallas_call(kernel, out_shape=(jax.ShapeDtypeStruct((PART4, 128), BF16...  2.42 us
    unnamed x12, local copies, waits for them, and re-layouts  2.13 us
  transfers between devices with their start and end apart: 14, of which 3 were waited for; matrix products, arithmetic and copies ran while one was open for 0% of the time, Pallas kernels for 12%

profile of v5, /device:TPU:1, one launch (start us, length us, event | category | flops | bytes accessed | tf_op | source)
XLA Modules:
  0.0 100.0 jit_solution(17657263136968535918)
XLA Ops:
  0.0 0.1 pad_add_fusion.pos_ref
  0.1 1.4 %copy-done = bf16[4,4,6,64,64]{4,3,2,1,0:T(8,128)(2,1)S(1)} copy-done((bf16[4,4,6,64,64]{4,3,2,1,0:T(8,128)(2,1)S(1)}, bf16[4,4,6,64,64]{4,3,2,1,0:T(8,128)(2,1)}, u32[]{:S(2)}) %copy-start) | copy-done | bytes 786456
  1.5 0.7 copy-done.3
  2.2 1.2 %shard_map.55 = (bf16[832,128]{1,0:T(8,128)(2,1)S(1)}, bf16[832,128]{1,0:T(8,128)(2,1)S(1)}) custom-call(s32[3]{0:T(128)S(1)} %pad_add_fusion.pos_ref, s32[4,4,6]{2,1,0:T(4,128)S(1)} %copy-done.3, bf16[96,64,64]{2,1,0:T(8,128)(2,1)S(1)} %bitcast.7), custom_call_target="tpu_custom_call" | custom-call | bytes 2000000 | tf_op jit(solution)/shard_map/pallas_call | solution.py:96
  3.4 4.6 %collective-permute-start = (bf16[832,128]{1,0:T(8,128)(2,1)S(1)}, bf16[832,128]{1,0:T(8,128)(2,1)S(1)}, u32[]{:S(2)}, u32[]{:S(2)}) collective-permute-start(bf16[832,128]{1,0:T(8,128)(2,1)S(1)} %get-tuple-element.21), channel_id=1, source_target_pairs={{0,31},{1,2},{2,1},{3,4},{4,3},{5,6},{6,5},{7,8},{8,7},{9,10},{10,... | collective-permute-start | bytes 638984 | tf_op jit(solution)/shard_map/ppermute | solution.py:26
  8.0 6.1 %collective-permute-start.1 = (bf16[832,128]{1,0:T(8,128)(2,1)S(1)}, bf16[832,128]{1,0:T(8,128)(2,1)S(1)}, u32[]{:S(2)}, u32[]{:S(2)}) collective-permute-start(bf16[832,128]{1,0:T(8,128)(2,1)S(1)} %get-tuple-element.22), channel_id=1, source_target_pairs={{0,1},{1,0},{2,3},{3,2},{4,5},{5,4},{6,7},{7,6},{8,9},{9,8},{10,11... | collective-permute-start | bytes 638984 | tf_op jit(solution)/shard_map/ppermute | solution.py:26
  14.1 1.2 %shard_map.56 = (bf16[832,128]{1,0:T(8,128)(2,1)S(1)}, bf16[832,128]{1,0:T(8,128)(2,1)S(1)}) custom-call(s32[3]{0:T(128)S(1)} %pad_add_fusion.pos_ref, s32[4,4,6]{2,1,0:T(4,128)S(1)} %copy-done.3, bf16[96,64,64]{2,1,0:T(8,128)(2,1)S(1)} %bitcast.8), custom_call_target="tpu_custom_call" | custom-call | bytes 2000000 | tf_op jit(solution)/shard_map/pallas_call | solution.py:96
  15.3 0.0 copy-start.2
  15.3 0.0 copy-start.4
  15.3 0.0 copy-start.5
  15.3 0.0 collective-permute-done.cross_ref
  15.4 0.0 collective-permute-done.1.chip_ref
  15.4 3.0 %collective-permute-start.2 = (bf16[1248,128]{1,0:T(8,128)(2,1)S(1)}, bf16[1248,128]{1,0:T(8,128)(2,1)S(1)}, u32[]{:S(2)}, u32[]{:S(2)}) collective-permute-start(bf16[1248,128]{1,0:T(8,128)(2,1)S(1)} %get-tuple-element.29), channel_id=1, source_target_pairs={{0,32},{1,33},{2,34},{3,35},{4,36},{5,37},{6,38},{7,39},{8,40},{9,... | collective-permute-start | bytes 958472 | tf_op jit(solution)/shard_map/ppermute | solution.py:26
  18.4 9.5 %collective-permute-start.3 = (bf16[1248,128]{1,0:T(8,128)(2,1)S(1)}, bf16[1248,128]{1,0:T(8,128)(2,1)S(1)}, u32[]{:S(2)}, u32[]{:S(2)}) collective-permute-start(bf16[1248,128]{1,0:T(8,128)(2,1)S(1)} %get-tuple-element.30), channel_id=1, source_target_pairs={{0,480},{1,481},{2,482},{3,483},{4,484},{5,485},{6,486},{7,487},{8... | collective-permute-start | bytes 958472 | tf_op jit(solution)/shard_map/ppermute | solution.py:26
  27.9 0.0 copy-done.1
  27.9 3.6 %place.1.po_ref = bf16[1024,768]{1,0:T(8,128)(2,1)S(1)} custom-call(s32[3]{0:T(128)S(1)} %pad_add_fusion.pos_ref, s32[4,4,6]{2,1,0:T(4,128)S(1)} %copy-done.3, bf16[96,64,64]{2,1,0:T(8,128)(2,1)S(1)} %bitcast.9), custom_call_target="tpu_custom_call" | custom-call | bytes 2000000 | tf_op jit(solution)/shard_map/place/pallas_call | solution.py:140
  31.5 5.1 %local_products.1 = (bf16[4,256,1152]{2,1,0:T(8,128)(2,1)S(1)}, bf16[256,1024]{1,0:T(8,128)(2,1)S(1)}, bf16[512,1024]{1,0:T(8,128)(2,1)S(1)}, f32[1024,768]{1,0:T(8,128)S(1)}, bf16[2,256,768]{2,1,0:T(8,128)(2,1)S(1)}) custom-call(s32[3]{0:T(128)S(1)} %pad_add_fusion.pos_ref, s32[4,4,9]{2,1,0:T(4,128)S(1)} %copy-done.4, s32[4,4]{1,0:T(4,128)S(1)} %copy-done.5, ...), custom_call_target="tpu_custom_call" | custom-call | flops 1000000000 | bytes 12000000 | tf_op jit(solution)/shard_map/local_products/pallas_call | solution.py:254
  36.6 0.0 collective-permute-done.2.up_ref
  36.6 0.0 collective-permute-done.3.down_ref
  36.6 3.1 %halo_products.1 = (bf16[1024,1280]{1,0:T(8,128)(2,1)S(1)}, bf16[128,1280]{1,0:T(8,128)(2,1)S(1)}, bf16[128,1280]{1,0:T(8,128)(2,1)S(1)}) custom-call(s32[3]{0:T(128)S(1)} %pad_add_fusion.pos_ref, bf16[4,256,1152]{2,1,0:T(8,128)(2,1)S(1)} %get-tuple-element.23.ad_ref, bf16[256,1024]{1,0:T(8,128)(2,1)S(1)} %get-tuple-element.24.pt_ref, ...), custom_call_target="tpu_custom_call" | custom-call | flops 1500000000 | bytes 12000000 | tf_op jit(solution)/shard_map/halo_products/pallas_call | solution.py:328
  39.8 1.1 %own_pieces.1 = (f32[256,1280]{1,0:T(8,128)S(1)}, bf16[256,1280]{1,0:T(8,128)(2,1)S(1)}) custom-call(bf16[512,1024]{1,0:T(8,128)(2,1)S(1)} %get-tuple-element.32.pt_ref, bf16[1024,1280]{1,0:T(8,128)(2,1)S(1)} %get-tuple-element.33.im_ref), custom_call_target="tpu_custom_call" | custom-call | flops 1400000000 | bytes 6000000 | tf_op jit(solution)/shard_map/own_pieces/pallas_call | solution.py:349
  40.9 2.8 %collective-permute-start.5 = (bf16[256,1280]{1,0:T(8,128)(2,1)S(1)}, bf16[256,1280]{1,0:T(8,128)(2,1)S(1)}, u32[]{:S(2)}, u32[]{:S(2)}) collective-permute-start(bf16[256,1280]{1,0:T(8,128)(2,1)S(1)} %get-tuple-element.35), channel_id=1, source_target_pairs={{0,1},{1,0},{2,3},{3,2},{4,5},{5,4},{6,7},{7,6},{8,9},{9,8},{10,11... | collective-permute-start | bytes 1966088 | tf_op jit(solution)/shard_map/ppermute | solution.py:26
  43.7 1.9 %collective-permute-start.9 = (bf16[128,1280]{1,0:T(8,128)(2,1)S(1)}, bf16[128,1280]{1,0:T(8,128)(2,1)S(1)}, u32[]{:S(2)}, u32[]{:S(2)}) collective-permute-start(bf16[128,1280]{1,0:T(8,128)(2,1)S(1)} %get-tuple-element.36), channel_id=1, source_target_pairs={{0,30},{1,3},{2,0},{3,5},{4,2},{5,7},{6,4},{7,9},{8,6},{9,11},{10,... | collective-permute-start | bytes 983048 | tf_op jit(solution)/shard_map/ppermute | solution.py:26
  45.6 3.5 %collective-permute-start.4 = (bf16[128,1280]{1,0:T(8,128)(2,1)S(1)}, bf16[128,1280]{1,0:T(8,128)(2,1)S(1)}, u32[]{:S(2)}, u32[]{:S(2)}) collective-permute-start(bf16[128,1280]{1,0:T(8,128)(2,1)S(1)} %get-tuple-element.31), channel_id=1, source_target_pairs={{0,31},{1,2},{2,1},{3,4},{4,3},{5,6},{6,5},{7,8},{8,7},{9,10},{10,... | collective-permute-start | bytes 983048 | tf_op jit(solution)/shard_map/ppermute | solution.py:26
  49.2 5.7 %collective-permute-done.9.high_ref = bf16[128,1280]{1,0:T(8,128)(2,1)S(1)} collective-permute-done((bf16[128,1280]{1,0:T(8,128)(2,1)S(1)}, bf16[128,1280]{1,0:T(8,128)(2,1)S(1)}, u32[]{:S(2)}, u32[]{:S(2)}) %collective-permute-start.9) | collective-permute-done | bytes 327712 | tf_op jit(solution)/shard_map/ppermute | solution.py:26
  54.8 0.0 collective-permute-done.5.high_ref.middle_ref
  54.8 0.7 shard_map.60
  55.5 3.6 %collective-permute-start.10 = (bf16[64,1792]{1,0:T(8,128)(2,1)S(1)}, bf16[64,1792]{1,0:T(8,128)(2,1)S(1)}, u32[]{:S(2)}, u32[]{:S(2)}) collective-permute-start(bf16[64,1792]{1,0:T(8,128)(2,1)S(1)} %shard_map.60), channel_id=1, source_target_pairs={{0,32},{1,481},{2,34},{3,483},{4,36},{5,485},{6,38},{7,487},{8,40}... | collective-permute-start | bytes 688136 | tf_op jit(solution)/shard_map/ppermute | solution.py:26
  59.2 0.0 collective-permute-done.4.low_ref
  59.2 0.7 shard_map.58
  59.8 2.6 %collective-permute-start.6 = (bf16[64,1792]{1,0:T(8,128)(2,1)S(1)}, bf16[64,1792]{1,0:T(8,128)(2,1)S(1)}, u32[]{:S(2)}, u32[]{:S(2)}) collective-permute-start(bf16[64,1792]{1,0:T(8,128)(2,1)S(1)} %shard_map.58), channel_id=1, source_target_pairs={{0,32},{1,481},{2,34},{3,483},{4,36},{5,485},{6,38},{7,487},{8,40}... | collective-permute-start | bytes 688136 | tf_op jit(solution)/shard_map/ppermute | solution.py:26
  62.5 0.7 shard_map.59
  63.2 0.7 shard_map.57
  63.8 0.0 collective-permute-done.10
  63.9 0.1 slice_add_fusion.1
  63.9 4.3 %collective-permute-start.11 = (bf16[32,1792]{1,0:T(8,128)(2,1)S(1)}, bf16[32,1792]{1,0:T(8,128)(2,1)S(1)}, u32[]{:S(2)}, u32[]{:S(2)}) collective-permute-start(bf16[32,1792]{1,0:T(8,128)(2,1)S(1)} %get-tuple-element.40), channel_id=1, source_target_pairs={{0,64},{1,449},{2,66},{3,451},{4,68},{5,453},{6,70},{7,455},{8,72}... | collective-permute-start | bytes 344072 | tf_op jit(solution)/shard_map/ppermute | solution.py:26
  68.3 0.0 collective-permute-done.6
  68.3 0.1 slice_add_fusion.3
  68.4 3.1 %collective-permute-start.7 = (bf16[32,1792]{1,0:T(8,128)(2,1)S(1)}, bf16[32,1792]{1,0:T(8,128)(2,1)S(1)}, u32[]{:S(2)}, u32[]{:S(2)}) collective-permute-start(bf16[32,1792]{1,0:T(8,128)(2,1)S(1)} %get-tuple-element.38), channel_id=1, source_target_pairs={{0,64},{1,449},{2,66},{3,451},{4,68},{5,453},{6,70},{7,455},{8,72}... | collective-permute-start | bytes 344072 | tf_op jit(solution)/shard_map/ppermute | solution.py:26
  71.5 0.0 collective-permute-done.11
  71.5 5.6 %collective-permute-start.12 = (bf16[16,1792]{1,0:T(8,128)(2,1)S(1)}, bf16[16,1792]{1,0:T(8,128)(2,1)S(1)}, u32[]{:S(2)}, u32[]{:S(2)}) collective-permute-start(bf16[16,1792]{1,0:T(8,128)(2,1)S(1)} %fusion.2), channel_id=1, source_target_pairs={{0,128},{1,385},{2,130},{3,387},{4,132},{5,389},{6,134},{7,391},{8... | collective-permute-start | bytes 172040 | tf_op jit(solution)/shard_map/ppermute | solution.py:26
  77.1 0.0 collective-permute-done.7
  77.2 3.3 %collective-permute-done.12 = bf16[16,1792]{1,0:T(8,128)(2,1)S(1)} collective-permute-done((bf16[16,1792]{1,0:T(8,128)(2,1)S(1)}, bf16[16,1792]{1,0:T(8,128)(2,1)S(1)}, u32[]{:S(2)}, u32[]{:S(2)}) %collective-permute-start.12) | collective-permute-done | bytes 57376 | tf_op jit(solution)/shard_map/ppermute | solution.py:26
  80.4 9.8 %collective-permute-start.13 = (f32[16,1792]{1,0:T(8,128)S(1)}, f32[16,1792]{1,0:T(8,128)S(1)}, u32[]{:S(2)}, u32[]{:S(2)}) collective-permute-start(f32[16,1792]{1,0:T(8,128)S(1)} %fusion.3), channel_id=1, source_target_pairs={{0,33},{1,480},{2,35},{3,482},{4,37},{5,484},{6,39},{7,486},{8,41}... | collective-permute-start | bytes 344072 | tf_op jit(solution)/shard_map/ppermute | solution.py:26
  90.3 4.7 %collective-permute-start.8 = (bf16[16,1792]{1,0:T(8,128)(2,1)S(1)}, bf16[16,1792]{1,0:T(8,128)(2,1)S(1)}, u32[]{:S(2)}, u32[]{:S(2)}) collective-permute-start(bf16[16,1792]{1,0:T(8,128)(2,1)S(1)} %fusion.4), channel_id=1, source_target_pairs={{0,128},{1,385},{2,130},{3,387},{4,132},{5,389},{6,134},{7,391},{8... | collective-permute-start | bytes 172040 | tf_op jit(solution)/shard_map/ppermute | solution.py:26
  94.9 4.4 %collective-permute-done.8 = bf16[16,1792]{1,0:T(8,128)(2,1)S(1)} collective-permute-done((bf16[16,1792]{1,0:T(8,128)(2,1)S(1)}, bf16[16,1792]{1,0:T(8,128)(2,1)S(1)}, u32[]{:S(2)}, u32[]{:S(2)}) %collective-permute-start.8) | collective-permute-done | bytes 57376 | tf_op jit(solution)/shard_map/ppermute | solution.py:26
  99.3 0.0 collective-permute-done.13
  99.3 0.7 fusion.7
  (14 shorter events, 0.2 us)
Async XLA Ops:
  0.1 1.4 %copy-start = (bf16[4,4,6,64,64]{4,3,2,1,0:T(8,128)(2,1)S(1)}, bf16[4,4,6,64,64]{4,3,2,1,0:T(8,128)(2,1)}, u32[]{:S(2)}) copy-start(bf16[4,4,6,64,64]{4,3,2,1,0:T(8,128)(2,1)} %param.8) | copy-start | bytes 2359300
  1.5 0.7 copy-start.3
  2.2 25.7 %copy-start.1 = (bf16[4,4,6,64,64]{4,3,2,1,0:T(8,128)(2,1)S(1)}, bf16[4,4,6,64,64]{4,3,2,1,0:T(8,128)(2,1)}, u32[]{:S(2)}) copy-start(bf16[4,4,6,64,64]{4,3,2,1,0:T(8,128)(2,1)} %param.8) | copy-start | bytes 2359300
  3.4 11.9 %collective-permute-start = (bf16[832,128]{1,0:T(8,128)(2,1)S(1)}, bf16[832,128]{1,0:T(8,128)(2,1)S(1)}, u32[]{:S(2)}, u32[]{:S(2)}) collective-permute-start(bf16[832,128]{1,0:T(8,128)(2,1)S(1)} %get-tuple-element.21), channel_id=1, source_target_pairs={{0,31},{1,2},{2,1},{3,4},{4,3},{5,6},{6,5},{7,8},{8,7},{9,10},{10,... | collective-permute-start | bytes 638984 | tf_op jit(solution)/shard_map/ppermute | solution.py:26
  8.0 7.3 %collective-permute-start.1 = (bf16[832,128]{1,0:T(8,128)(2,1)S(1)}, bf16[832,128]{1,0:T(8,128)(2,1)S(1)}, u32[]{:S(2)}, u32[]{:S(2)}) collective-permute-start(bf16[832,128]{1,0:T(8,128)(2,1)S(1)} %get-tuple-element.22), channel_id=1, source_target_pairs={{0,1},{1,0},{2,3},{3,2},{4,5},{5,4},{6,7},{7,6},{8,9},{9,8},{10,11... | collective-permute-start | bytes 638984 | tf_op jit(solution)/shard_map/ppermute | solution.py:26
  15.3 16.2 %copy-start.2 = (bf16[4,4,9,64,64]{4,3,2,1,0:T(8,128)(2,1)S(1)}, bf16[4,4,9,64,64]{4,3,2,1,0:T(8,128)(2,1)}, u32[]{:S(2)}) copy-start(bf16[4,4,9,64,64]{4,3,2,1,0:T(8,128)(2,1)} %param.5) | copy-start | bytes 3538948
  15.3 16.2 %copy-start.4 = (s32[4,4,9]{2,1,0:T(4,128)S(1)}, s32[4,4,9]{2,1,0:T(4,128)}, u32[]{:S(2)}) copy-start(s32[4,4,9]{2,1,0:T(4,128)} %codes_ref.1) | copy-start | bytes 1732
  15.3 16.2 %copy-start.5 = (s32[4,4]{1,0:T(4,128)S(1)}, s32[4,4]{1,0:T(4,128)}, u32[]{:S(2)}) copy-start(s32[4,4]{1,0:T(4,128)} %live_ref.1) | copy-start | bytes 196
  15.4 21.2 %collective-permute-start.2 = (bf16[1248,128]{1,0:T(8,128)(2,1)S(1)}, bf16[1248,128]{1,0:T(8,128)(2,1)S(1)}, u32[]{:S(2)}, u32[]{:S(2)}) collective-permute-start(bf16[1248,128]{1,0:T(8,128)(2,1)S(1)} %get-tuple-element.29), channel_id=1, source_target_pairs={{0,32},{1,33},{2,34},{3,35},{4,36},{5,37},{6,38},{7,39},{8,40},{9,... | collective-permute-start | bytes 958472 | tf_op jit(solution)/shard_map/ppermute | solution.py:26
  18.4 18.2 %collective-permute-start.3 = (bf16[1248,128]{1,0:T(8,128)(2,1)S(1)}, bf16[1248,128]{1,0:T(8,128)(2,1)S(1)}, u32[]{:S(2)}, u32[]{:S(2)}) collective-permute-start(bf16[1248,128]{1,0:T(8,128)(2,1)S(1)} %get-tuple-element.30), channel_id=1, source_target_pairs={{0,480},{1,481},{2,482},{3,483},{4,484},{5,485},{6,486},{7,487},{8... | collective-permute-start | bytes 958472 | tf_op jit(solution)/shard_map/ppermute | solution.py:26
  40.9 14.0 %collective-permute-start.5 = (bf16[256,1280]{1,0:T(8,128)(2,1)S(1)}, bf16[256,1280]{1,0:T(8,128)(2,1)S(1)}, u32[]{:S(2)}, u32[]{:S(2)}) collective-permute-start(bf16[256,1280]{1,0:T(8,128)(2,1)S(1)} %get-tuple-element.35), channel_id=1, source_target_pairs={{0,1},{1,0},{2,3},{3,2},{4,5},{5,4},{6,7},{7,6},{8,9},{9,8},{10,11... | collective-permute-start | bytes 1966088 | tf_op jit(solution)/shard_map/ppermute | solution.py:26
  43.7 11.1 %collective-permute-start.9 = (bf16[128,1280]{1,0:T(8,128)(2,1)S(1)}, bf16[128,1280]{1,0:T(8,128)(2,1)S(1)}, u32[]{:S(2)}, u32[]{:S(2)}) collective-permute-start(bf16[128,1280]{1,0:T(8,128)(2,1)S(1)} %get-tuple-element.36), channel_id=1, source_target_pairs={{0,30},{1,3},{2,0},{3,5},{4,2},{5,7},{6,4},{7,9},{8,6},{9,11},{10,... | collective-permute-start | bytes 983048 | tf_op jit(solution)/shard_map/ppermute | solution.py:26
  45.6 13.5 %collective-permute-start.4 = (bf16[128,1280]{1,0:T(8,128)(2,1)S(1)}, bf16[128,1280]{1,0:T(8,128)(2,1)S(1)}, u32[]{:S(2)}, u32[]{:S(2)}) collective-permute-start(bf16[128,1280]{1,0:T(8,128)(2,1)S(1)} %get-tuple-element.31), channel_id=1, source_target_pairs={{0,31},{1,2},{2,1},{3,4},{4,3},{5,6},{6,5},{7,8},{8,7},{9,10},{10,... | collective-permute-start | bytes 983048 | tf_op jit(solution)/shard_map/ppermute | solution.py:26
  55.5 8.3 %collective-permute-start.10 = (bf16[64,1792]{1,0:T(8,128)(2,1)S(1)}, bf16[64,1792]{1,0:T(8,128)(2,1)S(1)}, u32[]{:S(2)}, u32[]{:S(2)}) collective-permute-start(bf16[64,1792]{1,0:T(8,128)(2,1)S(1)} %shard_map.60), channel_id=1, source_target_pairs={{0,32},{1,481},{2,34},{3,483},{4,36},{5,485},{6,38},{7,487},{8,40}... | collective-permute-start | bytes 688136 | tf_op jit(solution)/shard_map/ppermute | solution.py:26
  59.8 8.4 %collective-permute-start.6 = (bf16[64,1792]{1,0:T(8,128)(2,1)S(1)}, bf16[64,1792]{1,0:T(8,128)(2,1)S(1)}, u32[]{:S(2)}, u32[]{:S(2)}) collective-permute-start(bf16[64,1792]{1,0:T(8,128)(2,1)S(1)} %shard_map.58), channel_id=1, source_target_pairs={{0,32},{1,481},{2,34},{3,483},{4,36},{5,485},{6,38},{7,487},{8,40}... | collective-permute-start | bytes 688136 | tf_op jit(solution)/shard_map/ppermute | solution.py:26
  63.9 7.5 %collective-permute-start.11 = (bf16[32,1792]{1,0:T(8,128)(2,1)S(1)}, bf16[32,1792]{1,0:T(8,128)(2,1)S(1)}, u32[]{:S(2)}, u32[]{:S(2)}) collective-permute-start(bf16[32,1792]{1,0:T(8,128)(2,1)S(1)} %get-tuple-element.40), channel_id=1, source_target_pairs={{0,64},{1,449},{2,66},{3,451},{4,68},{5,453},{6,70},{7,455},{8,72}... | collective-permute-start | bytes 344072 | tf_op jit(solution)/shard_map/ppermute | solution.py:26
  68.4 8.7 %collective-permute-start.7 = (bf16[32,1792]{1,0:T(8,128)(2,1)S(1)}, bf16[32,1792]{1,0:T(8,128)(2,1)S(1)}, u32[]{:S(2)}, u32[]{:S(2)}) collective-permute-start(bf16[32,1792]{1,0:T(8,128)(2,1)S(1)} %get-tuple-element.38), channel_id=1, source_target_pairs={{0,64},{1,449},{2,66},{3,451},{4,68},{5,453},{6,70},{7,455},{8,72}... | collective-permute-start | bytes 344072 | tf_op jit(solution)/shard_map/ppermute | solution.py:26
  71.5 8.9 %collective-permute-start.12 = (bf16[16,1792]{1,0:T(8,128)(2,1)S(1)}, bf16[16,1792]{1,0:T(8,128)(2,1)S(1)}, u32[]{:S(2)}, u32[]{:S(2)}) collective-permute-start(bf16[16,1792]{1,0:T(8,128)(2,1)S(1)} %fusion.2), channel_id=1, source_target_pairs={{0,128},{1,385},{2,130},{3,387},{4,132},{5,389},{6,134},{7,391},{8... | collective-permute-start | bytes 172040 | tf_op jit(solution)/shard_map/ppermute | solution.py:26
  80.4 18.9 %collective-permute-start.13 = (f32[16,1792]{1,0:T(8,128)S(1)}, f32[16,1792]{1,0:T(8,128)S(1)}, u32[]{:S(2)}, u32[]{:S(2)}) collective-permute-start(f32[16,1792]{1,0:T(8,128)S(1)} %fusion.3), channel_id=1, source_target_pairs={{0,33},{1,480},{2,35},{3,482},{4,37},{5,484},{6,39},{7,486},{8,41}... | collective-permute-start | bytes 344072 | tf_op jit(solution)/shard_map/ppermute | solution.py:26
  90.3 9.0 %collective-permute-start.8 = (bf16[16,1792]{1,0:T(8,128)(2,1)S(1)}, bf16[16,1792]{1,0:T(8,128)(2,1)S(1)}, u32[]{:S(2)}, u32[]{:S(2)}) collective-permute-start(bf16[16,1792]{1,0:T(8,128)(2,1)S(1)} %fusion.4), channel_id=1, source_target_pairs={{0,128},{1,385},{2,130},{3,387},{4,132},{5,389},{6,134},{7,391},{8... | collective-permute-start | bytes 172040 | tf_op jit(solution)/shard_map/ppermute | solution.py:26
